TPU v7x, 32 devices: a whole 2x2x4 slice. The times are simulated.
32 devices in a mesh: fsdp: 8 (over y, x, core), tp: 4 (over z).
Axes of the slice: x: 2, y: 2, z: 4, core: 2. Of those that a mesh axis runs over, the one named last changes fastest.
Arguments:
- grads: bfloat16 [64, 128, 8192], P('tp', None, 'fsdp'), may hold values from -60 to 60
- momentum: bfloat16 [64, 128, 8192], P('tp', None, 'fsdp'), may hold values from -6 to 6
- owner_table: int32 [64, 1], P('tp'), may hold values from 0 to 7; in each aligned block of 16 rows (0 to 15, 16 to 31, ...) at most 2 rows name the same one
- pool_map: int32 [4, 16], P('tp'), may hold values from 0 to 15, each once within a row
Outputs:
- new_momentum: bfloat16 [64, 128, 8192], P('tp', None, 'fsdp')
- pool_update: bfloat16 [64, 128, 8192], P('tp', None, 'fsdp')
- slot_rms: float32 [4, 16], P('tp', 'fsdp')
Inputs may be any that keep to these rules, and one draw needn't show every extreme that they name: `owner_table`: within each aligned block of 16 rows (the head blocks of one index of tp) no owner is named more than 2 times. `pool_map`: each row is a permutation of 0 to 15.
All inputs are finite; a program needn't handle non-finite values.
Results may differ from a plain program's by a relative error of at most 0.0058.
Values may be sent and summed in bfloat16 or wider, within the bound.
No kernel may reach another device: no remote copies, remote signals or barrier semaphores. Data moves between devices by JAX's collectives and lax.ppermute only.
A program may use at most 64 MiB of HBM per device.

v0:
```python
import functools
import math

import jax
import jax.numpy as jnp
from jax import lax
from jax.experimental import pallas as pl
from jax.experimental.pallas import tpu as pltpu
from jax.sharding import PartitionSpec as P


CAP = 2
ITERS = 3

momentum_rate = 0.95
step_size = 0.8
epsilon = 1e-07
poly_linear = 3.4445
poly_cubic = -4.775
poly_quintic = 2.0315


def nesterov_of(grads, momentum):
    g = grads.astype(jnp.float32)
    velocity = momentum_rate * momentum.astype(jnp.float32) + g
    return velocity, (g + momentum_rate * velocity).astype(jnp.bfloat16)


def first_kernel(wanted, pieces, codes_ref, g_ref, m_ref, *refs):
    count = len(wanted)
    outs = refs[:count]
    g_buf, m_buf, y_buf, g_sem, m_sem, y_sem = refs[count:]
    rows = g_buf.shape[2]
    group = codes_ref.shape[1] // lax.axis_size("tp")
    row = lax.axis_index("tp")

    def in_copies(i, p, source):
        part = pl.ds(p * rows, rows)
        return (
            pltpu.make_async_copy(g_ref.at[source, part], g_buf.at[i, p], g_sem.at[i, p]),
            pltpu.make_async_copy(m_ref.at[source, part], m_buf.at[i, p], m_sem.at[i, p]),
        )

    def out_copy(i, p):
        return pltpu.make_async_copy(y_buf.at[i, p], outs[i].at[0, pl.ds(p * rows, rows)], y_sem.at[i, p])

    reads = []
    for i, (place_of, c) in enumerate(wanted):
        place = place_of(row) * group + c
        source = jnp.int32(0)
        for j in range(codes_ref.shape[1]):
            source = jnp.where(codes_ref[0, j] == place, j, source)
        for p in range(pieces):
            reads.append((i, p, in_copies(i, p, source)))
            for copy in reads[-1][2]:
                copy.start()
    for i, p, copies in reads:
        for copy in copies:
            copy.wait()
        _, y = nesterov_of(g_buf[i, p], m_buf[i, p])
        y_buf[i, p] = y
        out_copy(i, p).start()
    for i, p, _ in reads:
        out_copy(i, p).wait()


def first_blocks(codes, grads, momentum, wanted, pieces=4):
    _, head, width = grads.shape
    count = len(wanted)
    buffer = pltpu.VMEM((count, pieces, head // pieces, width), jnp.bfloat16)
    return pl.pallas_call(
        functools.partial(first_kernel, wanted, pieces),
        out_shape=[jax.ShapeDtypeStruct((1, head, width), jnp.bfloat16)] * count,
        in_specs=[
            pl.BlockSpec(memory_space=pltpu.SMEM),
            pl.BlockSpec(memory_space=pl.ANY),
            pl.BlockSpec(memory_space=pl.ANY),
        ],
        out_specs=[pl.BlockSpec(memory_space=pl.ANY)] * count,
        scratch_shapes=[buffer] * 3 + [pltpu.SemaphoreType.DMA((count, pieces))] * 3,
        name="first_blocks",
    )(codes, grads, momentum)


def all_kernel(starts, source, place, g_ref, m_ref, newm_ref, gram_ref, diag_ref, *outs):
    step = pl.program_id(0)
    velocity, y = nesterov_of(g_ref[0], m_ref[0])
    newm_ref[0] = velocity.astype(jnp.bfloat16)
    gram = lax.dot_general(y, y, (((1,), (1,)), ((), ())), preferred_element_type=jnp.float32)
    gram_ref[0] = gram
    rows = lax.broadcasted_iota(jnp.int32, gram.shape, 0)
    columns = lax.broadcasted_iota(jnp.int32, gram.shape, 1)
    diagonal = jnp.sum(jnp.where(rows == columns, gram, 0.0), axis=0, keepdims=True)
    diag_ref[pl.ds(place[step], 1), :] = diagonal
    for (start, count), out in zip(starts, outs):

        @pl.when(jnp.logical_and(step >= start, step < start + count))
        def _():
            out[0] = y


def all_blocks(source, place, grads, momentum, starts):
    blocks, head, width = grads.shape
    block = (1, head, width)

    def chunk_spec(start, count):
        return pl.BlockSpec(block, lambda i, s, p: (jnp.clip(i - start, 0, count - 1), 0, 0))

    return pl.pallas_call(
        functools.partial(all_kernel, starts),
        out_shape=[
            jax.ShapeDtypeStruct(grads.shape, jnp.bfloat16),
            jax.ShapeDtypeStruct((blocks, head, head), jnp.float32),
            jax.ShapeDtypeStruct((blocks, head), jnp.float32),
        ]
        + [jax.ShapeDtypeStruct((count, head, width), jnp.bfloat16) for _, count in starts],
        grid_spec=pltpu.PrefetchScalarGridSpec(
            num_scalar_prefetch=2,
            grid=(blocks,),
            in_specs=[pl.BlockSpec(block, lambda i, s, p: (s[i], 0, 0))] * 2,
            out_specs=[
                pl.BlockSpec(block, lambda i, s, p: (s[i], 0, 0)),
                pl.BlockSpec((1, head, head), lambda i, s, p: (p[i], 0, 0)),
                pl.BlockSpec((blocks, head), lambda i, s, p: (0, 0)),
            ]
            + [chunk_spec(start, count) for start, count in starts],
        ),
        name="all_blocks",
    )(source, place, grads, momentum)


def apply_kernel(factor, starts, place, q_ref, *refs):
    step = pl.program_id(0)
    out = refs[-1]
    q = q_ref[0]
    head = q.shape[0]
    high = q.astype(jnp.bfloat16)
    low = (q - high.astype(jnp.float32)).astype(jnp.bfloat16)
    both = jnp.concatenate([high, low], axis=0)
    for (start, count), y_ref in zip(starts, refs):

        @pl.when(jnp.logical_and(step >= start, step < start + count))
        def _():
            ortho = jnp.dot(both, y_ref[0], preferred_element_type=jnp.float32)
            ortho = ortho[:head] + ortho[head:]
            ortho = ortho.astype(jnp.bfloat16).astype(jnp.float32)
            out[0] = (-factor * ortho).astype(jnp.bfloat16)


def apply_blocks(factor, place, transforms, chunks, into, tiles):
    head, width = chunks[0].shape[1:]
    blocks = transforms.shape[0]
    block = (1, head, width // tiles)
    starts, total = [], 0
    for chunk in chunks:
        starts.append((total, chunk.shape[0]))
        total += chunk.shape[0]

    def chunk_spec(start, count):
        def index(i, j, p):
            column = jnp.where(i < start, 0, jnp.where(i < start + count, j, tiles - 1))
            return (jnp.clip(i - start, 0, count - 1), 0, column)

        return pl.BlockSpec(block, index)

    in_specs = [pl.BlockSpec((1, head, head), lambda i, j, p: (p[i], 0, 0))]
    in_specs += [chunk_spec(start, count) for start, count in starts]
    operands = [transforms, *chunks]
    aliases = {}
    if into is not None:
        in_specs.append(pl.BlockSpec(memory_space=pl.ANY))
        operands.append(into)
        aliases = {len(operands): 0}
    return pl.pallas_call(
        functools.partial(apply_kernel, factor, starts),
        out_shape=jax.ShapeDtypeStruct((blocks, head, width), jnp.bfloat16),
        grid_spec=pltpu.PrefetchScalarGridSpec(
            num_scalar_prefetch=1,
            grid=(total, tiles),
            in_specs=in_specs,
            out_specs=pl.BlockSpec(block, lambda i, j, p: (p[i], 0, j)),
        ),
        input_output_aliases=aliases,
        name="apply_blocks",
    )(place, *operands)


def transforms_of(gram):
    high = lax.Precision.HIGHEST
    identity = jnp.eye(gram.shape[1], dtype=jnp.float32)[None]
    squares = jnp.sum(gram * identity, axis=(1, 2))
    inverse = 1.0 / (jnp.sqrt(squares) + epsilon)
    gram = gram * (inverse * inverse)[:, None, None]
    transform = None
    for i in range(ITERS):
        square_gram = jnp.einsum("kil,klm->kim", gram, gram, precision=high)
        mixed = poly_linear * identity + poly_cubic * gram + poly_quintic * square_gram
        if transform is None:
            transform = mixed
        else:
            transform = jnp.einsum("kil,klm->kim", mixed, transform, precision=high)
        if i + 1 < ITERS:
            right_side = jnp.einsum("kil,klm->kim", gram, mixed, precision=high)
            gram = jnp.einsum("kil,klm->kim", mixed, right_side, precision=high)
    return transform * inverse[:, None, None]


def local(grads, momentum, owner_table, pool_map):
    n_fsdp, n_tp = lax.axis_size("fsdp"), lax.axis_size("tp")
    here, row = lax.axis_index("fsdp"), lax.axis_index("tp")
    blocks, head, width = grads.shape
    group = blocks // n_tp
    paired = n_tp & (n_tp - 1) == 0

    def partner(t, x):
        return t ^ x if paired else (t + x) % n_tp

    def sender(t, x):
        return t ^ x if paired else (t - x) % n_tp

    far = [x for x in range(1, n_tp) if x >= n_tp // 2]
    near = [x for x in range(1, n_tp) if x < n_tp // 2]
    cut = max(1, group // 2)
    first = [(x, (0,)) for x in far]
    second = [(x, (c,)) for c in range(1, cut) for x in far]
    third = [(x, tuple(range(group))) for x in near]
    late = [(x, (c,)) for c in range(cut, group) for x in far]
    own = [(0, tuple(range(group)))]
    chunks = first + second + third + late + own
    steps = [(x, c) for x, cs in chunks for c in cs]

    codes = pool_map[0]
    position = jnp.arange(blocks, dtype=jnp.int32)
    offsets = jnp.array([c for _, c in steps], jnp.int32)
    partners = jnp.array([x for x, _ in steps], jnp.int32)
    place_out = partner(row, partners) * group + offsets
    place_in = sender(row, partners) * group + offsets
    source = jnp.sum(jnp.where(codes[None, :] == place_out[:, None], position[None, :], 0), axis=1)

    starts, total = {}, 0
    for chunk in chunks:
        starts[chunk] = (total, len(chunk[1]))
        total += len(chunk[1])

    got = {}

    def send(chunk, array):
        got[chunk] = lax.ppermute(array, "tp", [(t, partner(t, chunk[0])) for t in range(n_tp)])

    wanted = [(functools.partial(partner, x=x), cs[0]) for x, cs in first]
    for chunk, array in zip(first, first_blocks(pool_map, grads, momentum, wanted)):
        send(chunk, array)
    rest = second + third + late + own
    new_momentum, gram, diagonal, *ys = all_blocks(
        source, place_out, grads, momentum, [starts[chunk] for chunk in rest]
    )
    ys = dict(zip(rest, ys))
    for chunk in second + third + late:
        send(chunk, ys[chunk])

    spread = -(-blocks // n_fsdp)
    users = blocks // spread
    parts = gram.reshape(users, spread * head, head)
    parts = jnp.pad(parts, ((0, n_fsdp - users), (0, 0), (0, 0)))
    parts = jnp.concatenate([parts, jnp.broadcast_to(diagonal[None], (n_fsdp, blocks, head))], axis=1)
    arrived = lax.all_to_all(parts, "fsdp", split_axis=0, concat_axis=0, tiled=True)
    summed = jnp.sum(arrived, axis=0)
    squares = jnp.sum(summed[spread * head :], axis=1)
    transform = transforms_of(summed[: spread * head].reshape(spread, head, head))

    pairs = []
    per_row = group // spread
    for f in range(users):
        for t in range(n_tp):
            to = (t * per_row + f % per_row) * n_tp + f // per_row
            pairs.append((f * n_tp + t, to))
    transform = lax.ppermute(transform, ("fsdp", "tp"), pairs)
    spread_out = jnp.broadcast_to(transform[None], (n_fsdp,) + transform.shape)
    transforms = lax.all_to_all(spread_out, "fsdp", split_axis=0, concat_axis=0, tiled=True)
    transforms = transforms.reshape(n_fsdp * spread, head, head)[:blocks]

    owners = owner_table[:, 0]
    earlier = position[None, :] < position[:, None]
    slots = jnp.sum(jnp.logical_and(owners[:, None] == owners[None, :], earlier), axis=1)
    rms_by_place = jnp.sqrt(squares / (head * width * n_fsdp))
    by_block = jnp.sum(jnp.where(codes[:, None] == position[None, :], rms_by_place[None, :], 0.0), axis=1)
    slot_range = jnp.arange(CAP, dtype=jnp.int32)
    pick = jnp.logical_and((owners == here)[None, :], slots[None, :] == slot_range[:, None])
    slot_out = jnp.sum(jnp.where(pick, by_block[None, :], 0.0), axis=1)[None, :]

    factor = step_size * 0.2 * math.sqrt(width * n_fsdp)
    for chunk in own:
        got[chunk] = ys[chunk]
    rounds = [own + first + second]
    if third:
        rounds.append(third)
    rounds += [late[i : i + len(far)] for i in range(0, len(late) - len(far), len(far))]
    rounds += [[chunk] for chunk in late[-len(far) :]]
    rounds = [members for members in rounds if members]
    update = None
    for members in rounds:
        where = jnp.concatenate([place_in[s : s + n] for s, n in (starts[chunk] for chunk in members)])
        tiles = 1 if len(where) > 2 or width < 512 else 4
        update = apply_blocks(factor, where, transforms, [got[chunk] for chunk in members], update, tiles)
    return (new_momentum, update, slot_out)


def solution(mesh):
    def step(*args):
        return local(*args)

    in_specs = (P("tp", None, "fsdp"), P("tp", None, "fsdp"), P("tp", None), P("tp", None))
    out_specs = (P("tp", None, "fsdp"), P("tp", None, "fsdp"), P("tp", "fsdp"))
    step = jax.shard_map(step, mesh=mesh, in_specs=in_specs, out_specs=out_specs, check_vma=False)
    return step
```

profile of v0, /device:TPU:18, one launch (start us, length us, event | category | flops | bytes accessed | tf_op | source)
XLA Modules:
  0.0 155.9 jit_solution(3522304124536824333)
XLA Ops:
  0.6 0.7 multiply_add_fusion.place
  1.3 1.3 select_reduce_fusion.1.source
  2.7 15.3 %all_blocks.1 = (bf16[16,128,1024]{2,1,0:T(8,128)(2,1)}, f32[16,128,128]{2,1,0:T(8,128)}, f32[16,128]{1,0:T(8,128)}, bf16[1,128,1024]{2,1,0:T(8,128)(2,1)}, bf16...) custom-call(s32[16]{0:T(128)} %select_reduce_fusion.1.source, ...), custom_call_target="tpu_custom_call" | custom-call | tf_op jit(solution)/shard_map/all_blocks/pallas_call | solution.py:109
  18.0 0.7 broadcast_in_dim.70
  18.7 2.3 %pad_maximum_fusion = f32[8,272,128]{2,1,0:T(8,128)} fusion(f32[8,16,128]{2,1,0:T(8,128)S(1)} %broadcast_in_dim.70, f32[8,256,128]{2,1,0:T(8,128)} %bitcast.35), kind=kLoop, calls=%fused_computation.7 | loop fusion | flops 278528 | bytes 2228224 | tf_op jit(solution)/shard_map/concatenate | solution.py:265
  21.0 4.3 %all-to-all-start = ((f32[8,272,128]{2,1,0:T(8,128)}), f32[8,272,128]{2,1,0:T(8,128)S(1)}, u32[]{:S(2)}, u32[]{:S(2)}) async-start(f32[8,272,128]{2,1,0:T(8,128)} %pad_maximum_fusion), calls=%async_computation | async-start | bytes 2228224 | tf_op jit(solution)/shard_map/all_to_all | solution.py:266
  25.2 2.8 %first_blocks.1 = (bf16[1,128,1024]{2,1,0:T(8,128)(2,1)}, bf16[1,128,1024]{2,1,0:T(8,128)(2,1)}) custom-call(s32[1,16]{1,0:T(1,128)} %codes_ref.1, bf16[16,128,1024]{2,1,0:T(8,128)(2,1)} %g_ref.3, bf16[16,128,1024]{2,1,0:T(8,128)(2,1)} %m_ref.3), custom_call_target="tpu_custom_call" | custom-call | tf_op jit(solution)/shard_map/first_blocks/pallas_call | solution.py:71
  28.0 0.4 collective-permute-start.6
  28.4 2.7 %collective-permute-start.7 = (bf16[1,128,1024]{2,1,0:T(8,128)(2,1)}, bf16[1,128,1024]{2,1,0:T(8,128)(2,1)S(1)}, u32[]{:S(2)}, u32[]{:S(2)}) collective-permute-start(bf16[1,128,1024]{2,1,0:T(8,128)(2,1)} %get-tuple-element.26), channel_id=1, source_target_pairs={{0,3},{1,2},{2,1},{3,0},{4,7},{5,6},{6,5},{7,4},{8,11},{9,10},{10,... | collective-permute-start | bytes 786440 | tf_op jit(solution)/shard_map/ppermute | solution.py:248
  31.1 1.2 collective-permute-start.8
  32.4 1.6 %collective-permute-start.9 = (bf16[1,128,1024]{2,1,0:T(8,128)(2,1)}, bf16[1,128,1024]{2,1,0:T(8,128)(2,1)S(1)}, u32[]{:S(2)}, u32[]{:S(2)}) collective-permute-start(bf16[1,128,1024]{2,1,0:T(8,128)(2,1)} %get-tuple-element.28), channel_id=1, source_target_pairs={{0,3},{1,2},{2,1},{3,0},{4,7},{5,6},{6,5},{7,4},{8,11},{9,10},{10,... | collective-permute-start | bytes 786440 | tf_op jit(solution)/shard_map/ppermute | solution.py:248
  34.0 5.8 %all-to-all-done = f32[8,272,128]{2,1,0:T(8,128)S(1)} async-done(((f32[8,272,128]{2,1,0:T(8,128)}), f32[8,272,128]{2,1,0:T(8,128)S(1)}, u32[]{:S(2)}, u32[]{:S(2)}) %all-to-all-start) | async-done | bytes 1114144 | tf_op jit(solution)/shard_map/all_to_all | solution.py:266
  40.1 0.4 fusion.2
  40.5 0.3 fusion.5
  40.8 0.3 fusion.16
  41.1 0.3 fusion.1
  41.6 0.3 fusion.17
  42.2 0.3 fusion
  42.4 0.3 convolution_multiply_fusion
  42.7 3.3 %collective-permute-start = (f32[2,128,128]{2,1,0:T(8,128)S(1)}, f32[2,128,128]{2,1,0:T(8,128)S(1)}, u32[]{:S(2)}, u32[]{:S(2)}) collective-permute-start(f32[2,128,128]{2,1,0:T(8,128)S(1)} %convolution_multiply_fusion), channel_id=1, source_target_pairs={{0,0},{1,8},{2,16},{3,24},{4,4},{5,12},{6,20},{7,28},{8,1},{9,9},{... | collective-permute-start | bytes 393224 | tf_op jit(solution)/shard_map/ppermute | solution.py:277
  46.0 0.6 fusion.14
  46.6 36.8 %collective-permute-done = f32[2,128,128]{2,1,0:T(8,128)S(1)} collective-permute-done((f32[2,128,128]{2,1,0:T(8,128)S(1)}, f32[2,128,128]{2,1,0:T(8,128)S(1)}, u32[]{:S(2)}, u32[]{:S(2)}) %collective-permute-start) | collective-permute-done | bytes 131104 | tf_op jit(solution)/shard_map/ppermute | solution.py:277
  83.5 1.6 %collective-permute-start.5 = (bf16[4,128,1024]{2,1,0:T(8,128)(2,1)}, bf16[4,128,1024]{2,1,0:T(8,128)(2,1)S(1)}, u32[]{:S(2)}, u32[]{:S(2)}) collective-permute-start(bf16[4,128,1024]{2,1,0:T(8,128)(2,1)} %get-tuple-element.23), channel_id=1, source_target_pairs={{0,1},{1,0},{2,3},{3,2},{4,5},{5,4},{6,7},{7,6},{8,9},{9,8},{10,11... | collective-permute-start | bytes 3145736 | tf_op jit(solution)/shard_map/ppermute | solution.py:248
  85.0 1.1 broadcast_in_dim.71
  86.1 3.5 %all-to-all-start.1 = ((f32[8,2,128,128]{3,2,1,0:T(8,128)}), f32[8,2,128,128]{3,2,1,0:T(8,128)S(1)}, u32[]{:S(2)}, u32[]{:S(2)}) async-start(f32[8,2,128,128]{3,2,1,0:T(8,128)} %broadcast_in_dim.71), calls=%async_computation.1 | async-start | bytes 2097152 | tf_op jit(solution)/shard_map/all_to_all | solution.py:279
  89.6 0.7 fusion.15
  90.3 0.6 pad_add_fusion.place
  90.9 0.6 concatenate.10.place
  91.9 0.7 copy-done.7
  92.6 2.8 %collective-permute-start.2 = (bf16[1,128,1024]{2,1,0:T(8,128)(2,1)}, bf16[1,128,1024]{2,1,0:T(8,128)(2,1)S(1)}, u32[]{:S(2)}, u32[]{:S(2)}) collective-permute-start(bf16[1,128,1024]{2,1,0:T(8,128)(2,1)} %get-tuple-element.20), channel_id=1, source_target_pairs={{0,2},{1,3},{2,0},{3,1},{4,6},{5,7},{6,4},{7,5},{8,10},{9,11},{10,... | collective-permute-start | bytes 786440 | tf_op jit(solution)/shard_map/ppermute | solution.py:248
  95.4 0.7 copy-done.8
  96.3 0.7 copy-done.9
  96.9 2.0 %collective-permute-start.4 = (bf16[1,128,1024]{2,1,0:T(8,128)(2,1)}, bf16[1,128,1024]{2,1,0:T(8,128)(2,1)S(1)}, u32[]{:S(2)}, u32[]{:S(2)}) collective-permute-start(bf16[1,128,1024]{2,1,0:T(8,128)(2,1)} %get-tuple-element.22), channel_id=1, source_target_pairs={{0,3},{1,2},{2,1},{3,0},{4,7},{5,6},{6,5},{7,4},{8,11},{9,10},{10,... | collective-permute-start | bytes 786440 | tf_op jit(solution)/shard_map/ppermute | solution.py:248
  99.1 0.6 fusion.12
  99.8 3.5 %all-to-all-done.1 = f32[8,2,128,128]{3,2,1,0:T(8,128)S(1)} async-done(((f32[8,2,128,128]{3,2,1,0:T(8,128)}), f32[8,2,128,128]{3,2,1,0:T(8,128)S(1)}, u32[]{:S(2)}, u32[]{:S(2)}) %all-to-all-start.1) | async-done | bytes 1048608 | tf_op jit(solution)/shard_map/all_to_all | solution.py:279
  103.3 1.0 copy-done
  104.3 7.5 %apply_blocks.5.refs_1_ = bf16[16,128,1024]{2,1,0:T(8,128)(2,1)} custom-call(s32[8]{0:T(128)} %pad_add_fusion.place, f32[16,128,128]{2,1,0:T(8,128)} %bitcast.28, bf16[4,128,1024]{2,1,0:T(8,128)(2,1)} %get-tuple-element.24.refs_0_, bf16[1,128,1024]{2,1,0:T(8,128)(2,1)} %copy-done.6, bf16[1,128,1024]{2,1,0:T(8,128)(2,1)} %copy-done.7, ...), custom_call_target="tpu_custom_call" | custom-call | tf_op jit(solution)/shard_map/apply_blocks/pallas_call | solution.py:174
  111.8 7.3 %collective-permute-done.5.refs_0_ = bf16[4,128,1024]{2,1,0:T(8,128)(2,1)S(1)} collective-permute-done((bf16[4,128,1024]{2,1,0:T(8,128)(2,1)}, bf16[4,128,1024]{2,1,0:T(8,128)(2,1)S(1)}, u32[]{:S(2)}, u32[]{:S(2)}) %collective-permute-start.5) | collective-permute-done | bytes 1048608 | tf_op jit(solution)/shard_map/ppermute | solution.py:248
  119.1 1.0 copy-done.1
  120.1 4.7 %apply_blocks.6.refs_2_ = bf16[16,128,1024]{2,1,0:T(8,128)(2,1)} custom-call(s32[4]{0:T(128)} %get-tuple-element.35.place, f32[16,128,128]{2,1,0:T(8,128)} %bitcast.29, bf16[4,128,1024]{2,1,0:T(8,128)(2,1)} %copy-done.1, bf16[16,128,1024]{2,1,0:T(8,128)(2,1)} %apply_blocks.5.refs_1_), custom_call_target="tpu_custom_call", output_to_operand_aliasing={{}: (3, {})} | custom-call | tf_op jit(solution)/shard_map/apply_blocks/pallas_call | solution.py:174
  124.8 7.8 %collective-permute-done.3.refs_0_ = bf16[1,128,1024]{2,1,0:T(8,128)(2,1)S(1)} collective-permute-done((bf16[1,128,1024]{2,1,0:T(8,128)(2,1)}, bf16[1,128,1024]{2,1,0:T(8,128)(2,1)S(1)}, u32[]{:S(2)}, u32[]{:S(2)}) %collective-permute-start.3) | collective-permute-done | bytes 262176 | tf_op jit(solution)/shard_map/ppermute | solution.py:248
  132.6 6.9 %collective-permute-done.4.refs_1_ = bf16[1,128,1024]{2,1,0:T(8,128)(2,1)S(1)} collective-permute-done((bf16[1,128,1024]{2,1,0:T(8,128)(2,1)}, bf16[1,128,1024]{2,1,0:T(8,128)(2,1)S(1)}, u32[]{:S(2)}, u32[]{:S(2)}) %collective-permute-start.4) | collective-permute-done | bytes 262176 | tf_op jit(solution)/shard_map/ppermute | solution.py:248
  139.5 0.7 copy-done.5
  140.2 6.3 %apply_blocks.7.refs_1_ = bf16[16,128,1024]{2,1,0:T(8,128)(2,1)} custom-call(s32[2]{0:T(128)} %concatenate.10.place, f32[16,128,128]{2,1,0:T(8,128)} %bitcast.30, bf16[1,128,1024]{2,1,0:T(8,128)(2,1)} %copy-done.4, bf16[1,128,1024]{2,1,0:T(8,128)(2,1)} %copy-done.5, bf16[16,128,1024]{2,1,0:T(8,128)(2,1)} %apply_blocks.6.refs_2_), custom_call_target="tpu_custom_call", output_to_operand_aliasing={{}: (4, {})} | custom-call | tf_op jit(solution)/shard_map/apply_blocks/pallas_call | solution.py:174
  146.5 0.7 copy-done.3
  147.2 4.0 %apply_blocks.8.refs_1_ = bf16[16,128,1024]{2,1,0:T(8,128)(2,1)} custom-call(s32[1]{0:T(128)} %get-tuple-element.36.place, f32[16,128,128]{2,1,0:T(8,128)} %bitcast.31, bf16[1,128,1024]{2,1,0:T(8,128)(2,1)} %copy-done.3, bf16[16,128,1024]{2,1,0:T(8,128)(2,1)} %apply_blocks.7.refs_1_), custom_call_target="tpu_custom_call", output_to_operand_aliasing={{}: (3, {})} | custom-call | tf_op jit(solution)/shard_map/apply_blocks/pallas_call | solution.py:174
  151.2 0.7 copy-done.2
  151.9 4.0 %apply_blocks.9 = bf16[16,128,1024]{2,1,0:T(8,128)(2,1)} custom-call(s32[1]{0:T(128)} %get-tuple-element.37.place, f32[16,128,128]{2,1,0:T(8,128)} %bitcast.32, bf16[1,128,1024]{2,1,0:T(8,128)(2,1)} %copy-done.2, bf16[16,128,1024]{2,1,0:T(8,128)(2,1)} %apply_blocks.8.refs_1_), custom_call_target="tpu_custom_call", output_to_operand_aliasing={{}: (3, {})} | custom-call | tf_op jit(solution)/shard_map/apply_blocks/pallas_call | solution.py:174
  (41 shorter events, 1.6 us)
Async XLA Ops:
  1.3 1.4 copy-start.10
  21.0 18.8 %all-to-all-start = ((f32[8,272,128]{2,1,0:T(8,128)}), f32[8,272,128]{2,1,0:T(8,128)S(1)}, u32[]{:S(2)}, u32[]{:S(2)}) async-start(f32[8,272,128]{2,1,0:T(8,128)} %pad_maximum_fusion), calls=%async_computation | async-start | bytes 2228224 | tf_op jit(solution)/shard_map/all_to_all | solution.py:266
  28.0 18.0 %copy-start.11 = (s32[16]{0:T(128)S(1)}, s32[16]{0:T(128)}, u32[]{:S(2)}) copy-start(s32[16]{0:T(128)} %copy-done.10) | copy-start | bytes 196
  28.0 63.8 %collective-permute-start.6 = (bf16[1,128,1024]{2,1,0:T(8,128)(2,1)}, bf16[1,128,1024]{2,1,0:T(8,128)(2,1)S(1)}, u32[]{:S(2)}, u32[]{:S(2)}) collective-permute-start(bf16[1,128,1024]{2,1,0:T(8,128)(2,1)} %get-tuple-element.25), channel_id=1, source_target_pairs={{0,2},{1,3},{2,0},{3,1},{4,6},{5,7},{6,4},{7,5},{8,10},{9,11},{10,... | collective-permute-start | bytes 786440 | tf_op jit(solution)/shard_map/ppermute | solution.py:248
  28.4 63.5 %collective-permute-start.7 = (bf16[1,128,1024]{2,1,0:T(8,128)(2,1)}, bf16[1,128,1024]{2,1,0:T(8,128)(2,1)S(1)}, u32[]{:S(2)}, u32[]{:S(2)}) collective-permute-start(bf16[1,128,1024]{2,1,0:T(8,128)(2,1)} %get-tuple-element.26), channel_id=1, source_target_pairs={{0,3},{1,2},{2,1},{3,0},{4,7},{5,6},{6,5},{7,4},{8,11},{9,10},{10,... | collective-permute-start | bytes 786440 | tf_op jit(solution)/shard_map/ppermute | solution.py:248
  31.1 64.3 %collective-permute-start.8 = (bf16[1,128,1024]{2,1,0:T(8,128)(2,1)}, bf16[1,128,1024]{2,1,0:T(8,128)(2,1)S(1)}, u32[]{:S(2)}, u32[]{:S(2)}) collective-permute-start(bf16[1,128,1024]{2,1,0:T(8,128)(2,1)} %get-tuple-element.27), channel_id=1, source_target_pairs={{0,2},{1,3},{2,0},{3,1},{4,6},{5,7},{6,4},{7,5},{8,10},{9,11},{10,... | collective-permute-start | bytes 786440 | tf_op jit(solution)/shard_map/ppermute | solution.py:248
  32.4 63.9 %collective-permute-start.9 = (bf16[1,128,1024]{2,1,0:T(8,128)(2,1)}, bf16[1,128,1024]{2,1,0:T(8,128)(2,1)S(1)}, u32[]{:S(2)}, u32[]{:S(2)}) collective-permute-start(bf16[1,128,1024]{2,1,0:T(8,128)(2,1)} %get-tuple-element.28), channel_id=1, source_target_pairs={{0,3},{1,2},{2,1},{3,0},{4,7},{5,6},{6,5},{7,4},{8,11},{9,10},{10,... | collective-permute-start | bytes 786440 | tf_op jit(solution)/shard_map/ppermute | solution.py:248
  34.0 55.6 %copy-start.13 = (s32[16,1]{0,1:T(1,128)S(1)}, s32[16,1]{0,1:T(1,128)}, u32[]{:S(2)}) copy-start(s32[16,1]{0,1:T(1,128)} %param.8) | copy-start | bytes 196
  34.0 65.0 %copy-start.12 = (s32[1,16]{1,0:T(1,128)S(1)}, s32[1,16]{1,0:T(1,128)}, u32[]{:S(2)}) copy-start(s32[1,16]{1,0:T(1,128)} %codes_ref.1) | copy-start | bytes 196
  42.7 40.7 %collective-permute-start = (f32[2,128,128]{2,1,0:T(8,128)S(1)}, f32[2,128,128]{2,1,0:T(8,128)S(1)}, u32[]{:S(2)}, u32[]{:S(2)}) collective-permute-start(f32[2,128,128]{2,1,0:T(8,128)S(1)} %convolution_multiply_fusion), channel_id=1, source_target_pairs={{0,0},{1,8},{2,16},{3,24},{4,4},{5,12},{6,20},{7,28},{8,1},{9,9},{... | collective-permute-start | bytes 393224 | tf_op jit(solution)/shard_map/ppermute | solution.py:277
  83.5 35.7 %collective-permute-start.5 = (bf16[4,128,1024]{2,1,0:T(8,128)(2,1)}, bf16[4,128,1024]{2,1,0:T(8,128)(2,1)S(1)}, u32[]{:S(2)}, u32[]{:S(2)}) collective-permute-start(bf16[4,128,1024]{2,1,0:T(8,128)(2,1)} %get-tuple-element.23), channel_id=1, source_target_pairs={{0,1},{1,0},{2,3},{3,2},{4,5},{5,4},{6,7},{7,6},{8,9},{9,8},{10,11... | collective-permute-start | bytes 3145736 | tf_op jit(solution)/shard_map/ppermute | solution.py:248
  86.1 17.2 %all-to-all-start.1 = ((f32[8,2,128,128]{3,2,1,0:T(8,128)}), f32[8,2,128,128]{3,2,1,0:T(8,128)S(1)}, u32[]{:S(2)}, u32[]{:S(2)}) async-start(f32[8,2,128,128]{3,2,1,0:T(8,128)} %broadcast_in_dim.71), calls=%async_computation.1 | async-start | bytes 2097152 | tf_op jit(solution)/shard_map/all_to_all | solution.py:279
  91.8 11.5 %copy-start.6 = (bf16[1,128,1024]{2,1,0:T(8,128)(2,1)}, bf16[1,128,1024]{2,1,0:T(8,128)(2,1)S(1)}, u32[]{:S(2)}) copy-start(bf16[1,128,1024]{2,1,0:T(8,128)(2,1)S(1)} %collective-permute-done.6.refs_1_) | copy-start | bytes 786436
  91.8 59.4 %collective-permute-start.1 = (bf16[1,128,1024]{2,1,0:T(8,128)(2,1)}, bf16[1,128,1024]{2,1,0:T(8,128)(2,1)S(1)}, u32[]{:S(2)}, u32[]{:S(2)}) collective-permute-start(bf16[1,128,1024]{2,1,0:T(8,128)(2,1)} %get-tuple-element.19), channel_id=1, source_target_pairs={{0,3},{1,2},{2,1},{3,0},{4,7},{5,6},{6,5},{7,4},{8,11},{9,10},{10,... | collective-permute-start | bytes 786440 | tf_op jit(solution)/shard_map/ppermute | solution.py:248
  91.9 0.7 copy-start.7
  92.6 53.9 %collective-permute-start.2 = (bf16[1,128,1024]{2,1,0:T(8,128)(2,1)}, bf16[1,128,1024]{2,1,0:T(8,128)(2,1)S(1)}, u32[]{:S(2)}, u32[]{:S(2)}) collective-permute-start(bf16[1,128,1024]{2,1,0:T(8,128)(2,1)} %get-tuple-element.20), channel_id=1, source_target_pairs={{0,2},{1,3},{2,0},{3,1},{4,6},{5,7},{6,4},{7,5},{8,10},{9,11},{10,... | collective-permute-start | bytes 786440 | tf_op jit(solution)/shard_map/ppermute | solution.py:248
  95.4 0.7 copy-start.8
  96.1 36.5 %collective-permute-start.3 = (bf16[1,128,1024]{2,1,0:T(8,128)(2,1)}, bf16[1,128,1024]{2,1,0:T(8,128)(2,1)S(1)}, u32[]{:S(2)}, u32[]{:S(2)}) collective-permute-start(bf16[1,128,1024]{2,1,0:T(8,128)(2,1)} %get-tuple-element.21), channel_id=1, source_target_pairs={{0,2},{1,3},{2,0},{3,1},{4,6},{5,7},{6,4},{7,5},{8,10},{9,11},{10,... | collective-permute-start | bytes 786440 | tf_op jit(solution)/shard_map/ppermute | solution.py:248
  96.3 0.7 copy-start.9
  96.9 42.6 %collective-permute-start.4 = (bf16[1,128,1024]{2,1,0:T(8,128)(2,1)}, bf16[1,128,1024]{2,1,0:T(8,128)(2,1)S(1)}, u32[]{:S(2)}, u32[]{:S(2)}) collective-permute-start(bf16[1,128,1024]{2,1,0:T(8,128)(2,1)} %get-tuple-element.22), channel_id=1, source_target_pairs={{0,3},{1,2},{2,1},{3,0},{4,7},{5,6},{6,5},{7,4},{8,11},{9,10},{10,... | collective-permute-start | bytes 786440 | tf_op jit(solution)/shard_map/ppermute | solution.py:248
  103.3 1.0 copy-start
  119.1 1.0 copy-start.1
  132.6 6.9 %copy-start.4 = (bf16[1,128,1024]{2,1,0:T(8,128)(2,1)}, bf16[1,128,1024]{2,1,0:T(8,128)(2,1)S(1)}, u32[]{:S(2)}) copy-start(bf16[1,128,1024]{2,1,0:T(8,128)(2,1)S(1)} %collective-permute-done.3.refs_0_) | copy-start | bytes 786436
  139.5 0.7 copy-start.5
  146.5 0.7 copy-start.3
  151.2 0.7 copy-start.2
where the time goes:
time: 158 us; the launch traced here: 156 us
  waiting for transfers between devices  68.1 us (43%)
  Pallas kernels  44.6 us (28%)
  starting transfers between devices  23.5 us (15%)
  local copies, waits for them, and re-layouts  9.89 us (6%)
  other arithmetic  6.37 us (4%)
  matrix products  2.54 us (2%)
    ppermute x1, waiting for transfers between devices, local(): transform = lax.ppermute(transform, ('fsdp', 'tp'), pairs)  36.8 us
    pallas_call x5, Pallas kernels, apply_blocks(): pl.pallas_call(functools.partial(apply_kernel, factor, starts), out_shape...  26.5 us
    ppermute x9, waiting for transfers between devices, send(): lax.ppermute(array, 'tp', [(t, partner(t, chunk[0])) for t in range(n_tp)])  22 us
    pallas_call x1, Pallas kernels, all_blocks(): pl.pallas_call(functools.partial(all_kernel, starts), out_shape=[jax.Shap...  15.3 us
    ppermute x9, starting transfers between devices, send(): lax.ppermute(array, 'tp', [(t, partner(t, chunk[0])) for t in range(n_tp)])  12.5 us
    unnamed x28, local copies, waits for them, and re-layouts  6.25 us
    all_to_all x1, waiting for transfers between devices, local(): lax.all_to_all(parts, 'fsdp', split_axis=0, concat_axis=0, tiled=True)  5.8 us
    all_to_all x1, starting transfers between devices, local(): lax.all_to_all(parts, 'fsdp', split_axis=0, concat_axis=0, tiled=True)  4.25 us
  transfers between devices with their start and end apart: 12, of which 6 were waited for; matrix products, arithmetic and copies ran while one was open for 5% of the time, Pallas kernels for 16%

commit v1 on v0

v1 whole, which is shorter than its diff:
```python
import functools
import math

import jax
import jax.numpy as jnp
from jax import lax
from jax.experimental import pallas as pl
from jax.experimental.pallas import tpu as pltpu
from jax.sharding import PartitionSpec as P


CAP = 2
ITERS = 3

momentum_rate = 0.95
step_size = 0.8
epsilon = 1e-07
poly_linear = 3.4445
poly_cubic = -4.775
poly_quintic = 2.0315


HBM = pl.BlockSpec(memory_space=pltpu.HBM)
SMEM = pl.BlockSpec(memory_space=pltpu.SMEM)
VMEM = pl.BlockSpec(memory_space=pltpu.VMEM)


def nesterov_of(grads, momentum):
    g = grads.astype(jnp.float32)
    velocity = momentum_rate * momentum.astype(jnp.float32) + g
    return velocity, (g + momentum_rate * velocity).astype(jnp.bfloat16)


def iotas(shape):
    return lax.broadcasted_iota(jnp.int32, shape, 0), lax.broadcasted_iota(jnp.int32, shape, 1)


def diagonal_of(square):
    rows, columns = iotas(square.shape)
    return jnp.sum(jnp.where(rows == columns, square, 0.0), axis=0, keepdims=True)


def pack(square):
    half = square.shape[0] // 2
    rows, columns = iotas((half, 2 * half))
    lower = jnp.concatenate([square[half:, half:], square[half:, :half]], axis=1)
    return jnp.where(columns >= rows, square[:half], lower)


def unpack(packed, diagonal):
    half = packed.shape[0]
    rows, columns = iotas(packed.shape)
    top = jnp.where(columns > rows, packed, 0.0)
    turned = jnp.concatenate([packed[:, half:], packed[:, :half]], axis=1)
    keep = jnp.logical_and(columns >= half, columns - half < rows)
    strict = jnp.concatenate([top, jnp.where(keep, turned, 0.0)], axis=0)
    rows, columns = iotas(strict.shape)
    return strict + strict.T + jnp.where(rows == columns, diagonal, 0.0)


def first_kernel(wanted, pieces, codes_ref, g_ref, m_ref, *refs):
    count = len(wanted)
    outs = refs[:count]
    g_buf, m_buf, y_buf, g_sem, m_sem, y_sem = refs[count:]
    rows = g_buf.shape[2]
    group = codes_ref.shape[1] // lax.axis_size("tp")
    row = lax.axis_index("tp")

    def in_copies(i, p, source):
        part = pl.ds(p * rows, rows)
        return (
            pltpu.make_async_copy(g_ref.at[source, part], g_buf.at[i, p], g_sem.at[i, p]),
            pltpu.make_async_copy(m_ref.at[source, part], m_buf.at[i, p], m_sem.at[i, p]),
        )

    def out_copy(i, p):
        return pltpu.make_async_copy(y_buf.at[i, p], outs[i].at[0, pl.ds(p * rows, rows)], y_sem.at[i, p])

    reads = []
    for i, (place_of, c) in enumerate(wanted):
        place = place_of(row) * group + c
        source = jnp.int32(0)
        for j in range(codes_ref.shape[1]):
            source = jnp.where(codes_ref[0, j] == place, j, source)
        for p in range(pieces):
            reads.append((i, p, in_copies(i, p, source)))
            for copy in reads[-1][2]:
                copy.start()
    for i, p, copies in reads:
        for copy in copies:
            copy.wait()
        _, y = nesterov_of(g_buf[i, p], m_buf[i, p])
        y_buf[i, p] = y
        out_copy(i, p).start()
    for i, p, _ in reads:
        out_copy(i, p).wait()


def first_blocks(codes, grads, momentum, wanted, pieces=4):
    _, head, width = grads.shape
    count = len(wanted)
    buffer = pltpu.VMEM((count, pieces, head // pieces, width), jnp.bfloat16)
    return pl.pallas_call(
        functools.partial(first_kernel, wanted, pieces),
        out_shape=[jax.ShapeDtypeStruct((1, head, width), jnp.bfloat16)] * count,
        in_specs=[SMEM, HBM, HBM],
        out_specs=[HBM] * count,
        scratch_shapes=[buffer] * 3 + [pltpu.SemaphoreType.DMA((count, pieces))] * 3,
        name="first_blocks",
    )(codes, grads, momentum)


def all_kernel(spans, spread, tile, source, place, g_ref, m_ref, newm_ref, parts_ref, *refs):
    outs = refs[: len(spans)]
    g_buf, m_buf, v_buf, y_buf, g_sem, m_sem, v_sem, y_sem = refs[len(spans) :]
    blocks, head, width = g_buf.shape
    half = head // 2
    users = blocks // spread

    def in_copies(i):
        return (
            pltpu.make_async_copy(g_ref.at[source[i]], g_buf.at[i], g_sem.at[i]),
            pltpu.make_async_copy(m_ref.at[source[i]], m_buf.at[i], m_sem.at[i]),
        )

    def newm_copy(i):
        return pltpu.make_async_copy(v_buf.at[i], newm_ref.at[source[i]], v_sem.at[i])

    @pl.loop(0, blocks)
    def _(i):
        for copy in in_copies(i):
            copy.start()

    for f in range(users, parts_ref.shape[0]):
        parts_ref[f, : spread * half] = jnp.zeros((spread * half, head), jnp.float32)

    @pl.loop(0, blocks)
    def _(i):
        for copy in in_copies(i):
            copy.wait()
        gram = jnp.zeros((head, head), jnp.float32)
        for k in range(0, width, tile):
            part = pl.ds(k, tile)
            velocity, y = nesterov_of(g_buf[i, :, part], m_buf[i, :, part])
            v_buf[i, :, part] = velocity.astype(jnp.bfloat16)
            y_buf[i, :, part] = y
            gram = gram + lax.dot_general(
                y, y, (((1,), (1,)), ((), ())), preferred_element_type=jnp.float32
            )
        newm_copy(i).start()
        for (start, count), out in zip(spans, outs):

            @pl.when(jnp.logical_and(i >= start, i < start + count))
            def _():
                pltpu.make_async_copy(y_buf.at[i], out.at[i - start], y_sem.at[i]).start()

        to = place[i] // spread
        at = pl.multiple_of(place[i] % spread * half, half)
        parts_ref[to, pl.ds(at, half)] = pack(gram)
        diagonal = diagonal_of(gram)
        for f in range(parts_ref.shape[0]):
            parts_ref[f, pl.ds(spread * half + place[i], 1)] = diagonal

    @pl.loop(0, blocks)
    def _(i):
        newm_copy(i).wait()

    for (start, count), out in zip(spans, outs):
        for k in range(count):
            i = start + k
            pltpu.make_async_copy(y_buf.at[i], out.at[k], y_sem.at[i]).wait()


def all_blocks(source, place, grads, momentum, spans, spread, devices):
    blocks, head, width = grads.shape
    buffer = pltpu.VMEM(grads.shape, jnp.bfloat16)
    return pl.pallas_call(
        functools.partial(all_kernel, spans, spread, min(width, 256)),
        out_shape=[
            jax.ShapeDtypeStruct(grads.shape, jnp.bfloat16),
            jax.ShapeDtypeStruct((devices, spread * head // 2 + blocks, head), jnp.float32),
        ]
        + [jax.ShapeDtypeStruct((count, head, width), jnp.bfloat16) for _, count in spans],
        in_specs=[SMEM, SMEM, HBM, HBM],
        out_specs=[HBM, VMEM] + [HBM] * len(spans),
        scratch_shapes=[buffer] * 4 + [pltpu.SemaphoreType.DMA((blocks,))] * 4,
        name="all_blocks",
    )(source, place, grads, momentum)


def solve_kernel(spread, count, elements, owners, codes, parts_ref, out_ref, slot_ref, sum_ref):
    n_fsdp, _, head = parts_ref.shape
    half = head // 2
    here = lax.axis_index("fsdp")
    total = parts_ref[0]
    for f in range(1, n_fsdp):
        total = total + parts_ref[f]
    diagonals = total[spread * half :]
    squares = jnp.sum(diagonals, axis=1, keepdims=True)
    sum_ref[:count] = diagonals
    sum_ref[count:] = jnp.broadcast_to(jnp.sqrt(squares / elements), (count, head))
    _, lanes = iotas((1, head))
    slots = jnp.zeros((1, head), jnp.float32)
    taken = jnp.int32(0)
    for j in range(count):
        mine = owners[j, 0] == here
        value = sum_ref[pl.ds(count + codes[0, j], 1)]
        slots = slots + jnp.where(jnp.logical_and(mine, lanes == taken), value, 0.0)
        taken = taken + mine.astype(jnp.int32)
    slot_ref[...] = slots

    def dot(a, b):
        return jnp.dot(a, b, precision=lax.Precision.HIGHEST, preferred_element_type=jnp.float32)

    eye_rows, eye_columns = iotas((head, head))
    identity = jnp.where(eye_rows == eye_columns, 1.0, 0.0)
    work = []
    for k in range(spread):
        at = jnp.minimum(here * spread + k, count - 1)
        diagonal = sum_ref[pl.ds(at, 1)]
        inverse = 1.0 / (jnp.sqrt(jnp.sum(diagonal, axis=1, keepdims=True)) + epsilon)
        gram = unpack(total[k * half : (k + 1) * half], diagonal) * (inverse * inverse)
        work.append((inverse, gram, None))
    for i in range(ITERS):
        last = i + 1 == ITERS
        squared = [dot(gram, gram) for _, gram, _ in work]
        mixed = [
            poly_linear * identity + poly_cubic * gram + poly_quintic * s
            for (_, gram, _), s in zip(work, squared)
        ]
        right = [None if last else dot(gram, m) for (_, gram, _), m in zip(work, mixed)]
        turned = [m if q is None else dot(m, q) for (_, _, q), m in zip(work, mixed)]
        grams = [None if last else dot(m, r) for m, r in zip(mixed, right)]
        work = [(inverse, gram, q) for (inverse, _, _), gram, q in zip(work, grams, turned)]
    for k, (inverse, _, q) in enumerate(work):
        q = q * inverse
        out_ref[k * half : (k + 1) * half] = pack(q)
        out_ref[spread * half + k : spread * half + k + 1] = diagonal_of(q)
    rest = out_ref.shape[0] - spread * half - spread
    out_ref[spread * half + spread :] = jnp.zeros((rest, head), jnp.float32)


def solve(parts, owners, codes, spread, elements):
    _, _, head = parts.shape
    count = codes.shape[1]
    return pl.pallas_call(
        functools.partial(solve_kernel, spread, count, elements),
        out_shape=[
            jax.ShapeDtypeStruct((spread * head // 2 + 8 * -(-spread // 8), head), jnp.float32),
            jax.ShapeDtypeStruct((1, head), jnp.float32),
        ],
        in_specs=[SMEM, SMEM, VMEM],
        out_specs=[VMEM, VMEM],
        scratch_shapes=[pltpu.VMEM((2 * count, head), jnp.float32)],
        name="solve",
    )(owners, codes, parts)


def unpack_kernel(spread, packed_ref, out_ref):
    head = packed_ref.shape[2]
    half = head // 2

    @pl.loop(0, out_ref.shape[0] // spread)
    def _(f):
        for k in range(spread):
            packed = packed_ref[f, k * half : (k + 1) * half]
            q = unpack(packed, packed_ref[f, spread * half + k : spread * half + k + 1])
            high = q.astype(jnp.bfloat16)
            out_ref[f * spread + k, :head] = high
            out_ref[f * spread + k, head:] = (q - high.astype(jnp.float32)).astype(jnp.bfloat16)


def unpack_all(packed, spread, blocks):
    head = packed.shape[2]
    return pl.pallas_call(
        functools.partial(unpack_kernel, spread),
        out_shape=jax.ShapeDtypeStruct((blocks, 2 * head, head), jnp.bfloat16),
        in_specs=[VMEM],
        out_specs=VMEM,
        name="unpack_all",
    )(packed)


def apply_kernel(factor, counts, tiles, aliased, place, q_ref, *refs):
    chunks = refs[: len(counts)]
    out = refs[len(counts) + aliased]
    q_buf, y_buf, u_buf, q_sem, y_sem, u_sem = refs[len(counts) + aliased + 1 :]
    head = y_buf.shape[1]
    width = y_buf.shape[2] // tiles
    members = [(chunk, k) for chunk, count in zip(chunks, counts) for k in range(count)]

    def q_copy(i):
        return pltpu.make_async_copy(q_ref.at[place[i]], q_buf.at[i], q_sem.at[i])

    def y_copy(i, j):
        chunk, k = members[i]
        part = pl.ds(j * width, width)
        return pltpu.make_async_copy(chunk.at[k, :, part], y_buf.at[i, :, part], y_sem.at[i, j])

    def u_copy(i, j):
        part = pl.ds(j * width, width)
        return pltpu.make_async_copy(u_buf.at[i, :, part], out.at[place[i], :, part], u_sem.at[i, j])

    for i in range(len(members)):
        q_copy(i).start()
        for j in range(tiles):
            y_copy(i, j).start()
    for i in range(len(members)):
        q_copy(i).wait()
        for j in range(tiles):
            y_copy(i, j).wait()
            part = pl.ds(j * width, width)
            ortho = jnp.dot(q_buf[i], y_buf[i, :, part], preferred_element_type=jnp.float32)
            ortho = ortho[:head] + ortho[head:]
            ortho = ortho.astype(jnp.bfloat16).astype(jnp.float32)
            u_buf[i, :, part] = (-factor * ortho).astype(jnp.bfloat16)
            u_copy(i, j).start()
    for i in range(len(members)):
        for j in range(tiles):
            u_copy(i, j).wait()


def apply_blocks(factor, place, transforms, chunks, into, tiles):
    head, width = chunks[0].shape[1:]
    blocks = transforms.shape[0]
    counts = [chunk.shape[0] for chunk in chunks]
    total = sum(counts)
    in_specs = [SMEM] + [HBM] * (1 + len(chunks))
    operands = [place, transforms, *chunks]
    aliases = {}
    if into is not None:
        aliases = {len(operands): 0}
        in_specs.append(HBM)
        operands.append(into)
    buffer = pltpu.VMEM((total, head, width), jnp.bfloat16)
    copies = pltpu.SemaphoreType.DMA((total, tiles))
    return pl.pallas_call(
        functools.partial(apply_kernel, factor, counts, tiles, len(aliases)),
        out_shape=jax.ShapeDtypeStruct((blocks, head, width), jnp.bfloat16),
        in_specs=in_specs,
        out_specs=HBM,
        scratch_shapes=[
            pltpu.VMEM((total, 2 * head, head), jnp.bfloat16),
            buffer,
            buffer,
            pltpu.SemaphoreType.DMA((total,)),
            copies,
            copies,
        ],
        input_output_aliases=aliases,
        name="apply_blocks",
    )(*operands)


def local(grads, momentum, owner_table, pool_map):
    n_fsdp, n_tp = lax.axis_size("fsdp"), lax.axis_size("tp")
    row = lax.axis_index("tp")
    blocks, head, width = grads.shape
    group = blocks // n_tp
    spread = -(-blocks // n_fsdp)
    paired = n_tp & (n_tp - 1) == 0

    def partner(t, x):
        return t ^ x if paired else (t + x) % n_tp

    def sender(t, x):
        return t ^ x if paired else (t - x) % n_tp

    far = [x for x in range(1, n_tp) if x >= n_tp // 2]
    near = [x for x in range(1, n_tp) if x < n_tp // 2]
    singles = [(x, (c,)) for c in range(group) for x in far]
    held = max(1, len(singles) * 3 // 8)
    first, middle, late = singles[:1], singles[1 : len(singles) - held], singles[len(singles) - held :]
    early = first + [(x, tuple(range(group))) for x in near] + middle
    own = [(0, tuple(range(group)))]
    chunks = early + late + own
    steps = [(x, c) for x, cs in chunks for c in cs]

    codes = pool_map[0]
    position = jnp.arange(blocks, dtype=jnp.int32)
    offsets = jnp.array([c for _, c in steps], jnp.int32)
    partners = jnp.array([x for x, _ in steps], jnp.int32)
    place_out = partner(row, partners) * group + offsets
    place_in = sender(row, partners) * group + offsets
    source = jnp.sum(jnp.where(codes[None, :] == place_out[:, None], position[None, :], 0), axis=1)

    starts, total = {}, 0
    for chunk in chunks:
        starts[chunk] = (total, len(chunk[1]))
        total += len(chunk[1])

    got = {}

    def send(chunk, array):
        got[chunk] = lax.ppermute(array, "tp", [(t, partner(t, chunk[0])) for t in range(n_tp)])

    wanted = [(functools.partial(partner, x=x), cs[0]) for x, cs in first]
    for chunk, array in zip(first, first_blocks(pool_map, grads, momentum, wanted)):
        send(chunk, array)
    rest = chunks[len(first) :]
    new_momentum, parts, *ys = all_blocks(
        source, place_out, grads, momentum, [starts[chunk] for chunk in rest], spread, n_fsdp
    )
    ys = dict(zip(rest, ys))
    for chunk in rest[: -len(own)]:
        send(chunk, ys[chunk])

    parts = lax.all_to_all(parts, "fsdp", split_axis=0, concat_axis=0, tiled=True)
    packed, slots = solve(parts, owner_table, pool_map, spread, head * width * n_fsdp)

    pairs = []
    per_row = group // spread
    for f in range(blocks // spread):
        for t in range(n_tp):
            to = (t * per_row + f % per_row) * n_tp + f // per_row
            pairs.append((f * n_tp + t, to))
    packed = lax.ppermute(packed, ("fsdp", "tp"), pairs)
    packed = jnp.broadcast_to(packed[None], (n_fsdp,) + packed.shape)
    packed = lax.all_to_all(packed, "fsdp", split_axis=0, concat_axis=0, tiled=True)
    transforms = unpack_all(packed, spread, blocks)

    factor = step_size * 0.2 * math.sqrt(width * n_fsdp)
    for chunk in own:
        got[chunk] = ys[chunk]
    update = None
    for members in [own + early] + [[chunk] for chunk in late]:
        where = jnp.concatenate([place_in[s : s + n] for s, n in (starts[chunk] for chunk in members)])
        tiles = 1 if len(members) > 1 or width < 512 else 4
        update = apply_blocks(factor, where, transforms, [got[chunk] for chunk in members], update, tiles)
    return (new_momentum, update, slots[:, :CAP])


def solution(mesh):
    def step(*args):
        return local(*args)

    in_specs = (P("tp", None, "fsdp"), P("tp", None, "fsdp"), P("tp", None), P("tp", None))
    out_specs = (P("tp", None, "fsdp"), P("tp", None, "fsdp"), P("tp", "fsdp"))
    step = jax.shard_map(step, mesh=mesh, in_specs=in_specs, out_specs=out_specs, check_vma=False)
    return step
```

time: 158 us -> 136 us (0.86)
  the two profiles are of different devices: /device:TPU:18 before, /device:TPU:0 now
where the time goes in v1:
time: 136 us; the launch traced here: 135 us
  starting transfers between devices  51.9 us (38%)
  waiting for transfers between devices  37.7 us (28%)
  Pallas kernels  35.5 us (26%)
  local copies, waits for them, and re-layouts  6.32 us (5%)
  other arithmetic  2.64 us (2%)
    ppermute x9, starting transfers between devices, send(): lax.ppermute(array, 'tp', [(t, partner(t, chunk[0])) for t in range(n_tp)])  32.5 us
    ppermute x9, waiting for transfers between devices, send(): lax.ppermute(array, 'tp', [(t, partner(t, chunk[0])) for t in range(n_tp)])  29.6 us
    pallas_call x4, Pallas kernels, apply_blocks(): pl.pallas_call(functools.partial(apply_kernel, factor, counts, tiles, len...  15.7 us
    all_to_all x1, starting transfers between devices, local(): lax.all_to_all(packed, 'fsdp', split_axis=0, concat_axis=0, tiled=True)  12.5 us
    pallas_call x1, Pallas kernels, all_blocks(): pl.pallas_call(functools.partial(all_kernel, spans, spread, min(width, 25...  10.1 us
    all_to_all x1, waiting for transfers between devices, local(): lax.all_to_all(parts, 'fsdp', split_axis=0, concat_axis=0, tiled=True)  8.16 us
    all_to_all x1, starting transfers between devices, local(): lax.all_to_all(parts, 'fsdp', split_axis=0, concat_axis=0, tiled=True)  5.21 us
    unnamed x31, local copies, waits for them, and re-layouts  4.78 us
  transfers between devices with their start and end apart: 12, of which 4 were waited for; matrix products, arithmetic and copies ran while one was open for 2% of the time, Pallas kernels for 17%

profile of v1, /device:TPU:0, one launch (start us, length us, event | category | flops | bytes accessed | tf_op | source)
XLA Modules:
  0.0 134.8 jit_solution(6200479876519569022)
XLA Ops:
  0.6 0.7 multiply_add_fusion.place
  1.3 1.4 %select_reduce_fusion.source = s32[16]{0:T(128)} fusion(s32[16]{0:T(128)} %bitcast.4, s32[16]{0:T(128)S(1)} %multiply_add_fusion.place), kind=kLoop, calls=%fused_computation | loop fusion | flops 752 | bytes 192 | tf_op jit(solution)/shard_map/reduce_sum | solution.py:385
  2.7 10.1 %all_blocks.1 = (bf16[16,128,1024]{2,1,0:T(8,128)(2,1)}, f32[8,144,128]{2,1,0:T(8,128)}, bf16[4,128,1024]{2,1,0:T(8,128)(2,1)}, bf16[1,128,1024]{2,1,0:T(8,128)(...) custom-call(s32[16]{0:T(128)} %select_reduce_fusion.source, ...), custom_call_target="tpu_custom_call" | custom-call | tf_op jit(solution)/shard_map/all_blocks/pallas_call | solution.py:177
  12.7 5.2 %all-to-all-start = ((f32[8,144,128]{2,1,0:T(8,128)}), f32[8,144,128]{2,1,0:T(8,128)S(1)}, u32[]{:S(2)}, u32[]{:S(2)}) async-start(f32[8,144,128]{2,1,0:T(8,128)} %get-tuple-element.17), calls=%async_computation | async-start | bytes 1179648 | tf_op jit(solution)/shard_map/all_to_all | solution.py:408
  17.9 1.6 %collective-permute-start.5 = (bf16[4,128,1024]{2,1,0:T(8,128)(2,1)}, bf16[4,128,1024]{2,1,0:T(8,128)(2,1)S(1)}, u32[]{:S(2)}, u32[]{:S(2)}) collective-permute-start(bf16[4,128,1024]{2,1,0:T(8,128)(2,1)} %get-tuple-element.23), channel_id=1, source_target_pairs={{0,1},{1,0},{2,3},{3,2},{4,5},{5,4},{6,7},{7,6},{8,9},{9,8},{10,11... | collective-permute-start | bytes 3145736 | tf_op jit(solution)/shard_map/ppermute | solution.py:395
  19.5 0.7 copy.13.owners
  20.2 8.2 %all-to-all-done.parts_ref = f32[8,144,128]{2,1,0:T(8,128)S(1)} async-done(((f32[8,144,128]{2,1,0:T(8,128)}), f32[8,144,128]{2,1,0:T(8,128)S(1)}, u32[]{:S(2)}, u32[]{:S(2)}) %all-to-all-start) | async-done | bytes 589856 | tf_op jit(solution)/shard_map/all_to_all | solution.py:408
  28.4 0.8 copy-done
  29.2 3.9 %solve.1 = (f32[136,128]{1,0:T(8,128)}, f32[1,128]{1,0:T(1,128)}) custom-call(s32[16,1]{1,0:T(8,128)} %copy.13.owners, s32[1,16]{1,0:T(1,128)} %codes_ref.1, f32[8,144,128]{2,1,0:T(8,128)} %copy-done), custom_call_target="tpu_custom_call" | custom-call | tf_op jit(solution)/shard_map/solve/pallas_call | solution.py:246
  33.1 1.7 %collective-permute-start = (f32[136,128]{1,0:T(8,128)}, f32[136,128]{1,0:T(8,128)S(1)}, u32[]{:S(2)}, u32[]{:S(2)}) collective-permute-start(f32[136,128]{1,0:T(8,128)} %get-tuple-element.18), channel_id=1, source_target_pairs={{0,0},{1,8},{2,16},{3,24},{4,4},{5,12},{6,20},{7,28},{8,1},{9,9},{... | collective-permute-start | bytes 208904 | tf_op jit(solution)/shard_map/ppermute | solution.py:417
  34.8 2.5 %first_blocks.1 = bf16[1,128,1024]{2,1,0:T(8,128)(2,1)} custom-call(s32[1,16]{1,0:T(1,128)} %codes_ref.1, bf16[16,128,1024]{2,1,0:T(8,128)(2,1)} %g_ref.3, bf16[16,128,1024]{2,1,0:T(8,128)(2,1)} %m_ref.3), custom_call_target="tpu_custom_call" | custom-call | tf_op jit(solution)/shard_map/first_blocks/pallas_call | solution.py:103
  37.3 3.4 %collective-permute-start.4 = (bf16[1,128,1024]{2,1,0:T(8,128)(2,1)}, bf16[1,128,1024]{2,1,0:T(8,128)(2,1)S(1)}, u32[]{:S(2)}, u32[]{:S(2)}) collective-permute-start(bf16[1,128,1024]{2,1,0:T(8,128)(2,1)} %first_blocks.1), channel_id=1, source_target_pairs={{0,2},{1,3},{2,0},{3,1},{4,6},{5,7},{6,4},{7,5},{8,10},{9,11},{10,... | collective-permute-start | bytes 786440 | tf_op jit(solution)/shard_map/ppermute | solution.py:395
  40.7 0.0 copy-done.14
  40.7 1.5 %collective-permute-start.6 = (bf16[1,128,1024]{2,1,0:T(8,128)(2,1)S(1)}, bf16[1,128,1024]{2,1,0:T(8,128)(2,1)S(1)}, u32[]{:S(2)}, u32[]{:S(2)}) collective-permute-start(bf16[1,128,1024]{2,1,0:T(8,128)(2,1)S(1)} %copy-done.14), channel_id=1, source_target_pairs={{0,3},{1,2},{2,1},{3,0},{4,7},{5,6},{6,5},{7,4},{8,11},{9,10},{10,... | collective-permute-start | bytes 786440 | tf_op jit(solution)/shard_map/ppermute | solution.py:395
  42.1 1.5 %collective-permute-start.7 = (bf16[1,128,1024]{2,1,0:T(8,128)(2,1)}, bf16[1,128,1024]{2,1,0:T(8,128)(2,1)S(1)}, u32[]{:S(2)}, u32[]{:S(2)}) collective-permute-start(bf16[1,128,1024]{2,1,0:T(8,128)(2,1)} %get-tuple-element.25), channel_id=1, source_target_pairs={{0,2},{1,3},{2,0},{3,1},{4,6},{5,7},{6,4},{7,5},{8,10},{9,11},{10,... | collective-permute-start | bytes 786440 | tf_op jit(solution)/shard_map/ppermute | solution.py:395
  43.6 0.0 collective-permute-done
  43.6 7.9 %collective-permute-start.8 = (bf16[1,128,1024]{2,1,0:T(8,128)(2,1)S(1)}, bf16[1,128,1024]{2,1,0:T(8,128)(2,1)S(1)}, u32[]{:S(2)}, u32[]{:S(2)}) collective-permute-start(bf16[1,128,1024]{2,1,0:T(8,128)(2,1)S(1)} %copy-done.13), channel_id=1, source_target_pairs={{0,3},{1,2},{2,1},{3,0},{4,7},{5,6},{6,5},{7,4},{8,11},{9,10},{10,... | collective-permute-start | bytes 786440 | tf_op jit(solution)/shard_map/ppermute | solution.py:395
  51.5 0.9 broadcast_in_dim.22
  52.4 12.5 %all-to-all-start.1 = ((f32[8,136,128]{2,1,0:T(8,128)}), f32[8,136,128]{2,1,0:T(8,128)S(1)}, u32[]{:S(2)}, u32[]{:S(2)}) async-start(f32[8,136,128]{2,1,0:T(8,128)} %broadcast_in_dim.22), calls=%async_computation.1 | async-start | bytes 1114112 | tf_op jit(solution)/shard_map/all_to_all | solution.py:419
  64.9 6.8 %collective-permute-done.4.refs_1_ = bf16[1,128,1024]{2,1,0:T(8,128)(2,1)S(1)} collective-permute-done((bf16[1,128,1024]{2,1,0:T(8,128)(2,1)}, bf16[1,128,1024]{2,1,0:T(8,128)(2,1)S(1)}, u32[]{:S(2)}, u32[]{:S(2)}) %collective-permute-start.4) | collective-permute-done | bytes 262176 | tf_op jit(solution)/shard_map/ppermute | solution.py:395
  71.7 0.0 collective-permute-start.9
  71.7 0.0 collective-permute-done.6.refs_3_
  71.7 5.5 %collective-permute-start.3 = (bf16[1,128,1024]{2,1,0:T(8,128)(2,1)}, bf16[1,128,1024]{2,1,0:T(8,128)(2,1)S(1)}, u32[]{:S(2)}, u32[]{:S(2)}) collective-permute-start(bf16[1,128,1024]{2,1,0:T(8,128)(2,1)} %get-tuple-element.21), channel_id=1, source_target_pairs={{0,3},{1,2},{2,1},{3,0},{4,7},{5,6},{6,5},{7,4},{8,11},{9,10},{10,... | collective-permute-start | bytes 786440 | tf_op jit(solution)/shard_map/ppermute | solution.py:395
  77.2 16.9 %collective-permute-done.7.refs_4_ = bf16[1,128,1024]{2,1,0:T(8,128)(2,1)S(1)} collective-permute-done((bf16[1,128,1024]{2,1,0:T(8,128)(2,1)}, bf16[1,128,1024]{2,1,0:T(8,128)(2,1)S(1)}, u32[]{:S(2)}, u32[]{:S(2)}) %collective-permute-start.7) | collective-permute-done | bytes 262176 | tf_op jit(solution)/shard_map/ppermute | solution.py:395
  94.1 0.0 collective-permute-start.2
  94.1 0.0 collective-permute-done.8.refs_5_
  94.2 0.0 copy-start.6
  94.2 11.2 %collective-permute-start.1 = (bf16[1,128,1024]{2,1,0:T(8,128)(2,1)}, bf16[1,128,1024]{2,1,0:T(8,128)(2,1)S(1)}, u32[]{:S(2)}, u32[]{:S(2)}) collective-permute-start(bf16[1,128,1024]{2,1,0:T(8,128)(2,1)} %get-tuple-element.19), channel_id=1, source_target_pairs={{0,3},{1,2},{2,1},{3,0},{4,7},{5,6},{6,5},{7,4},{8,11},{9,10},{10,... | collective-permute-start | bytes 786440 | tf_op jit(solution)/shard_map/ppermute | solution.py:395
  105.3 0.0 copy-done.11
  105.3 0.1 slice.27
  105.4 0.6 pad_add_fusion.place
  106.0 0.6 fusion
  106.6 0.0 all-to-all-done.1.packed_ref
  106.6 0.8 copy-done.1
  107.5 3.3 %unpack_all.1.q_ref = bf16[16,256,128]{2,1,0:T(8,128)(2,1)} custom-call(f32[8,136,128]{2,1,0:T(8,128)} %copy-done.1), custom_call_target="tpu_custom_call" | custom-call | tf_op jit(solution)/shard_map/unpack_all/pallas_call | solution.py:275
  110.8 5.9 %collective-permute-done.9.refs_6_ = bf16[1,128,1024]{2,1,0:T(8,128)(2,1)S(1)} collective-permute-done((bf16[1,128,1024]{2,1,0:T(8,128)(2,1)}, bf16[1,128,1024]{2,1,0:T(8,128)(2,1)S(1)}, u32[]{:S(2)}, u32[]{:S(2)}) %collective-permute-start.9) | collective-permute-done | bytes 262176 | tf_op jit(solution)/shard_map/ppermute | solution.py:395
  116.6 0.0 collective-permute-done.5.refs_2_
  116.7 0.7 copy-done.7
  117.3 0.4 copy-done.2
  117.7 6.4 %apply_blocks.4.refs_1_ = bf16[16,128,1024]{2,1,0:T(8,128)(2,1)} custom-call(s32[13]{0:T(128)} %pad_add_fusion.place, bf16[16,256,128]{2,1,0:T(8,128)(2,1)} %unpack_all.1.q_ref, bf16[4,128,1024]{2,1,0:T(8,128)(2,1)} %get-tuple-element.22.refs_0_, bf16[1,128,1024]{2,1,0:T(8,128)(2,1)} %copy-done.3, bf16[4,128,1024]{2,1,0:T(8,128)(2,1)} %copy-done.2, ...), custom_call_target="tpu_custom_call" | custom-call | tf_op jit(solution)/shard_map/apply_blocks/pallas_call | solution.py:337
  124.2 0.0 collective-permute-done.3.refs_0_
  124.2 0.7 copy-done.9
  124.9 3.1 %apply_blocks.5.refs_1_ = bf16[16,128,1024]{2,1,0:T(8,128)(2,1)} custom-call(s32[1]{0:T(128)} %get-tuple-element.29.place, bf16[16,256,128]{2,1,0:T(8,128)(2,1)} %unpack_all.1.q_ref, bf16[1,128,1024]{2,1,0:T(8,128)(2,1)} %copy-done.9, bf16[16,128,1024]{2,1,0:T(8,128)(2,1)} %apply_blocks.4.refs_1_), custom_call_target="tpu_custom_call", output_to_operand_aliasing={{}: (3, {})} | custom-call | tf_op jit(solution)/shard_map/apply_blocks/pallas_call | solution.py:337
  128.0 0.0 collective-permute-done.2.refs_0_
  128.0 3.1 %apply_blocks.6.refs_1_ = bf16[16,128,1024]{2,1,0:T(8,128)(2,1)} custom-call(s32[1]{0:T(128)} %get-tuple-element.30.place, bf16[16,256,128]{2,1,0:T(8,128)(2,1)} %unpack_all.1.q_ref, bf16[1,128,1024]{2,1,0:T(8,128)(2,1)} %collective-permute-done.2.refs_0_, bf16[16,128,1024]{2,1,0:T(8,128)(2,1)} %apply_blocks.5.refs_1_), custom_call_target="tpu_custom_call", output_to_operand_aliasing={{}: (3, {})} | custom-call | tf_op jit(solution)/shard_map/apply_blocks/pallas_call | solution.py:337
  131.0 0.0 collective-permute-done.1.refs_0_
  131.1 0.7 copy-done.8
  131.8 3.1 %apply_blocks.7 = bf16[16,128,1024]{2,1,0:T(8,128)(2,1)} custom-call(s32[1]{0:T(128)} %get-tuple-element.31.place, bf16[16,256,128]{2,1,0:T(8,128)(2,1)} %unpack_all.1.q_ref, bf16[1,128,1024]{2,1,0:T(8,128)(2,1)} %copy-done.8, bf16[16,128,1024]{2,1,0:T(8,128)(2,1)} %apply_blocks.6.refs_1_), custom_call_target="tpu_custom_call", output_to_operand_aliasing={{}: (3, {})} | custom-call | tf_op jit(solution)/shard_map/apply_blocks/pallas_call | solution.py:337
  (21 shorter events, 0.0 us)
Async XLA Ops:
  1.3 1.4 %copy-start.10 = (s32[16]{0:T(128)}, s32[16]{0:T(128)S(1)}, u32[]{:S(2)}) copy-start(s32[16]{0:T(128)S(1)} %multiply_add_fusion.place) | copy-start | bytes 196
  2.7 16.9 %copy-start.12 = (s32[16,1]{0,1:T(1,128)S(1)}, s32[16,1]{0,1:T(1,128)}, u32[]{:S(2)}) copy-start(s32[16,1]{0,1:T(1,128)} %param.8) | copy-start | bytes 196
  12.7 15.6 %all-to-all-start = ((f32[8,144,128]{2,1,0:T(8,128)}), f32[8,144,128]{2,1,0:T(8,128)S(1)}, u32[]{:S(2)}, u32[]{:S(2)}) async-start(f32[8,144,128]{2,1,0:T(8,128)} %get-tuple-element.17), calls=%async_computation | async-start | bytes 1179648 | tf_op jit(solution)/shard_map/all_to_all | solution.py:408
  17.9 98.7 %collective-permute-start.5 = (bf16[4,128,1024]{2,1,0:T(8,128)(2,1)}, bf16[4,128,1024]{2,1,0:T(8,128)(2,1)S(1)}, u32[]{:S(2)}, u32[]{:S(2)}) collective-permute-start(bf16[4,128,1024]{2,1,0:T(8,128)(2,1)} %get-tuple-element.23), channel_id=1, source_target_pairs={{0,1},{1,0},{2,3},{3,2},{4,5},{5,4},{6,7},{7,6},{8,9},{9,8},{10,11... | collective-permute-start | bytes 3145736 | tf_op jit(solution)/shard_map/ppermute | solution.py:395
  28.4 0.8 copy-start
  33.1 7.6 %copy-start.14 = (bf16[1,128,1024]{2,1,0:T(8,128)(2,1)S(1)}, bf16[1,128,1024]{2,1,0:T(8,128)(2,1)}, u32[]{:S(2)}) copy-start(bf16[1,128,1024]{2,1,0:T(8,128)(2,1)} %get-tuple-element.24) | copy-start | bytes 786436
  33.1 10.5 %copy-start.13 = (bf16[1,128,1024]{2,1,0:T(8,128)(2,1)S(1)}, bf16[1,128,1024]{2,1,0:T(8,128)(2,1)}, u32[]{:S(2)}) copy-start(bf16[1,128,1024]{2,1,0:T(8,128)(2,1)} %get-tuple-element.26) | copy-start | bytes 786436
  33.1 72.2 %copy-start.11 = (s32[16]{0:T(128)S(1)}, s32[16]{0:T(128)}, u32[]{:S(2)}) copy-start(s32[16]{0:T(128)} %copy-done.10) | copy-start | bytes 196
  33.1 10.5 %collective-permute-start = (f32[136,128]{1,0:T(8,128)}, f32[136,128]{1,0:T(8,128)S(1)}, u32[]{:S(2)}, u32[]{:S(2)}) collective-permute-start(f32[136,128]{1,0:T(8,128)} %get-tuple-element.18), channel_id=1, source_target_pairs={{0,0},{1,8},{2,16},{3,24},{4,4},{5,12},{6,20},{7,28},{8,1},{9,9},{... | collective-permute-start | bytes 208904 | tf_op jit(solution)/shard_map/ppermute | solution.py:417
  37.3 34.4 %collective-permute-start.4 = (bf16[1,128,1024]{2,1,0:T(8,128)(2,1)}, bf16[1,128,1024]{2,1,0:T(8,128)(2,1)S(1)}, u32[]{:S(2)}, u32[]{:S(2)}) collective-permute-start(bf16[1,128,1024]{2,1,0:T(8,128)(2,1)} %first_blocks.1), channel_id=1, source_target_pairs={{0,2},{1,3},{2,0},{3,1},{4,6},{5,7},{6,4},{7,5},{8,10},{9,11},{10,... | collective-permute-start | bytes 786440 | tf_op jit(solution)/shard_map/ppermute | solution.py:395
  40.7 31.0 %collective-permute-start.6 = (bf16[1,128,1024]{2,1,0:T(8,128)(2,1)S(1)}, bf16[1,128,1024]{2,1,0:T(8,128)(2,1)S(1)}, u32[]{:S(2)}, u32[]{:S(2)}) collective-permute-start(bf16[1,128,1024]{2,1,0:T(8,128)(2,1)S(1)} %copy-done.14), channel_id=1, source_target_pairs={{0,3},{1,2},{2,1},{3,0},{4,7},{5,6},{6,5},{7,4},{8,11},{9,10},{10,... | collective-permute-start | bytes 786440 | tf_op jit(solution)/shard_map/ppermute | solution.py:395
  42.1 52.0 %collective-permute-start.7 = (bf16[1,128,1024]{2,1,0:T(8,128)(2,1)}, bf16[1,128,1024]{2,1,0:T(8,128)(2,1)S(1)}, u32[]{:S(2)}, u32[]{:S(2)}) collective-permute-start(bf16[1,128,1024]{2,1,0:T(8,128)(2,1)} %get-tuple-element.25), channel_id=1, source_target_pairs={{0,2},{1,3},{2,0},{3,1},{4,6},{5,7},{6,4},{7,5},{8,10},{9,11},{10,... | collective-permute-start | bytes 786440 | tf_op jit(solution)/shard_map/ppermute | solution.py:395
  43.6 50.5 %collective-permute-start.8 = (bf16[1,128,1024]{2,1,0:T(8,128)(2,1)S(1)}, bf16[1,128,1024]{2,1,0:T(8,128)(2,1)S(1)}, u32[]{:S(2)}, u32[]{:S(2)}) collective-permute-start(bf16[1,128,1024]{2,1,0:T(8,128)(2,1)S(1)} %copy-done.13), channel_id=1, source_target_pairs={{0,3},{1,2},{2,1},{3,0},{4,7},{5,6},{6,5},{7,4},{8,11},{9,10},{10,... | collective-permute-start | bytes 786440 | tf_op jit(solution)/shard_map/ppermute | solution.py:395
  52.4 54.3 %all-to-all-start.1 = ((f32[8,136,128]{2,1,0:T(8,128)}), f32[8,136,128]{2,1,0:T(8,128)S(1)}, u32[]{:S(2)}, u32[]{:S(2)}) async-start(f32[8,136,128]{2,1,0:T(8,128)} %broadcast_in_dim.22), calls=%async_computation.1 | async-start | bytes 1114112 | tf_op jit(solution)/shard_map/all_to_all | solution.py:419
  71.7 45.0 %copy-start.3 = (bf16[1,128,1024]{2,1,0:T(8,128)(2,1)}, bf16[1,128,1024]{2,1,0:T(8,128)(2,1)S(1)}, u32[]{:S(2)}) copy-start(bf16[1,128,1024]{2,1,0:T(8,128)(2,1)S(1)} %collective-permute-done.4.refs_1_) | copy-start | bytes 786436
  71.7 44.9 %collective-permute-start.9 = (bf16[1,128,1024]{2,1,0:T(8,128)(2,1)}, bf16[1,128,1024]{2,1,0:T(8,128)(2,1)S(1)}, u32[]{:S(2)}, u32[]{:S(2)}) collective-permute-start(bf16[1,128,1024]{2,1,0:T(8,128)(2,1)} %get-tuple-element.27), channel_id=1, source_target_pairs={{0,2},{1,3},{2,0},{3,1},{4,6},{5,7},{6,4},{7,5},{8,10},{9,11},{10,... | collective-permute-start | bytes 786440 | tf_op jit(solution)/shard_map/ppermute | solution.py:395
  71.7 44.9 %copy-start.4 = (bf16[1,128,1024]{2,1,0:T(8,128)(2,1)}, bf16[1,128,1024]{2,1,0:T(8,128)(2,1)S(1)}, u32[]{:S(2)}) copy-start(bf16[1,128,1024]{2,1,0:T(8,128)(2,1)S(1)} %collective-permute-done.6.refs_3_) | copy-start | bytes 786436
  71.7 52.5 %collective-permute-start.3 = (bf16[1,128,1024]{2,1,0:T(8,128)(2,1)}, bf16[1,128,1024]{2,1,0:T(8,128)(2,1)S(1)}, u32[]{:S(2)}, u32[]{:S(2)}) collective-permute-start(bf16[1,128,1024]{2,1,0:T(8,128)(2,1)} %get-tuple-element.21), channel_id=1, source_target_pairs={{0,3},{1,2},{2,1},{3,0},{4,7},{5,6},{6,5},{7,4},{8,11},{9,10},{10,... | collective-permute-start | bytes 786440 | tf_op jit(solution)/shard_map/ppermute | solution.py:395
  94.1 22.5 %copy-start.5 = (bf16[1,128,1024]{2,1,0:T(8,128)(2,1)}, bf16[1,128,1024]{2,1,0:T(8,128)(2,1)S(1)}, u32[]{:S(2)}) copy-start(bf16[1,128,1024]{2,1,0:T(8,128)(2,1)S(1)} %collective-permute-done.7.refs_4_) | copy-start | bytes 786436
  94.1 33.8 %collective-permute-start.2 = (bf16[1,128,1024]{2,1,0:T(8,128)(2,1)}, bf16[1,128,1024]{2,1,0:T(8,128)(2,1)}, u32[]{:S(2)}, u32[]{:S(2)}) collective-permute-start(bf16[1,128,1024]{2,1,0:T(8,128)(2,1)} %get-tuple-element.20), channel_id=1, source_target_pairs={{0,2},{1,3},{2,0},{3,1},{4,6},{5,7},{6,4},{7,5},{8,10},{9,11},{10,... | collective-permute-start | bytes 786440 | tf_op jit(solution)/shard_map/ppermute | solution.py:395
  94.2 22.5 %copy-start.6 = (bf16[1,128,1024]{2,1,0:T(8,128)(2,1)}, bf16[1,128,1024]{2,1,0:T(8,128)(2,1)S(1)}, u32[]{:S(2)}) copy-start(bf16[1,128,1024]{2,1,0:T(8,128)(2,1)S(1)} %collective-permute-done.8.refs_5_) | copy-start | bytes 786436
  94.2 36.9 %collective-permute-start.1 = (bf16[1,128,1024]{2,1,0:T(8,128)(2,1)}, bf16[1,128,1024]{2,1,0:T(8,128)(2,1)S(1)}, u32[]{:S(2)}, u32[]{:S(2)}) collective-permute-start(bf16[1,128,1024]{2,1,0:T(8,128)(2,1)} %get-tuple-element.19), channel_id=1, source_target_pairs={{0,3},{1,2},{2,1},{3,0},{4,7},{5,6},{6,5},{7,4},{8,11},{9,10},{10,... | collective-permute-start | bytes 786440 | tf_op jit(solution)/shard_map/ppermute | solution.py:395
  106.6 0.8 copy-start.1
  116.6 0.7 copy-start.7
  116.6 1.1 copy-start.2
  124.2 0.7 copy-start.9
  131.1 0.7 copy-start.8

commit v2 on v1

--- a/solution.py
+++ b/solution.py
@@ -20,6 +20,7 @@
 poly_quintic = 2.0315
 
 
+VMEM_BYTES = 67043328
 HBM = pl.BlockSpec(memory_space=pltpu.HBM)
 SMEM = pl.BlockSpec(memory_space=pltpu.SMEM)
 VMEM = pl.BlockSpec(memory_space=pltpu.VMEM)
@@ -348,6 +349,7 @@
             copies,
         ],
         input_output_aliases=aliases,
+        compiler_params=pltpu.CompilerParams(vmem_limit_bytes=VMEM_BYTES),
         name="apply_blocks",
     )(*operands)
 
@@ -366,12 +368,22 @@
     def sender(t, x):
         return t ^ x if paired else (t - x) % n_tp
 
-    far = [x for x in range(1, n_tp) if x >= n_tp // 2]
+    far = [x for x in reversed(range(1, n_tp)) if x >= n_tp // 2]
     near = [x for x in range(1, n_tp) if x < n_tp // 2]
-    singles = [(x, (c,)) for c in range(group) for x in far]
-    held = max(1, len(singles) * 3 // 8)
-    first, middle, late = singles[:1], singles[1 : len(singles) - held], singles[len(singles) - held :]
-    early = first + [(x, tuple(range(group))) for x in near] + middle
+    cut = max(1, group // 2)
+
+    def singles(partners, places):
+        return [(x, (c,)) for c in places for x in partners]
+
+    first = singles(far, range(1))
+    middle = [chunk for c in range(1, cut) for chunk in singles(near, [c - 1]) + singles(far, [c])]
+    early = first + middle
+    late = singles(near, range(cut - 1, cut))
+    for c in range(cut, group - 1):
+        late += singles(far, [c]) + singles(near, [c])
+    late += singles(near, [group - 1]) if group > cut else []
+    last = singles(far, range(max(cut, group - 1), group))
+    late += last
     own = [(0, tuple(range(group)))]
     chunks = early + late + own
     steps = [(x, c) for x, cs in chunks for c in cs]
@@ -423,7 +435,9 @@
     for chunk in own:
         got[chunk] = ys[chunk]
     update = None
-    for members in [own + early] + [[chunk] for chunk in late]:
+    between = [chunk for chunk in late if chunk not in last]
+    rounds = [own + early] + ([between] if between else []) + [[chunk] for chunk in last]
+    for members in rounds:
         where = jnp.concatenate([place_in[s : s + n] for s, n in (starts[chunk] for chunk in members)])
         tiles = 1 if len(members) > 1 or width < 512 else 4
         update = apply_blocks(factor, where, transforms, [got[chunk] for chunk in members], update, tiles)

time: 136 us -> 123 us (0.904)
  waiting for transfers between devices: 37.7 us -> 22.5 us
  starting transfers between devices: 51.9 us -> 56.8 us
  local copies, waits for them, and re-layouts: 6.32 us -> 4.57 us
    ppermute x9 -> x12, waiting for transfers between devices: 29.6 us -> 16.8 us  [send(): lax.ppermute(array, 'tp', [(t, partner(t, chunk[0])) for t in range(n_tp)])]
    all_to_all x1, starting transfers between devices: 12.5 us -> 17.2 us  [local(): lax.all_to_all(packed, 'fsdp', split_axis=0, concat_axis=0, tiled=True)]
    all_to_all x1, waiting for transfers between devices: 8.16 us -> 5.68 us  [local(): lax.all_to_all(parts, 'fsdp', split_axis=0, concat_axis=0, tiled=True)]
    unnamed x31 -> x29, local copies, waits for them, and re-layouts: 4.78 us -> 2.34 us
    ppermute x9 -> x12, starting transfers between devices: 32.5 us -> 32.9 us  [send(): lax.ppermute(array, 'tp', [(t, partner(t, chunk[0])) for t in range(n_tp)])]
  transfers between devices with their start and end apart: 12 -> 15, of which waited for: 4 -> 3; matrix products, arithmetic and copies ran while one was open for 2% -> 3% of each run, Pallas kernels for 17% -> 18%
where the time goes in v2:
time: 123 us
  starting transfers between devices  56.8 us (46%)
  Pallas kernels  35.4 us (29%)
  waiting for transfers between devices  22.5 us (18%)
  local copies, waits for them, and re-layouts  4.57 us (4%)
  other arithmetic  2.7 us (2%)
    ppermute x12, starting transfers between devices, send(): lax.ppermute(array, 'tp', [(t, partner(t, chunk[0])) for t in range(n_tp)])  32.9 us
    all_to_all x1, starting transfers between devices, local(): lax.all_to_all(packed, 'fsdp', split_axis=0, concat_axis=0, tiled=True)  17.2 us
    ppermute x12, waiting for transfers between devices, send(): lax.ppermute(array, 'tp', [(t, partner(t, chunk[0])) for t in range(n_tp)])  16.8 us
    pallas_call x4, Pallas kernels, apply_blocks(): pl.pallas_call(functools.partial(apply_kernel, factor, counts, tiles, len...  15.3 us
    pallas_call x1, Pallas kernels, all_blocks(): pl.pallas_call(functools.partial(all_kernel, spans, spread, min(width, 25...  10.1 us
    all_to_all x1, waiting for transfers between devices, local(): lax.all_to_all(parts, 'fsdp', split_axis=0, concat_axis=0, tiled=True)  5.68 us
    all_to_all x1, starting transfers between devices, local(): lax.all_to_all(parts, 'fsdp', split_axis=0, concat_axis=0, tiled=True)  5.21 us
    pallas_call x1, Pallas kernels, solve(): pl.pallas_call(functools.partial(solve_kernel, spread, count, elements),...  3.94 us
  transfers between devices with their start and end apart: 15, of which 3 were waited for; matrix products, arithmetic and copies ran while one was open for 3% of the time, Pallas kernels for 18%

profile of v2, /device:TPU:0, one launch (start us, length us, event | category | flops | bytes accessed | tf_op | source)
XLA Modules:
  0.0 122.8 jit_solution(1639861242633918746)
XLA Ops:
  0.6 0.7 multiply_add_fusion.place
  1.3 1.3 %select_reduce_fusion.source = s32[16]{0:T(128)} fusion(s32[16]{0:T(128)} %bitcast.2, s32[16]{0:T(128)S(1)} %multiply_add_fusion.place), kind=kLoop, calls=%fused_computation | loop fusion | flops 752 | bytes 192 | tf_op jit(solution)/shard_map/reduce_sum | solution.py:397
  2.7 10.1 %all_blocks.1 = (bf16[16,128,1024]{2,1,0:T(8,128)(2,1)}, f32[8,144,128]{2,1,0:T(8,128)}, bf16[1,128,1024]{2,1,0:T(8,128)(2,1)}, bf16[1,128,1024]{2,1,0:T(8,128)(...) custom-call(s32[16]{0:T(128)} %select_reduce_fusion.source, ...), custom_call_target="tpu_custom_call" | custom-call | tf_op jit(solution)/shard_map/all_blocks/pallas_call | solution.py:178
  12.7 5.2 %all-to-all-start = ((f32[8,144,128]{2,1,0:T(8,128)}), f32[8,144,128]{2,1,0:T(8,128)S(1)}, u32[]{:S(2)}, u32[]{:S(2)}) async-start(f32[8,144,128]{2,1,0:T(8,128)} %get-tuple-element.21), calls=%async_computation | async-start | bytes 1179648 | tf_op jit(solution)/shard_map/all_to_all | solution.py:420
  17.9 1.6 %collective-permute-start.10 = (bf16[1,128,1024]{2,1,0:T(8,128)(2,1)}, bf16[1,128,1024]{2,1,0:T(8,128)(2,1)S(1)}, u32[]{:S(2)}, u32[]{:S(2)}) collective-permute-start(bf16[1,128,1024]{2,1,0:T(8,128)(2,1)} %get-tuple-element.33), channel_id=1, source_target_pairs={{0,1},{1,0},{2,3},{3,2},{4,5},{5,4},{6,7},{7,6},{8,9},{9,8},{10,11... | collective-permute-start | bytes 786440 | tf_op jit(solution)/shard_map/ppermute | solution.py:407
  19.5 2.5 %collective-permute-start.11 = (bf16[1,128,1024]{2,1,0:T(8,128)(2,1)}, bf16[1,128,1024]{2,1,0:T(8,128)(2,1)S(1)}, u32[]{:S(2)}, u32[]{:S(2)}) collective-permute-start(bf16[1,128,1024]{2,1,0:T(8,128)(2,1)} %get-tuple-element.34), channel_id=1, source_target_pairs={{0,3},{1,2},{2,1},{3,0},{4,7},{5,6},{6,5},{7,4},{8,11},{9,10},{10,... | collective-permute-start | bytes 786440 | tf_op jit(solution)/shard_map/ppermute | solution.py:407
  22.0 0.7 copy.13.owners
  22.7 5.7 %all-to-all-done.parts_ref = f32[8,144,128]{2,1,0:T(8,128)S(1)} async-done(((f32[8,144,128]{2,1,0:T(8,128)}), f32[8,144,128]{2,1,0:T(8,128)S(1)}, u32[]{:S(2)}, u32[]{:S(2)}) %all-to-all-start) | async-done | bytes 589856 | tf_op jit(solution)/shard_map/all_to_all | solution.py:420
  28.4 0.8 copy-done
  29.2 3.9 %solve.1 = (f32[136,128]{1,0:T(8,128)}, f32[1,128]{1,0:T(1,128)}) custom-call(s32[16,1]{1,0:T(8,128)} %copy.13.owners, s32[1,16]{1,0:T(1,128)} %codes_ref.1, f32[8,144,128]{2,1,0:T(8,128)} %copy-done), custom_call_target="tpu_custom_call" | custom-call | tf_op jit(solution)/shard_map/solve/pallas_call | solution.py:247
  33.1 1.5 %collective-permute-start = (f32[136,128]{1,0:T(8,128)}, f32[136,128]{1,0:T(8,128)S(1)}, u32[]{:S(2)}, u32[]{:S(2)}) collective-permute-start(f32[136,128]{1,0:T(8,128)} %get-tuple-element.22), channel_id=1, source_target_pairs={{0,0},{1,8},{2,16},{3,24},{4,4},{5,12},{6,20},{7,28},{8,1},{9,9},{... | collective-permute-start | bytes 208904 | tf_op jit(solution)/shard_map/ppermute | solution.py:429
  34.6 3.4 %collective-permute-start.12 = (bf16[1,128,1024]{2,1,0:T(8,128)(2,1)}, bf16[1,128,1024]{2,1,0:T(8,128)(2,1)S(1)}, u32[]{:S(2)}, u32[]{:S(2)}) collective-permute-start(bf16[1,128,1024]{2,1,0:T(8,128)(2,1)} %get-tuple-element.35), channel_id=1, source_target_pairs={{0,2},{1,3},{2,0},{3,1},{4,6},{5,7},{6,4},{7,5},{8,10},{9,11},{10,... | collective-permute-start | bytes 786440 | tf_op jit(solution)/shard_map/ppermute | solution.py:407
  38.0 2.8 %first_blocks.1 = (bf16[1,128,1024]{2,1,0:T(8,128)(2,1)}, bf16[1,128,1024]{2,1,0:T(8,128)(2,1)}) custom-call(s32[1,16]{1,0:T(1,128)} %codes_ref.1, bf16[16,128,1024]{2,1,0:T(8,128)(2,1)} %g_ref.3, bf16[16,128,1024]{2,1,0:T(8,128)(2,1)} %m_ref.3), custom_call_target="tpu_custom_call" | custom-call | tf_op jit(solution)/shard_map/first_blocks/pallas_call | solution.py:104
  40.8 1.5 %collective-permute-start.8 = (bf16[1,128,1024]{2,1,0:T(8,128)(2,1)}, bf16[1,128,1024]{2,1,0:T(8,128)(2,1)S(1)}, u32[]{:S(2)}, u32[]{:S(2)}) collective-permute-start(bf16[1,128,1024]{2,1,0:T(8,128)(2,1)} %get-tuple-element.31), channel_id=1, source_target_pairs={{0,3},{1,2},{2,1},{3,0},{4,7},{5,6},{6,5},{7,4},{8,11},{9,10},{10,... | collective-permute-start | bytes 786440 | tf_op jit(solution)/shard_map/ppermute | solution.py:407
  42.3 0.0 collective-permute-done.10.refs_3_
  42.4 1.5 %collective-permute-start.9 = (bf16[1,128,1024]{2,1,0:T(8,128)(2,1)}, bf16[1,128,1024]{2,1,0:T(8,128)(2,1)S(1)}, u32[]{:S(2)}, u32[]{:S(2)}) collective-permute-start(bf16[1,128,1024]{2,1,0:T(8,128)(2,1)} %get-tuple-element.32), channel_id=1, source_target_pairs={{0,2},{1,3},{2,0},{3,1},{4,6},{5,7},{6,4},{7,5},{8,10},{9,11},{10,... | collective-permute-start | bytes 786440 | tf_op jit(solution)/shard_map/ppermute | solution.py:407
  43.8 0.0 collective-permute-done.11.refs_4_
  43.8 1.5 %collective-permute-start.3 = (bf16[1,128,1024]{2,1,0:T(8,128)(2,1)S(1)}, bf16[1,128,1024]{2,1,0:T(8,128)(2,1)S(1)}, u32[]{:S(2)}, u32[]{:S(2)}) collective-permute-start(bf16[1,128,1024]{2,1,0:T(8,128)(2,1)S(1)} %copy-done.13), channel_id=1, source_target_pairs={{0,1},{1,0},{2,3},{3,2},{4,5},{5,4},{6,7},{7,6},{8,9},{9,8},{10,11... | collective-permute-start | bytes 786440 | tf_op jit(solution)/shard_map/ppermute | solution.py:407
  45.3 0.0 collective-permute-done
  45.4 1.5 %collective-permute-start.4 = (bf16[1,128,1024]{2,1,0:T(8,128)(2,1)S(1)}, bf16[1,128,1024]{2,1,0:T(8,128)(2,1)S(1)}, u32[]{:S(2)}, u32[]{:S(2)}) collective-permute-start(bf16[1,128,1024]{2,1,0:T(8,128)(2,1)S(1)} %copy-done.12), channel_id=1, source_target_pairs={{0,3},{1,2},{2,1},{3,0},{4,7},{5,6},{6,5},{7,4},{8,11},{9,10},{10,... | collective-permute-start | bytes 786440 | tf_op jit(solution)/shard_map/ppermute | solution.py:407
  46.8 0.8 broadcast_in_dim.22
  47.7 17.2 %all-to-all-start.1 = ((f32[8,136,128]{2,1,0:T(8,128)}), f32[8,136,128]{2,1,0:T(8,128)S(1)}, u32[]{:S(2)}, u32[]{:S(2)}) async-start(f32[8,136,128]{2,1,0:T(8,128)} %broadcast_in_dim.22), calls=%async_computation.1 | async-start | bytes 1114112 | tf_op jit(solution)/shard_map/all_to_all | solution.py:431
  64.9 11.5 %collective-permute-done.12.refs_5_ = bf16[1,128,1024]{2,1,0:T(8,128)(2,1)S(1)} collective-permute-done((bf16[1,128,1024]{2,1,0:T(8,128)(2,1)}, bf16[1,128,1024]{2,1,0:T(8,128)(2,1)S(1)}, u32[]{:S(2)}, u32[]{:S(2)}) %collective-permute-start.12) | collective-permute-done | bytes 262176 | tf_op jit(solution)/shard_map/ppermute | solution.py:407
  76.3 0.0 collective-permute-start.5
  76.3 0.0 collective-permute-done.8.refs_1_
  76.4 6.2 %collective-permute-start.6 = (bf16[1,128,1024]{2,1,0:T(8,128)(2,1)}, bf16[1,128,1024]{2,1,0:T(8,128)(2,1)}, u32[]{:S(2)}, u32[]{:S(2)}) collective-permute-start(bf16[1,128,1024]{2,1,0:T(8,128)(2,1)} %get-tuple-element.28), channel_id=1, source_target_pairs={{0,1},{1,0},{2,3},{3,2},{4,5},{5,4},{6,7},{7,6},{8,9},{9,8},{10,11... | collective-permute-start | bytes 786440 | tf_op jit(solution)/shard_map/ppermute | solution.py:407
  82.5 5.3 %collective-permute-done.9.refs_2_ = bf16[1,128,1024]{2,1,0:T(8,128)(2,1)S(1)} collective-permute-done((bf16[1,128,1024]{2,1,0:T(8,128)(2,1)}, bf16[1,128,1024]{2,1,0:T(8,128)(2,1)S(1)}, u32[]{:S(2)}, u32[]{:S(2)}) %collective-permute-start.9) | collective-permute-done | bytes 262176 | tf_op jit(solution)/shard_map/ppermute | solution.py:407
  87.9 0.0 collective-permute-start.7
  87.9 0.0 collective-permute-done.3.refs_0_
  87.9 0.8 collective-permute-start.2
  88.7 0.0 collective-permute-done.4.refs_1_
  88.7 12.5 %collective-permute-start.1 = (bf16[1,128,1024]{2,1,0:T(8,128)(2,1)}, bf16[1,128,1024]{2,1,0:T(8,128)(2,1)}, u32[]{:S(2)}, u32[]{:S(2)}) collective-permute-start(bf16[1,128,1024]{2,1,0:T(8,128)(2,1)} %get-tuple-element.23), channel_id=1, source_target_pairs={{0,2},{1,3},{2,0},{3,1},{4,6},{5,7},{6,4},{7,5},{8,10},{9,11},{10,... | collective-permute-start | bytes 786440 | tf_op jit(solution)/shard_map/ppermute | solution.py:407
  101.2 0.7 fusion
  101.8 0.1 slice.31
  101.9 0.7 pad_add_fusion.place
  102.6 0.7 fusion.1
  103.2 0.0 all-to-all-done.1.packed_ref
  103.3 0.8 copy-done.1
  104.1 3.3 %unpack_all.1.q_ref = bf16[16,256,128]{2,1,0:T(8,128)(2,1)} custom-call(f32[8,136,128]{2,1,0:T(8,128)} %copy-done.1), custom_call_target="tpu_custom_call" | custom-call | tf_op jit(solution)/shard_map/unpack_all/pallas_call | solution.py:276
  107.4 5.2 %apply_blocks.4.refs_5_ = bf16[16,128,1024]{2,1,0:T(8,128)(2,1)} custom-call(s32[9]{0:T(128)} %pad_add_fusion.place, bf16[16,256,128]{2,1,0:T(8,128)(2,1)} %unpack_all.1.q_ref, bf16[4,128,1024]{2,1,0:T(8,128)(2,1)} %get-tuple-element.30.refs_0_, bf16[1,128,1024]{2,1,0:T(8,128)(2,1)} %copy-done.5, bf16[1,128,1024]{2,1,0:T(8,128)(2,1)} %copy-done.8, ...), custom_call_target="tpu_custom_call" | custom-call | tf_op jit(solution)/shard_map/apply_blocks/pallas_call | solution.py:338
  112.6 0.0 collective-permute-done.5.refs_2_
  112.6 0.0 collective-permute-done.6.refs_3_
  112.6 0.0 collective-permute-done.7.refs_4_
  112.6 3.9 %apply_blocks.5.refs_1_ = bf16[16,128,1024]{2,1,0:T(8,128)(2,1)} custom-call(s32[5]{0:T(128)} %get-tuple-element.38.place, bf16[16,256,128]{2,1,0:T(8,128)(2,1)} %unpack_all.1.q_ref, bf16[1,128,1024]{2,1,0:T(8,128)(2,1)} %copy-done.6, bf16[1,128,1024]{2,1,0:T(8,128)(2,1)} %copy-done.7, ...), custom_call_target="tpu_custom_call", output_to_operand_aliasing={{}: (7, {})} | custom-call | tf_op jit(solution)/shard_map/apply_blocks/pallas_call | solution.py:338
  116.5 0.0 collective-permute-done.2.refs_0_
  116.6 3.2 %apply_blocks.6.refs_1_ = bf16[16,128,1024]{2,1,0:T(8,128)(2,1)} custom-call(s32[1]{0:T(128)} %get-tuple-element.39.place, bf16[16,256,128]{2,1,0:T(8,128)(2,1)} %unpack_all.1.q_ref, bf16[1,128,1024]{2,1,0:T(8,128)(2,1)} %collective-permute-done.2.refs_0_, bf16[16,128,1024]{2,1,0:T(8,128)(2,1)} %apply_blocks.5.refs_1_), custom_call_target="tpu_custom_call", output_to_operand_aliasing={{}: (3, {})} | custom-call | tf_op jit(solution)/shard_map/apply_blocks/pallas_call | solution.py:338
  119.7 0.0 collective-permute-done.1.refs_0_
  119.7 3.0 %apply_blocks.7 = bf16[16,128,1024]{2,1,0:T(8,128)(2,1)} custom-call(s32[1]{0:T(128)} %get-tuple-element.40.place, bf16[16,256,128]{2,1,0:T(8,128)(2,1)} %unpack_all.1.q_ref, bf16[1,128,1024]{2,1,0:T(8,128)(2,1)} %collective-permute-done.1.refs_0_, bf16[16,128,1024]{2,1,0:T(8,128)(2,1)} %apply_blocks.6.refs_1_), custom_call_target="tpu_custom_call", output_to_operand_aliasing={{}: (3, {})} | custom-call | tf_op jit(solution)/shard_map/apply_blocks/pallas_call | solution.py:338
  (26 shorter events, 0.0 us)
Async XLA Ops:
  1.3 1.4 %copy-start.9 = (s32[16]{0:T(128)}, s32[16]{0:T(128)S(1)}, u32[]{:S(2)}) copy-start(s32[16]{0:T(128)S(1)} %multiply_add_fusion.place) | copy-start | bytes 196
  2.7 19.3 %copy-start.11 = (s32[16,1]{0,1:T(1,128)S(1)}, s32[16,1]{0,1:T(1,128)}, u32[]{:S(2)}) copy-start(s32[16,1]{0,1:T(1,128)} %param.8) | copy-start | bytes 196
  12.7 15.6 %all-to-all-start = ((f32[8,144,128]{2,1,0:T(8,128)}), f32[8,144,128]{2,1,0:T(8,128)S(1)}, u32[]{:S(2)}, u32[]{:S(2)}) async-start(f32[8,144,128]{2,1,0:T(8,128)} %get-tuple-element.21), calls=%async_computation | async-start | bytes 1179648 | tf_op jit(solution)/shard_map/all_to_all | solution.py:420
  17.9 24.4 %collective-permute-start.10 = (bf16[1,128,1024]{2,1,0:T(8,128)(2,1)}, bf16[1,128,1024]{2,1,0:T(8,128)(2,1)S(1)}, u32[]{:S(2)}, u32[]{:S(2)}) collective-permute-start(bf16[1,128,1024]{2,1,0:T(8,128)(2,1)} %get-tuple-element.33), channel_id=1, source_target_pairs={{0,1},{1,0},{2,3},{3,2},{4,5},{5,4},{6,7},{7,6},{8,9},{9,8},{10,11... | collective-permute-start | bytes 786440 | tf_op jit(solution)/shard_map/ppermute | solution.py:407
  19.5 24.3 %collective-permute-start.11 = (bf16[1,128,1024]{2,1,0:T(8,128)(2,1)}, bf16[1,128,1024]{2,1,0:T(8,128)(2,1)S(1)}, u32[]{:S(2)}, u32[]{:S(2)}) collective-permute-start(bf16[1,128,1024]{2,1,0:T(8,128)(2,1)} %get-tuple-element.34), channel_id=1, source_target_pairs={{0,3},{1,2},{2,1},{3,0},{4,7},{5,6},{6,5},{7,4},{8,11},{9,10},{10,... | collective-permute-start | bytes 786440 | tf_op jit(solution)/shard_map/ppermute | solution.py:407
  28.4 0.8 copy-start
  33.1 12.2 %collective-permute-start = (f32[136,128]{1,0:T(8,128)}, f32[136,128]{1,0:T(8,128)S(1)}, u32[]{:S(2)}, u32[]{:S(2)}) collective-permute-start(f32[136,128]{1,0:T(8,128)} %get-tuple-element.22), channel_id=1, source_target_pairs={{0,0},{1,8},{2,16},{3,24},{4,4},{5,12},{6,20},{7,28},{8,1},{9,9},{... | collective-permute-start | bytes 208904 | tf_op jit(solution)/shard_map/ppermute | solution.py:429
  34.6 9.2 %copy-start.13 = (bf16[1,128,1024]{2,1,0:T(8,128)(2,1)S(1)}, bf16[1,128,1024]{2,1,0:T(8,128)(2,1)}, u32[]{:S(2)}) copy-start(bf16[1,128,1024]{2,1,0:T(8,128)(2,1)} %get-tuple-element.25) | copy-start | bytes 786436
  34.6 10.7 %copy-start.12 = (bf16[1,128,1024]{2,1,0:T(8,128)(2,1)S(1)}, bf16[1,128,1024]{2,1,0:T(8,128)(2,1)}, u32[]{:S(2)}) copy-start(bf16[1,128,1024]{2,1,0:T(8,128)(2,1)} %get-tuple-element.26) | copy-start | bytes 786436
  34.6 66.5 %copy-start.10 = (s32[16]{0:T(128)S(1)}, s32[16]{0:T(128)}, u32[]{:S(2)}) copy-start(s32[16]{0:T(128)} %copy-done.9) | copy-start | bytes 196
  34.6 41.7 %collective-permute-start.12 = (bf16[1,128,1024]{2,1,0:T(8,128)(2,1)}, bf16[1,128,1024]{2,1,0:T(8,128)(2,1)S(1)}, u32[]{:S(2)}, u32[]{:S(2)}) collective-permute-start(bf16[1,128,1024]{2,1,0:T(8,128)(2,1)} %get-tuple-element.35), channel_id=1, source_target_pairs={{0,2},{1,3},{2,0},{3,1},{4,6},{5,7},{6,4},{7,5},{8,10},{9,11},{10,... | collective-permute-start | bytes 786440 | tf_op jit(solution)/shard_map/ppermute | solution.py:407
  40.8 35.5 %collective-permute-start.8 = (bf16[1,128,1024]{2,1,0:T(8,128)(2,1)}, bf16[1,128,1024]{2,1,0:T(8,128)(2,1)S(1)}, u32[]{:S(2)}, u32[]{:S(2)}) collective-permute-start(bf16[1,128,1024]{2,1,0:T(8,128)(2,1)} %get-tuple-element.31), channel_id=1, source_target_pairs={{0,3},{1,2},{2,1},{3,0},{4,7},{5,6},{6,5},{7,4},{8,11},{9,10},{10,... | collective-permute-start | bytes 786440 | tf_op jit(solution)/shard_map/ppermute | solution.py:407
  42.4 65.0 %copy-start.2 = (bf16[1,128,1024]{2,1,0:T(8,128)(2,1)}, bf16[1,128,1024]{2,1,0:T(8,128)(2,1)S(1)}, u32[]{:S(2)}) copy-start(bf16[1,128,1024]{2,1,0:T(8,128)(2,1)S(1)} %collective-permute-done.10.refs_3_) | copy-start | bytes 786436
  42.4 45.5 %collective-permute-start.9 = (bf16[1,128,1024]{2,1,0:T(8,128)(2,1)}, bf16[1,128,1024]{2,1,0:T(8,128)(2,1)S(1)}, u32[]{:S(2)}, u32[]{:S(2)}) collective-permute-start(bf16[1,128,1024]{2,1,0:T(8,128)(2,1)} %get-tuple-element.32), channel_id=1, source_target_pairs={{0,2},{1,3},{2,0},{3,1},{4,6},{5,7},{6,4},{7,5},{8,10},{9,11},{10,... | collective-permute-start | bytes 786440 | tf_op jit(solution)/shard_map/ppermute | solution.py:407
  43.8 63.6 %copy-start.3 = (bf16[1,128,1024]{2,1,0:T(8,128)(2,1)}, bf16[1,128,1024]{2,1,0:T(8,128)(2,1)S(1)}, u32[]{:S(2)}) copy-start(bf16[1,128,1024]{2,1,0:T(8,128)(2,1)S(1)} %collective-permute-done.11.refs_4_) | copy-start | bytes 786436
  43.8 44.1 %collective-permute-start.3 = (bf16[1,128,1024]{2,1,0:T(8,128)(2,1)S(1)}, bf16[1,128,1024]{2,1,0:T(8,128)(2,1)S(1)}, u32[]{:S(2)}, u32[]{:S(2)}) collective-permute-start(bf16[1,128,1024]{2,1,0:T(8,128)(2,1)S(1)} %copy-done.13), channel_id=1, source_target_pairs={{0,1},{1,0},{2,3},{3,2},{4,5},{5,4},{6,7},{7,6},{8,9},{9,8},{10,11... | collective-permute-start | bytes 786440 | tf_op jit(solution)/shard_map/ppermute | solution.py:407
  45.4 43.4 %collective-permute-start.4 = (bf16[1,128,1024]{2,1,0:T(8,128)(2,1)S(1)}, bf16[1,128,1024]{2,1,0:T(8,128)(2,1)S(1)}, u32[]{:S(2)}, u32[]{:S(2)}) collective-permute-start(bf16[1,128,1024]{2,1,0:T(8,128)(2,1)S(1)} %copy-done.12), channel_id=1, source_target_pairs={{0,3},{1,2},{2,1},{3,0},{4,7},{5,6},{6,5},{7,4},{8,11},{9,10},{10,... | collective-permute-start | bytes 786440 | tf_op jit(solution)/shard_map/ppermute | solution.py:407
  47.7 55.6 %all-to-all-start.1 = ((f32[8,136,128]{2,1,0:T(8,128)}), f32[8,136,128]{2,1,0:T(8,128)S(1)}, u32[]{:S(2)}, u32[]{:S(2)}) async-start(f32[8,136,128]{2,1,0:T(8,128)} %broadcast_in_dim.22), calls=%async_computation.1 | async-start | bytes 1114112 | tf_op jit(solution)/shard_map/all_to_all | solution.py:431
  76.3 31.0 %copy-start.4 = (bf16[1,128,1024]{2,1,0:T(8,128)(2,1)}, bf16[1,128,1024]{2,1,0:T(8,128)(2,1)S(1)}, u32[]{:S(2)}) copy-start(bf16[1,128,1024]{2,1,0:T(8,128)(2,1)S(1)} %collective-permute-done.12.refs_5_) | copy-start | bytes 786436
  76.3 36.3 %collective-permute-start.5 = (bf16[1,128,1024]{2,1,0:T(8,128)(2,1)}, bf16[1,128,1024]{2,1,0:T(8,128)(2,1)}, u32[]{:S(2)}, u32[]{:S(2)}) collective-permute-start(bf16[1,128,1024]{2,1,0:T(8,128)(2,1)} %get-tuple-element.27), channel_id=1, source_target_pairs={{0,2},{1,3},{2,0},{3,1},{4,6},{5,7},{6,4},{7,5},{8,10},{9,11},{10,... | collective-permute-start | bytes 786440 | tf_op jit(solution)/shard_map/ppermute | solution.py:407
  76.4 31.0 %copy-start.5 = (bf16[1,128,1024]{2,1,0:T(8,128)(2,1)}, bf16[1,128,1024]{2,1,0:T(8,128)(2,1)S(1)}, u32[]{:S(2)}) copy-start(bf16[1,128,1024]{2,1,0:T(8,128)(2,1)S(1)} %collective-permute-done.8.refs_1_) | copy-start | bytes 786436
  76.4 36.3 %collective-permute-start.6 = (bf16[1,128,1024]{2,1,0:T(8,128)(2,1)}, bf16[1,128,1024]{2,1,0:T(8,128)(2,1)}, u32[]{:S(2)}, u32[]{:S(2)}) collective-permute-start(bf16[1,128,1024]{2,1,0:T(8,128)(2,1)} %get-tuple-element.28), channel_id=1, source_target_pairs={{0,1},{1,0},{2,3},{3,2},{4,5},{5,4},{6,7},{7,6},{8,9},{9,8},{10,11... | collective-permute-start | bytes 786440 | tf_op jit(solution)/shard_map/ppermute | solution.py:407
  87.9 19.5 %copy-start.8 = (bf16[1,128,1024]{2,1,0:T(8,128)(2,1)}, bf16[1,128,1024]{2,1,0:T(8,128)(2,1)S(1)}, u32[]{:S(2)}) copy-start(bf16[1,128,1024]{2,1,0:T(8,128)(2,1)S(1)} %collective-permute-done.9.refs_2_) | copy-start | bytes 786436
  87.9 24.8 %collective-permute-start.7 = (bf16[1,128,1024]{2,1,0:T(8,128)(2,1)}, bf16[1,128,1024]{2,1,0:T(8,128)(2,1)}, u32[]{:S(2)}, u32[]{:S(2)}) collective-permute-start(bf16[1,128,1024]{2,1,0:T(8,128)(2,1)} %get-tuple-element.29), channel_id=1, source_target_pairs={{0,1},{1,0},{2,3},{3,2},{4,5},{5,4},{6,7},{7,6},{8,9},{9,8},{10,11... | collective-permute-start | bytes 786440 | tf_op jit(solution)/shard_map/ppermute | solution.py:407
  87.9 19.5 %copy-start.6 = (bf16[1,128,1024]{2,1,0:T(8,128)(2,1)}, bf16[1,128,1024]{2,1,0:T(8,128)(2,1)S(1)}, u32[]{:S(2)}) copy-start(bf16[1,128,1024]{2,1,0:T(8,128)(2,1)S(1)} %collective-permute-done.3.refs_0_) | copy-start | bytes 786436
  87.9 28.7 %collective-permute-start.2 = (bf16[1,128,1024]{2,1,0:T(8,128)(2,1)}, bf16[1,128,1024]{2,1,0:T(8,128)(2,1)}, u32[]{:S(2)}, u32[]{:S(2)}) collective-permute-start(bf16[1,128,1024]{2,1,0:T(8,128)(2,1)} %get-tuple-element.24), channel_id=1, source_target_pairs={{0,3},{1,2},{2,1},{3,0},{4,7},{5,6},{6,5},{7,4},{8,11},{9,10},{10,... | collective-permute-start | bytes 786440 | tf_op jit(solution)/shard_map/ppermute | solution.py:407
  88.7 18.7 %copy-start.7 = (bf16[1,128,1024]{2,1,0:T(8,128)(2,1)}, bf16[1,128,1024]{2,1,0:T(8,128)(2,1)S(1)}, u32[]{:S(2)}) copy-start(bf16[1,128,1024]{2,1,0:T(8,128)(2,1)S(1)} %collective-permute-done.4.refs_1_) | copy-start | bytes 786436
  88.7 31.0 %collective-permute-start.1 = (bf16[1,128,1024]{2,1,0:T(8,128)(2,1)}, bf16[1,128,1024]{2,1,0:T(8,128)(2,1)}, u32[]{:S(2)}, u32[]{:S(2)}) collective-permute-start(bf16[1,128,1024]{2,1,0:T(8,128)(2,1)} %get-tuple-element.23), channel_id=1, source_target_pairs={{0,2},{1,3},{2,0},{3,1},{4,6},{5,7},{6,4},{7,5},{8,10},{9,11},{10,... | collective-permute-start | bytes 786440 | tf_op jit(solution)/shard_map/ppermute | solution.py:407
  103.3 0.8 copy-start.1

commit v3 on v2

--- a/solution.py
+++ b/solution.py
@@ -24,6 +24,14 @@
 HBM = pl.BlockSpec(memory_space=pltpu.HBM)
 SMEM = pl.BlockSpec(memory_space=pltpu.SMEM)
 VMEM = pl.BlockSpec(memory_space=pltpu.VMEM)
+
+
+def params(room):
+    return pltpu.CompilerParams(vmem_limit_bytes=max(room, 1 << 21))
+
+
+def params_beside(array):
+    return params(VMEM_BYTES - array.size * array.dtype.itemsize * 3 // 4)
 
 
 def nesterov_of(grads, momentum):
@@ -62,7 +70,7 @@
 def first_kernel(wanted, pieces, codes_ref, g_ref, m_ref, *refs):
     count = len(wanted)
     outs = refs[:count]
-    g_buf, m_buf, y_buf, g_sem, m_sem, y_sem = refs[count:]
+    g_buf, m_buf, g_sem, m_sem = refs[count:]
     rows = g_buf.shape[2]
     group = codes_ref.shape[1] // lax.axis_size("tp")
     row = lax.axis_index("tp")
@@ -73,9 +81,6 @@
             pltpu.make_async_copy(g_ref.at[source, part], g_buf.at[i, p], g_sem.at[i, p]),
             pltpu.make_async_copy(m_ref.at[source, part], m_buf.at[i, p], m_sem.at[i, p]),
         )
-
-    def out_copy(i, p):
-        return pltpu.make_async_copy(y_buf.at[i, p], outs[i].at[0, pl.ds(p * rows, rows)], y_sem.at[i, p])
 
     reads = []
     for i, (place_of, c) in enumerate(wanted):
@@ -91,10 +96,7 @@
         for copy in copies:
             copy.wait()
         _, y = nesterov_of(g_buf[i, p], m_buf[i, p])
-        y_buf[i, p] = y
-        out_copy(i, p).start()
-    for i, p, _ in reads:
-        out_copy(i, p).wait()
+        outs[i][0, p * rows : (p + 1) * rows] = y
 
 
 def first_blocks(codes, grads, momentum, wanted, pieces=4):
@@ -105,8 +107,9 @@
         functools.partial(first_kernel, wanted, pieces),
         out_shape=[jax.ShapeDtypeStruct((1, head, width), jnp.bfloat16)] * count,
         in_specs=[SMEM, HBM, HBM],
-        out_specs=[HBM] * count,
-        scratch_shapes=[buffer] * 3 + [pltpu.SemaphoreType.DMA((count, pieces))] * 3,
+        out_specs=[VMEM] * count,
+        scratch_shapes=[buffer] * 2 + [pltpu.SemaphoreType.DMA((count, pieces))] * 2,
+        compiler_params=params_beside(grads),
         name="first_blocks",
     )(codes, grads, momentum)
 
@@ -185,6 +188,7 @@
         in_specs=[SMEM, SMEM, HBM, HBM],
         out_specs=[HBM, VMEM] + [HBM] * len(spans),
         scratch_shapes=[buffer] * 4 + [pltpu.SemaphoreType.DMA((blocks,))] * 4,
+        compiler_params=params_beside(grads),
         name="all_blocks",
     )(source, place, grads, momentum)
 
@@ -253,6 +257,7 @@
         in_specs=[SMEM, SMEM, VMEM],
         out_specs=[VMEM, VMEM],
         scratch_shapes=[pltpu.VMEM((2 * count, head), jnp.float32)],
+        compiler_params=params(4 * parts.size * 4),
         name="solve",
     )(owners, codes, parts)
 
@@ -278,6 +283,7 @@
         out_shape=jax.ShapeDtypeStruct((blocks, 2 * head, head), jnp.bfloat16),
         in_specs=[VMEM],
         out_specs=VMEM,
+        compiler_params=params(4 * packed.size * 4),
         name="unpack_all",
     )(packed)
 
@@ -285,33 +291,20 @@
 def apply_kernel(factor, counts, tiles, aliased, place, q_ref, *refs):
     chunks = refs[: len(counts)]
     out = refs[len(counts) + aliased]
-    q_buf, y_buf, u_buf, q_sem, y_sem, u_sem = refs[len(counts) + aliased + 1 :]
-    head = y_buf.shape[1]
-    width = y_buf.shape[2] // tiles
+    u_buf, u_sem = refs[len(counts) + aliased + 1 :]
+    head = u_buf.shape[1]
+    width = u_buf.shape[2] // tiles
     members = [(chunk, k) for chunk, count in zip(chunks, counts) for k in range(count)]
-
-    def q_copy(i):
-        return pltpu.make_async_copy(q_ref.at[place[i]], q_buf.at[i], q_sem.at[i])
-
-    def y_copy(i, j):
-        chunk, k = members[i]
-        part = pl.ds(j * width, width)
-        return pltpu.make_async_copy(chunk.at[k, :, part], y_buf.at[i, :, part], y_sem.at[i, j])
 
     def u_copy(i, j):
         part = pl.ds(j * width, width)
         return pltpu.make_async_copy(u_buf.at[i, :, part], out.at[place[i], :, part], u_sem.at[i, j])
 
-    for i in range(len(members)):
-        q_copy(i).start()
+    for i, (chunk, k) in enumerate(members):
+        q = q_ref[place[i]]
         for j in range(tiles):
-            y_copy(i, j).start()
-    for i in range(len(members)):
-        q_copy(i).wait()
-        for j in range(tiles):
-            y_copy(i, j).wait()
             part = pl.ds(j * width, width)
-            ortho = jnp.dot(q_buf[i], y_buf[i, :, part], preferred_element_type=jnp.float32)
+            ortho = jnp.dot(q, chunk[k, :, part], preferred_element_type=jnp.float32)
             ortho = ortho[:head] + ortho[head:]
             ortho = ortho.astype(jnp.bfloat16).astype(jnp.float32)
             u_buf[i, :, part] = (-factor * ortho).astype(jnp.bfloat16)
@@ -326,30 +319,24 @@
     blocks = transforms.shape[0]
     counts = [chunk.shape[0] for chunk in chunks]
     total = sum(counts)
-    in_specs = [SMEM] + [HBM] * (1 + len(chunks))
+    in_specs = [SMEM] + [VMEM] * (1 + len(chunks))
     operands = [place, transforms, *chunks]
     aliases = {}
     if into is not None:
         aliases = {len(operands): 0}
         in_specs.append(HBM)
         operands.append(into)
-    buffer = pltpu.VMEM((total, head, width), jnp.bfloat16)
-    copies = pltpu.SemaphoreType.DMA((total, tiles))
     return pl.pallas_call(
         functools.partial(apply_kernel, factor, counts, tiles, len(aliases)),
         out_shape=jax.ShapeDtypeStruct((blocks, head, width), jnp.bfloat16),
         in_specs=in_specs,
         out_specs=HBM,
         scratch_shapes=[
-            pltpu.VMEM((total, 2 * head, head), jnp.bfloat16),
-            buffer,
-            buffer,
-            pltpu.SemaphoreType.DMA((total,)),
-            copies,
-            copies,
+            pltpu.VMEM((total, head, width), jnp.bfloat16),
+            pltpu.SemaphoreType.DMA((total, tiles)),
         ],
         input_output_aliases=aliases,
-        compiler_params=pltpu.CompilerParams(vmem_limit_bytes=VMEM_BYTES),
+        compiler_params=params(4 * total * head * width * 2),
         name="apply_blocks",
     )(*operands)
 

time: 123 us -> 120 us (0.976)
  waiting for transfers between devices: 22.5 us -> 30.3 us
  Pallas kernels: 35.4 us -> 27.7 us
  local copies, waits for them, and re-layouts: 4.57 us -> 1.75 us
    ppermute x12, waiting for transfers between devices: 16.8 us -> 24 us  [send(): lax.ppermute(array, 'tp', [(t, partner(t, chunk[0])) for t in range(n_tp)])]
    pallas_call x4, Pallas kernels: 15.3 us -> 10.5 us  [apply_blocks(): pl.pallas_call(functools.partial(apply_kernel, factor, counts, tiles, len...]
    unnamed x29 -> x11, local copies, waits for them, and re-layouts: 2.34 us -> 0.1 us
    pallas_call x1, Pallas kernels: 3.31 us -> 1.29 us  [unpack_all(): pl.pallas_call(functools.partial(unpack_kernel, spread), out_shape=jax.Sh...]
  transfers between devices with their start and end apart: 15 -> 15, of which waited for: 3 -> 5; matrix products, arithmetic and copies ran while one was open for 3% -> 2% of each run, Pallas kernels for 18% -> 13%
where the time goes in v3:
time: 120 us; the launch traced here: 119 us
  starting transfers between devices  56.5 us (47%)
  waiting for transfers between devices  30.3 us (25%)
  Pallas kernels  27.7 us (23%)
  other arithmetic  2.11 us (2%)
  local copies, waits for them, and re-layouts  1.75 us (1%)
    ppermute x12, starting transfers between devices, send(): lax.ppermute(array, 'tp', [(t, partner(t, chunk[0])) for t in range(n_tp)])  34 us
    ppermute x12, waiting for transfers between devices, send(): lax.ppermute(array, 'tp', [(t, partner(t, chunk[0])) for t in range(n_tp)])  24 us
    all_to_all x1, starting transfers between devices, local(): lax.all_to_all(packed, 'fsdp', split_axis=0, concat_axis=0, tiled=True)  16.7 us
    pallas_call x4, Pallas kernels, apply_blocks(): pl.pallas_call(functools.partial(apply_kernel, factor, counts, tiles, len...  10.5 us
    pallas_call x1, Pallas kernels, all_blocks(): pl.pallas_call(functools.partial(all_kernel, spans, spread, min(width, 25...  10 us
    all_to_all x1, waiting for transfers between devices, local(): lax.all_to_all(parts, 'fsdp', split_axis=0, concat_axis=0, tiled=True)  6.28 us
    all_to_all x1, starting transfers between devices, local(): lax.all_to_all(parts, 'fsdp', split_axis=0, concat_axis=0, tiled=True)  5.21 us
    pallas_call x1, Pallas kernels, solve(): pl.pallas_call(functools.partial(solve_kernel, spread, count, elements),...  2.92 us
  transfers between devices with their start and end apart: 15, of which 5 were waited for; matrix products, arithmetic and copies ran while one was open for 2% of the time, Pallas kernels for 13%

profile of v3, /device:TPU:0, one launch (start us, length us, event | category | flops | bytes accessed | tf_op | source)
XLA Modules:
  0.0 119.0 jit_solution(13620124485364491559)
XLA Ops:
  0.6 0.7 multiply_add_fusion.place
  1.3 1.3 %select_reduce_fusion.source = s32[16]{0:T(128)} fusion(s32[16]{0:T(128)} %bitcast.2, s32[16]{0:T(128)S(1)} %multiply_add_fusion.place), kind=kLoop, calls=%fused_computation | loop fusion | flops 752 | bytes 192 | tf_op jit(solution)/shard_map/reduce_sum | solution.py:384
  2.7 0.0 copy-done.2
  2.7 10.0 %all_blocks.1 = (bf16[16,128,1024]{2,1,0:T(8,128)(2,1)}, f32[8,144,128]{2,1,0:T(8,128)}, bf16[1,128,1024]{2,1,0:T(8,128)(2,1)}, bf16[1,128,1024]{2,1,0:T(8,128)(...) custom-call(s32[16]{0:T(128)} %select_reduce_fusion.source, ...), custom_call_target="tpu_custom_call" | custom-call | tf_op jit(solution)/shard_map/all_blocks/pallas_call | solution.py:181
  12.7 5.2 %all-to-all-start = ((f32[8,144,128]{2,1,0:T(8,128)}), f32[8,144,128]{2,1,0:T(8,128)S(1)}, u32[]{:S(2)}, u32[]{:S(2)}) async-start(f32[8,144,128]{2,1,0:T(8,128)} %get-tuple-element.21), calls=%async_computation | async-start | bytes 1179648 | tf_op jit(solution)/shard_map/all_to_all | solution.py:407
  17.9 1.6 %collective-permute-start.10 = (bf16[1,128,1024]{2,1,0:T(8,128)(2,1)}, bf16[1,128,1024]{2,1,0:T(8,128)(2,1)S(1)}, u32[]{:S(2)}, u32[]{:S(2)}) collective-permute-start(bf16[1,128,1024]{2,1,0:T(8,128)(2,1)} %get-tuple-element.33), channel_id=1, source_target_pairs={{0,1},{1,0},{2,3},{3,2},{4,5},{5,4},{6,7},{7,6},{8,9},{9,8},{10,11... | collective-permute-start | bytes 786440 | tf_op jit(solution)/shard_map/ppermute | solution.py:394
  19.5 2.5 %collective-permute-start.11 = (bf16[1,128,1024]{2,1,0:T(8,128)(2,1)}, bf16[1,128,1024]{2,1,0:T(8,128)(2,1)S(1)}, u32[]{:S(2)}, u32[]{:S(2)}) collective-permute-start(bf16[1,128,1024]{2,1,0:T(8,128)(2,1)} %get-tuple-element.34), channel_id=1, source_target_pairs={{0,3},{1,2},{2,1},{3,0},{4,7},{5,6},{6,5},{7,4},{8,11},{9,10},{10,... | collective-permute-start | bytes 786440 | tf_op jit(solution)/shard_map/ppermute | solution.py:394
  22.0 0.1 copy.13.owners
  22.1 6.3 %all-to-all-done.parts_ref = f32[8,144,128]{2,1,0:T(8,128)S(1)} async-done(((f32[8,144,128]{2,1,0:T(8,128)}), f32[8,144,128]{2,1,0:T(8,128)S(1)}, u32[]{:S(2)}, u32[]{:S(2)}) %all-to-all-start) | async-done | bytes 589856 | tf_op jit(solution)/shard_map/all_to_all | solution.py:407
  28.4 2.9 %solve.1 = (f32[136,128]{1,0:T(8,128)S(1)}, f32[1,128]{1,0:T(1,128)}) custom-call(s32[16,1]{1,0:T(8,128)S(1)} %copy.13.owners, s32[1,16]{1,0:T(1,128)S(1)} %copy-done.1, f32[8,144,128]{2,1,0:T(8,128)S(1)} %all-to-all-done.parts_ref), custom_call_target="tpu_custom_call" | custom-call | tf_op jit(solution)/shard_map/solve/pallas_call | solution.py:251
  31.3 0.7 collective-permute-start
  32.0 0.0 copy-start
  32.0 4.2 %collective-permute-start.12 = (bf16[1,128,1024]{2,1,0:T(8,128)(2,1)}, bf16[1,128,1024]{2,1,0:T(8,128)(2,1)S(1)}, u32[]{:S(2)}, u32[]{:S(2)}) collective-permute-start(bf16[1,128,1024]{2,1,0:T(8,128)(2,1)} %get-tuple-element.35), channel_id=1, source_target_pairs={{0,2},{1,3},{2,0},{3,1},{4,6},{5,7},{6,4},{7,5},{8,10},{9,11},{10,... | collective-permute-start | bytes 786440 | tf_op jit(solution)/shard_map/ppermute | solution.py:394
  36.2 2.9 %first_blocks.1 = (bf16[1,128,1024]{2,1,0:T(8,128)(2,1)}, bf16[1,128,1024]{2,1,0:T(8,128)(2,1)}) custom-call(s32[1,16]{1,0:T(1,128)} %codes_ref.1, bf16[16,128,1024]{2,1,0:T(8,128)(2,1)} %g_ref.3, bf16[16,128,1024]{2,1,0:T(8,128)(2,1)} %m_ref.3), custom_call_target="tpu_custom_call" | custom-call | tf_op jit(solution)/shard_map/first_blocks/pallas_call | solution.py:106
  39.1 1.5 %collective-permute-start.8 = (bf16[1,128,1024]{2,1,0:T(8,128)(2,1)}, bf16[1,128,1024]{2,1,0:T(8,128)(2,1)S(1)}, u32[]{:S(2)}, u32[]{:S(2)}) collective-permute-start(bf16[1,128,1024]{2,1,0:T(8,128)(2,1)} %get-tuple-element.31), channel_id=1, source_target_pairs={{0,3},{1,2},{2,1},{3,0},{4,7},{5,6},{6,5},{7,4},{8,11},{9,10},{10,... | collective-permute-start | bytes 786440 | tf_op jit(solution)/shard_map/ppermute | solution.py:394
  40.6 0.0 collective-permute-done.10.refs_3_
  40.6 1.5 %collective-permute-start.9 = (bf16[1,128,1024]{2,1,0:T(8,128)(2,1)}, bf16[1,128,1024]{2,1,0:T(8,128)(2,1)S(1)}, u32[]{:S(2)}, u32[]{:S(2)}) collective-permute-start(bf16[1,128,1024]{2,1,0:T(8,128)(2,1)} %get-tuple-element.32), channel_id=1, source_target_pairs={{0,2},{1,3},{2,0},{3,1},{4,6},{5,7},{6,4},{7,5},{8,10},{9,11},{10,... | collective-permute-start | bytes 786440 | tf_op jit(solution)/shard_map/ppermute | solution.py:394
  42.1 0.0 collective-permute-done.11.refs_4_
  42.1 1.5 %collective-permute-start.3 = (bf16[1,128,1024]{2,1,0:T(8,128)(2,1)}, bf16[1,128,1024]{2,1,0:T(8,128)(2,1)S(1)}, u32[]{:S(2)}, u32[]{:S(2)}) collective-permute-start(bf16[1,128,1024]{2,1,0:T(8,128)(2,1)} %get-tuple-element.25), channel_id=1, source_target_pairs={{0,1},{1,0},{2,3},{3,2},{4,5},{5,4},{6,7},{7,6},{8,9},{9,8},{10,11... | collective-permute-start | bytes 786440 | tf_op jit(solution)/shard_map/ppermute | solution.py:394
  43.5 0.0 collective-permute-done
  43.6 1.5 %collective-permute-start.4 = (bf16[1,128,1024]{2,1,0:T(8,128)(2,1)}, bf16[1,128,1024]{2,1,0:T(8,128)(2,1)S(1)}, u32[]{:S(2)}, u32[]{:S(2)}) collective-permute-start(bf16[1,128,1024]{2,1,0:T(8,128)(2,1)} %get-tuple-element.26), channel_id=1, source_target_pairs={{0,3},{1,2},{2,1},{3,0},{4,7},{5,6},{6,5},{7,4},{8,11},{9,10},{10,... | collective-permute-start | bytes 786440 | tf_op jit(solution)/shard_map/ppermute | solution.py:394
  45.0 0.9 broadcast_in_dim.22
  45.9 16.7 %all-to-all-start.1 = ((f32[8,136,128]{2,1,0:T(8,128)}), f32[8,136,128]{2,1,0:T(8,128)S(1)}, u32[]{:S(2)}, u32[]{:S(2)}) async-start(f32[8,136,128]{2,1,0:T(8,128)} %broadcast_in_dim.22), calls=%async_computation.1 | async-start | bytes 1114112 | tf_op jit(solution)/shard_map/all_to_all | solution.py:418
  62.5 11.8 %collective-permute-done.12.refs_5_ = bf16[1,128,1024]{2,1,0:T(8,128)(2,1)S(1)} collective-permute-done((bf16[1,128,1024]{2,1,0:T(8,128)(2,1)}, bf16[1,128,1024]{2,1,0:T(8,128)(2,1)S(1)}, u32[]{:S(2)}, u32[]{:S(2)}) %collective-permute-start.12) | collective-permute-done | bytes 262176 | tf_op jit(solution)/shard_map/ppermute | solution.py:394
  74.3 0.0 collective-permute-start.5
  74.3 0.0 collective-permute-done.8.refs_1_
  74.3 6.2 %collective-permute-start.6 = (bf16[1,128,1024]{2,1,0:T(8,128)(2,1)}, bf16[1,128,1024]{2,1,0:T(8,128)(2,1)}, u32[]{:S(2)}, u32[]{:S(2)}) collective-permute-start(bf16[1,128,1024]{2,1,0:T(8,128)(2,1)} %get-tuple-element.28), channel_id=1, source_target_pairs={{0,1},{1,0},{2,3},{3,2},{4,5},{5,4},{6,7},{7,6},{8,9},{9,8},{10,11... | collective-permute-start | bytes 786440 | tf_op jit(solution)/shard_map/ppermute | solution.py:394
  80.5 5.2 %collective-permute-done.9.refs_2_ = bf16[1,128,1024]{2,1,0:T(8,128)(2,1)S(1)} collective-permute-done((bf16[1,128,1024]{2,1,0:T(8,128)(2,1)}, bf16[1,128,1024]{2,1,0:T(8,128)(2,1)S(1)}, u32[]{:S(2)}, u32[]{:S(2)}) %collective-permute-start.9) | collective-permute-done | bytes 262176 | tf_op jit(solution)/shard_map/ppermute | solution.py:394
  85.6 0.0 collective-permute-start.7
  85.6 0.0 collective-permute-done.3.refs_0_
  85.6 1.0 collective-permute-start.2
  86.7 0.0 collective-permute-done.4.refs_1_
  86.7 12.6 %collective-permute-start.1 = (bf16[1,128,1024]{2,1,0:T(8,128)(2,1)}, bf16[1,128,1024]{2,1,0:T(8,128)(2,1)}, u32[]{:S(2)}, u32[]{:S(2)}) collective-permute-start(bf16[1,128,1024]{2,1,0:T(8,128)(2,1)} %get-tuple-element.23), channel_id=1, source_target_pairs={{0,2},{1,3},{2,0},{3,1},{4,6},{5,7},{6,4},{7,5},{8,10},{9,11},{10,... | collective-permute-start | bytes 786440 | tf_op jit(solution)/shard_map/ppermute | solution.py:394
  99.2 0.1 fusion
  99.3 0.1 slice.31
  99.4 0.1 pad_add_fusion.place
  99.5 0.6 fusion.1
  100.1 0.0 all-to-all-done.1.packed_ref
  100.1 1.3 %unpack_all.1.q_ref = bf16[16,256,128]{2,1,0:T(8,128)(2,1)S(1)} custom-call(f32[8,136,128]{2,1,0:T(8,128)S(1)} %all-to-all-done.1.packed_ref), custom_call_target="tpu_custom_call" | custom-call | tf_op jit(solution)/shard_map/unpack_all/pallas_call | solution.py:281
  101.4 2.7 %apply_blocks.4.refs_5_ = bf16[16,128,1024]{2,1,0:T(8,128)(2,1)} custom-call(s32[9]{0:T(128)S(1)} %pad_add_fusion.place, bf16[16,256,128]{2,1,0:T(8,128)(2,1)S(1)} %unpack_all.1.q_ref, bf16[4,128,1024]{2,1,0:T(8,128)(2,1)S(1)} %copy-done, bf16[1,128,1024]{2,1,0:T(8,128)(2,1)S(1)} %collective-permute-done.8.refs_1_, ...), custom_call_target="tpu_custom_call" | custom-call | tf_op jit(solution)/shard_map/apply_blocks/pallas_call | solution.py:329
  104.1 4.0 %collective-permute-done.5.refs_2_ = bf16[1,128,1024]{2,1,0:T(8,128)(2,1)} collective-permute-done((bf16[1,128,1024]{2,1,0:T(8,128)(2,1)}, bf16[1,128,1024]{2,1,0:T(8,128)(2,1)}, u32[]{:S(2)}, u32[]{:S(2)}) %collective-permute-start.5) | collective-permute-done | bytes 262176 | tf_op jit(solution)/shard_map/ppermute | solution.py:394
  108.1 0.0 collective-permute-done.6.refs_3_
  108.1 0.0 collective-permute-done.7.refs_4_
  108.1 2.7 %apply_blocks.5.refs_1_ = bf16[16,128,1024]{2,1,0:T(8,128)(2,1)} custom-call(s32[5]{0:T(128)S(1)} %get-tuple-element.38.place, bf16[16,256,128]{2,1,0:T(8,128)(2,1)S(1)} %unpack_all.1.q_ref, bf16[1,128,1024]{2,1,0:T(8,128)(2,1)S(1)} %collective-permute-done.3.refs_0_, ...), custom_call_target="tpu_custom_call", output_to_operand_aliasing={{}: (7, {})} | custom-call | tf_op jit(solution)/shard_map/apply_blocks/pallas_call | solution.py:329
  110.8 0.0 collective-permute-done.2.refs_0_
  110.8 2.6 %apply_blocks.6.refs_1_ = bf16[16,128,1024]{2,1,0:T(8,128)(2,1)} custom-call(s32[1]{0:T(128)} %get-tuple-element.39.place, bf16[16,256,128]{2,1,0:T(8,128)(2,1)S(1)} %unpack_all.1.q_ref, bf16[1,128,1024]{2,1,0:T(8,128)(2,1)} %collective-permute-done.2.refs_0_, bf16[16,128,1024]{2,1,0:T(8,128)(2,1)} %apply_blocks.5.refs_1_), custom_call_target="tpu_custom_call", output_to_operand_aliasing={{}: (3, {})} | custom-call | tf_op jit(solution)/shard_map/apply_blocks/pallas_call | solution.py:329
  113.4 3.1 %collective-permute-done.1.refs_0_ = bf16[1,128,1024]{2,1,0:T(8,128)(2,1)} collective-permute-done((bf16[1,128,1024]{2,1,0:T(8,128)(2,1)}, bf16[1,128,1024]{2,1,0:T(8,128)(2,1)}, u32[]{:S(2)}, u32[]{:S(2)}) %collective-permute-start.1) | collective-permute-done | bytes 262176 | tf_op jit(solution)/shard_map/ppermute | solution.py:394
  116.4 2.6 %apply_blocks.7 = bf16[16,128,1024]{2,1,0:T(8,128)(2,1)} custom-call(s32[1]{0:T(128)} %get-tuple-element.40.place, bf16[16,256,128]{2,1,0:T(8,128)(2,1)S(1)} %unpack_all.1.q_ref, bf16[1,128,1024]{2,1,0:T(8,128)(2,1)} %collective-permute-done.1.refs_0_, bf16[16,128,1024]{2,1,0:T(8,128)(2,1)} %apply_blocks.6.refs_1_), custom_call_target="tpu_custom_call", output_to_operand_aliasing={{}: (3, {})} | custom-call | tf_op jit(solution)/shard_map/apply_blocks/pallas_call | solution.py:329
  (8 shorter events, 0.0 us)
Async XLA Ops:
  1.3 1.4 %copy-start.2 = (s32[16]{0:T(128)}, s32[16]{0:T(128)S(1)}, u32[]{:S(2)}) copy-start(s32[16]{0:T(128)S(1)} %multiply_add_fusion.place) | copy-start | bytes 196
  2.7 19.3 %copy-start.4 = (s32[16,1]{0,1:T(1,128)S(1)}, s32[16,1]{0,1:T(1,128)}, u32[]{:S(2)}) copy-start(s32[16,1]{0,1:T(1,128)} %param.8) | copy-start | bytes 196
  2.7 25.7 %copy-start.1 = (s32[1,16]{1,0:T(1,128)S(1)}, s32[1,16]{1,0:T(1,128)}, u32[]{:S(2)}) copy-start(s32[1,16]{1,0:T(1,128)} %codes_ref.1) | copy-start | bytes 196
  12.7 15.6 %all-to-all-start = ((f32[8,144,128]{2,1,0:T(8,128)}), f32[8,144,128]{2,1,0:T(8,128)S(1)}, u32[]{:S(2)}, u32[]{:S(2)}) async-start(f32[8,144,128]{2,1,0:T(8,128)} %get-tuple-element.21), calls=%async_computation | async-start | bytes 1179648 | tf_op jit(solution)/shard_map/all_to_all | solution.py:407
  17.9 22.7 %collective-permute-start.10 = (bf16[1,128,1024]{2,1,0:T(8,128)(2,1)}, bf16[1,128,1024]{2,1,0:T(8,128)(2,1)S(1)}, u32[]{:S(2)}, u32[]{:S(2)}) collective-permute-start(bf16[1,128,1024]{2,1,0:T(8,128)(2,1)} %get-tuple-element.33), channel_id=1, source_target_pairs={{0,1},{1,0},{2,3},{3,2},{4,5},{5,4},{6,7},{7,6},{8,9},{9,8},{10,11... | collective-permute-start | bytes 786440 | tf_op jit(solution)/shard_map/ppermute | solution.py:394
  19.5 22.6 %collective-permute-start.11 = (bf16[1,128,1024]{2,1,0:T(8,128)(2,1)}, bf16[1,128,1024]{2,1,0:T(8,128)(2,1)S(1)}, u32[]{:S(2)}, u32[]{:S(2)}) collective-permute-start(bf16[1,128,1024]{2,1,0:T(8,128)(2,1)} %get-tuple-element.34), channel_id=1, source_target_pairs={{0,3},{1,2},{2,1},{3,0},{4,7},{5,6},{6,5},{7,4},{8,11},{9,10},{10,... | collective-permute-start | bytes 786440 | tf_op jit(solution)/shard_map/ppermute | solution.py:394
  31.3 12.3 %collective-permute-start = (f32[136,128]{1,0:T(8,128)S(1)}, f32[136,128]{1,0:T(8,128)S(1)}, u32[]{:S(2)}, u32[]{:S(2)}) collective-permute-start(f32[136,128]{1,0:T(8,128)S(1)} %get-tuple-element.22), channel_id=1, source_target_pairs={{0,0},{1,8},{2,16},{3,24},{4,4},{5,12},{6,20},{7,28},{8,1},{9,9},{... | collective-permute-start | bytes 208904 | tf_op jit(solution)/shard_map/ppermute | solution.py:416
  31.9 67.3 %copy-start.3 = (s32[16]{0:T(128)S(1)}, s32[16]{0:T(128)}, u32[]{:S(2)}) copy-start(s32[16]{0:T(128)} %copy-done.2) | copy-start | bytes 196
  32.0 69.4 %copy-start = (bf16[4,128,1024]{2,1,0:T(8,128)(2,1)S(1)}, bf16[4,128,1024]{2,1,0:T(8,128)(2,1)}, u32[]{:S(2)}) copy-start(bf16[4,128,1024]{2,1,0:T(8,128)(2,1)} %get-tuple-element.30.refs_0_) | copy-start | bytes 3145732
  32.0 42.3 %collective-permute-start.12 = (bf16[1,128,1024]{2,1,0:T(8,128)(2,1)}, bf16[1,128,1024]{2,1,0:T(8,128)(2,1)S(1)}, u32[]{:S(2)}, u32[]{:S(2)}) collective-permute-start(bf16[1,128,1024]{2,1,0:T(8,128)(2,1)} %get-tuple-element.35), channel_id=1, source_target_pairs={{0,2},{1,3},{2,0},{3,1},{4,6},{5,7},{6,4},{7,5},{8,10},{9,11},{10,... | collective-permute-start | bytes 786440 | tf_op jit(solution)/shard_map/ppermute | solution.py:394
  39.1 35.2 %collective-permute-start.8 = (bf16[1,128,1024]{2,1,0:T(8,128)(2,1)}, bf16[1,128,1024]{2,1,0:T(8,128)(2,1)S(1)}, u32[]{:S(2)}, u32[]{:S(2)}) collective-permute-start(bf16[1,128,1024]{2,1,0:T(8,128)(2,1)} %get-tuple-element.31), channel_id=1, source_target_pairs={{0,3},{1,2},{2,1},{3,0},{4,7},{5,6},{6,5},{7,4},{8,11},{9,10},{10,... | collective-permute-start | bytes 786440 | tf_op jit(solution)/shard_map/ppermute | solution.py:394
  40.6 45.0 %collective-permute-start.9 = (bf16[1,128,1024]{2,1,0:T(8,128)(2,1)}, bf16[1,128,1024]{2,1,0:T(8,128)(2,1)S(1)}, u32[]{:S(2)}, u32[]{:S(2)}) collective-permute-start(bf16[1,128,1024]{2,1,0:T(8,128)(2,1)} %get-tuple-element.32), channel_id=1, source_target_pairs={{0,2},{1,3},{2,0},{3,1},{4,6},{5,7},{6,4},{7,5},{8,10},{9,11},{10,... | collective-permute-start | bytes 786440 | tf_op jit(solution)/shard_map/ppermute | solution.py:394
  42.1 43.6 %collective-permute-start.3 = (bf16[1,128,1024]{2,1,0:T(8,128)(2,1)}, bf16[1,128,1024]{2,1,0:T(8,128)(2,1)S(1)}, u32[]{:S(2)}, u32[]{:S(2)}) collective-permute-start(bf16[1,128,1024]{2,1,0:T(8,128)(2,1)} %get-tuple-element.25), channel_id=1, source_target_pairs={{0,1},{1,0},{2,3},{3,2},{4,5},{5,4},{6,7},{7,6},{8,9},{9,8},{10,11... | collective-permute-start | bytes 786440 | tf_op jit(solution)/shard_map/ppermute | solution.py:394
  43.6 43.1 %collective-permute-start.4 = (bf16[1,128,1024]{2,1,0:T(8,128)(2,1)}, bf16[1,128,1024]{2,1,0:T(8,128)(2,1)S(1)}, u32[]{:S(2)}, u32[]{:S(2)}) collective-permute-start(bf16[1,128,1024]{2,1,0:T(8,128)(2,1)} %get-tuple-element.26), channel_id=1, source_target_pairs={{0,3},{1,2},{2,1},{3,0},{4,7},{5,6},{6,5},{7,4},{8,11},{9,10},{10,... | collective-permute-start | bytes 786440 | tf_op jit(solution)/shard_map/ppermute | solution.py:394
  45.9 54.2 %all-to-all-start.1 = ((f32[8,136,128]{2,1,0:T(8,128)}), f32[8,136,128]{2,1,0:T(8,128)S(1)}, u32[]{:S(2)}, u32[]{:S(2)}) async-start(f32[8,136,128]{2,1,0:T(8,128)} %broadcast_in_dim.22), calls=%async_computation.1 | async-start | bytes 1114112 | tf_op jit(solution)/shard_map/all_to_all | solution.py:418
  74.3 33.8 %collective-permute-start.5 = (bf16[1,128,1024]{2,1,0:T(8,128)(2,1)}, bf16[1,128,1024]{2,1,0:T(8,128)(2,1)}, u32[]{:S(2)}, u32[]{:S(2)}) collective-permute-start(bf16[1,128,1024]{2,1,0:T(8,128)(2,1)} %get-tuple-element.27), channel_id=1, source_target_pairs={{0,2},{1,3},{2,0},{3,1},{4,6},{5,7},{6,4},{7,5},{8,10},{9,11},{10,... | collective-permute-start | bytes 786440 | tf_op jit(solution)/shard_map/ppermute | solution.py:394
  74.3 33.8 %collective-permute-start.6 = (bf16[1,128,1024]{2,1,0:T(8,128)(2,1)}, bf16[1,128,1024]{2,1,0:T(8,128)(2,1)}, u32[]{:S(2)}, u32[]{:S(2)}) collective-permute-start(bf16[1,128,1024]{2,1,0:T(8,128)(2,1)} %get-tuple-element.28), channel_id=1, source_target_pairs={{0,1},{1,0},{2,3},{3,2},{4,5},{5,4},{6,7},{7,6},{8,9},{9,8},{10,11... | collective-permute-start | bytes 786440 | tf_op jit(solution)/shard_map/ppermute | solution.py:394
  85.6 22.5 %collective-permute-start.7 = (bf16[1,128,1024]{2,1,0:T(8,128)(2,1)}, bf16[1,128,1024]{2,1,0:T(8,128)(2,1)}, u32[]{:S(2)}, u32[]{:S(2)}) collective-permute-start(bf16[1,128,1024]{2,1,0:T(8,128)(2,1)} %get-tuple-element.29), channel_id=1, source_target_pairs={{0,1},{1,0},{2,3},{3,2},{4,5},{5,4},{6,7},{7,6},{8,9},{9,8},{10,11... | collective-permute-start | bytes 786440 | tf_op jit(solution)/shard_map/ppermute | solution.py:394
  85.6 25.2 %collective-permute-start.2 = (bf16[1,128,1024]{2,1,0:T(8,128)(2,1)}, bf16[1,128,1024]{2,1,0:T(8,128)(2,1)}, u32[]{:S(2)}, u32[]{:S(2)}) collective-permute-start(bf16[1,128,1024]{2,1,0:T(8,128)(2,1)} %get-tuple-element.24), channel_id=1, source_target_pairs={{0,3},{1,2},{2,1},{3,0},{4,7},{5,6},{6,5},{7,4},{8,11},{9,10},{10,... | collective-permute-start | bytes 786440 | tf_op jit(solution)/shard_map/ppermute | solution.py:394
  86.7 29.8 %collective-permute-start.1 = (bf16[1,128,1024]{2,1,0:T(8,128)(2,1)}, bf16[1,128,1024]{2,1,0:T(8,128)(2,1)}, u32[]{:S(2)}, u32[]{:S(2)}) collective-permute-start(bf16[1,128,1024]{2,1,0:T(8,128)(2,1)} %get-tuple-element.23), channel_id=1, source_target_pairs={{0,2},{1,3},{2,0},{3,1},{4,6},{5,7},{6,4},{7,5},{8,10},{9,11},{10,... | collective-permute-start | bytes 786440 | tf_op jit(solution)/shard_map/ppermute | solution.py:394

commit v4 on v3

--- a/solution.py
+++ b/solution.py
@@ -67,6 +67,22 @@
     return strict + strict.T + jnp.where(rows == columns, diagonal, 0.0)
 
 
+def row_of(user, n_tp):
+    rank = user % n_tp
+    return rank if n_tp % 2 else rank // 2 + rank % 2 * (n_tp // 2)
+
+
+def user_of(place, spread, per_row, n_tp):
+    unit = place // spread
+    row, k = unit // per_row, unit % per_row
+    rank = row if n_tp % 2 else row % (n_tp // 2) * 2 + row // (n_tp // 2)
+    return k * n_tp + rank
+
+
+def place_of(user, spread, per_row, n_tp):
+    return (row_of(user, n_tp) * per_row + user // n_tp) * spread
+
+
 def first_kernel(wanted, pieces, codes_ref, g_ref, m_ref, *refs):
     count = len(wanted)
     outs = refs[:count]
@@ -83,8 +99,8 @@
         )
 
     reads = []
-    for i, (place_of, c) in enumerate(wanted):
-        place = place_of(row) * group + c
+    for i, (partner, c) in enumerate(wanted):
+        place = partner(row) * group + c
         source = jnp.int32(0)
         for j in range(codes_ref.shape[1]):
             source = jnp.where(codes_ref[0, j] == place, j, source)
@@ -120,6 +136,8 @@
     blocks, head, width = g_buf.shape
     half = head // 2
     users = blocks // spread
+    n_tp = lax.axis_size("tp")
+    per_row = users // n_tp
 
     def in_copies(i):
         return (
@@ -158,7 +176,7 @@
             def _():
                 pltpu.make_async_copy(y_buf.at[i], out.at[i - start], y_sem.at[i]).start()
 
-        to = place[i] // spread
+        to = user_of(place[i], spread, per_row, n_tp)
         at = pl.multiple_of(place[i] % spread * half, half)
         parts_ref[to, pl.ds(at, half)] = pack(gram)
         diagonal = diagonal_of(gram)
@@ -197,6 +215,8 @@
     n_fsdp, _, head = parts_ref.shape
     half = head // 2
     here = lax.axis_index("fsdp")
+    n_tp = lax.axis_size("tp")
+    per_row = count // spread // n_tp
     total = parts_ref[0]
     for f in range(1, n_fsdp):
         total = total + parts_ref[f]
@@ -221,7 +241,7 @@
     identity = jnp.where(eye_rows == eye_columns, 1.0, 0.0)
     work = []
     for k in range(spread):
-        at = jnp.minimum(here * spread + k, count - 1)
+        at = jnp.minimum(place_of(here, spread, per_row, n_tp) + k, count - 1)
         diagonal = sum_ref[pl.ds(at, 1)]
         inverse = 1.0 / (jnp.sqrt(jnp.sum(diagonal, axis=1, keepdims=True)) + epsilon)
         gram = unpack(total[k * half : (k + 1) * half], diagonal) * (inverse * inverse)
@@ -288,23 +308,26 @@
     )(packed)
 
 
-def apply_kernel(factor, counts, tiles, aliased, place, q_ref, *refs):
-    chunks = refs[: len(counts)]
-    out = refs[len(counts) + aliased]
-    u_buf, u_sem = refs[len(counts) + aliased + 1 :]
+def apply_kernel(factor, members, at_end, tiles, q_ref, *refs):
+    out = refs[-3]
+    u_buf, u_sem = refs[-2:]
     head = u_buf.shape[1]
     width = u_buf.shape[2] // tiles
-    members = [(chunk, k) for chunk, count in zip(chunks, counts) for k in range(count)]
+    row = lax.axis_index("tp")
 
     def u_copy(i, j):
         part = pl.ds(j * width, width)
-        return pltpu.make_async_copy(u_buf.at[i, :, part], out.at[place[i], :, part], u_sem.at[i, j])
-
-    for i, (chunk, k) in enumerate(members):
-        q = q_ref[place[i]]
+        return pltpu.make_async_copy(u_buf.at[i, :, part], out.at[places[i], :, part], u_sem.at[i, j])
+
+    places = [place_at(row) for place_at, _, _ in members]
+    for i, (_, ways, k) in enumerate(members):
+        q = q_ref[places[i]]
         for j in range(tiles):
             part = pl.ds(j * width, width)
-            ortho = jnp.dot(q, chunk[k, :, part], preferred_element_type=jnp.float32)
+            y = refs[ways[0]][k, :, part]
+            if len(ways) > 1:
+                y = jnp.where(at_end(row), y, refs[ways[1]][k, :, part])
+            ortho = jnp.dot(q, y, preferred_element_type=jnp.float32)
             ortho = ortho[:head] + ortho[head:]
             ortho = ortho.astype(jnp.bfloat16).astype(jnp.float32)
             u_buf[i, :, part] = (-factor * ortho).astype(jnp.bfloat16)
@@ -314,20 +337,24 @@
             u_copy(i, j).wait()
 
 
-def apply_blocks(factor, place, transforms, chunks, into, tiles):
-    head, width = chunks[0].shape[1:]
+def apply_blocks(factor, transforms, chunks, into, at_end, tiles):
+    arrays, members = [], []
+    for ways, places in chunks:
+        at = range(len(arrays), len(arrays) + len(ways))
+        arrays += ways
+        members += [(place_at, at, k) for k, place_at in enumerate(places)]
+    head, width = arrays[0].shape[1:]
     blocks = transforms.shape[0]
-    counts = [chunk.shape[0] for chunk in chunks]
-    total = sum(counts)
-    in_specs = [SMEM] + [VMEM] * (1 + len(chunks))
-    operands = [place, transforms, *chunks]
+    total = len(members)
+    in_specs = [VMEM] * (1 + len(arrays))
+    operands = [transforms, *arrays]
     aliases = {}
     if into is not None:
         aliases = {len(operands): 0}
         in_specs.append(HBM)
         operands.append(into)
     return pl.pallas_call(
-        functools.partial(apply_kernel, factor, counts, tiles, len(aliases)),
+        functools.partial(apply_kernel, factor, members, at_end, tiles),
         out_shape=jax.ShapeDtypeStruct((blocks, head, width), jnp.bfloat16),
         in_specs=in_specs,
         out_specs=HBM,
@@ -380,7 +407,6 @@
     offsets = jnp.array([c for _, c in steps], jnp.int32)
     partners = jnp.array([x for x, _ in steps], jnp.int32)
     place_out = partner(row, partners) * group + offsets
-    place_in = sender(row, partners) * group + offsets
     source = jnp.sum(jnp.where(codes[None, :] == place_out[:, None], position[None, :], 0), axis=1)
 
     starts, total = {}, 0
@@ -388,30 +414,42 @@
         starts[chunk] = (total, len(chunk[1]))
         total += len(chunk[1])
 
+    def at_end(t):
+        return jnp.logical_or(t < n_tp // 4, t >= n_tp - n_tp // 4)
+
+    ends = [t for t in range(n_tp) if t < n_tp // 4 or t >= n_tp - n_tp // 4]
+    sends = [(chunk, None) for chunk in early + late if chunk not in last]
+    if ends:
+        sends += [(chunk, side) for side in (0, 1) for chunk in last]
+    else:
+        sends += [(chunk, None) for chunk in last]
     got = {}
 
-    def send(chunk, array):
-        got[chunk] = lax.ppermute(array, "tp", [(t, partner(t, chunk[0])) for t in range(n_tp)])
+    def send(chunk, side, array):
+        pairs = [(t, partner(t, chunk[0])) for t in range(n_tp)]
+        if side is not None:
+            pairs = [(t, to) for t, to in pairs if (to in ends) == (side == 0)]
+        got[chunk, side] = lax.ppermute(array, "tp", pairs)
 
     wanted = [(functools.partial(partner, x=x), cs[0]) for x, cs in first]
     for chunk, array in zip(first, first_blocks(pool_map, grads, momentum, wanted)):
-        send(chunk, array)
+        send(chunk, None, array)
     rest = chunks[len(first) :]
     new_momentum, parts, *ys = all_blocks(
         source, place_out, grads, momentum, [starts[chunk] for chunk in rest], spread, n_fsdp
     )
     ys = dict(zip(rest, ys))
-    for chunk in rest[: -len(own)]:
-        send(chunk, ys[chunk])
+    for chunk, side in sends[len(first) :]:
+        send(chunk, side, ys[chunk])
 
     parts = lax.all_to_all(parts, "fsdp", split_axis=0, concat_axis=0, tiled=True)
     packed, slots = solve(parts, owner_table, pool_map, spread, head * width * n_fsdp)
 
+    per_row = group // spread
     pairs = []
-    per_row = group // spread
     for f in range(blocks // spread):
         for t in range(n_tp):
-            to = (t * per_row + f % per_row) * n_tp + f // per_row
+            to = (t * per_row + f // n_tp) * n_tp + row_of(f, n_tp)
             pairs.append((f * n_tp + t, to))
     packed = lax.ppermute(packed, ("fsdp", "tp"), pairs)
     packed = jnp.broadcast_to(packed[None], (n_fsdp,) + packed.shape)
@@ -420,14 +458,18 @@
 
     factor = step_size * 0.2 * math.sqrt(width * n_fsdp)
     for chunk in own:
-        got[chunk] = ys[chunk]
+        got[chunk, None] = ys[chunk]
+
+    def arrival(chunk):
+        x, cs = chunk
+        ways = [got[chunk, side] for side in (0, 1, None) if (chunk, side) in got]
+        return ways, [functools.partial(lambda t, c: sender(t, x) * group + c, c=c) for c in cs]
+
     update = None
     between = [chunk for chunk in late if chunk not in last]
-    rounds = [own + early] + ([between] if between else []) + [[chunk] for chunk in last]
-    for members in rounds:
-        where = jnp.concatenate([place_in[s : s + n] for s, n in (starts[chunk] for chunk in members)])
-        tiles = 1 if len(members) > 1 or width < 512 else 4
-        update = apply_blocks(factor, where, transforms, [got[chunk] for chunk in members], update, tiles)
+    for members in [own + early] + ([between] if between else []) + [last]:
+        tiles = 1 if len(members) > 2 or width < 512 else 4
+        update = apply_blocks(factor, transforms, [arrival(m) for m in members], update, at_end, tiles)
     return (new_momentum, update, slots[:, :CAP])
 
 

time: 120 us -> 117 us (0.975)
  waiting for transfers between devices: 30.3 us -> 17.3 us
  starting transfers between devices: 56.5 us -> 67 us
  Pallas kernels: 27.7 us -> 23 us
  local copies, waits for them, and re-layouts: 1.75 us -> 5.87 us
    ppermute x12 -> x14, starting transfers between devices: 34 us -> 56.8 us  [send(): got[chunk, side] = lax.ppermute(array, 'tp', pairs)]
    all_to_all x1, starting transfers between devices: 16.7 us -> 4.26 us  [local(): lax.all_to_all(packed, 'fsdp', split_axis=0, concat_axis=0, tiled=True)]
    ppermute x12 -> x14, waiting for transfers between devices: 24 us -> 17 us  [send(): got[chunk, side] = lax.ppermute(array, 'tp', pairs)]
    all_to_all x1, waiting for transfers between devices: 6.28 us -> 0.29 us  [local(): lax.all_to_all(parts, 'fsdp', split_axis=0, concat_axis=0, tiled=True)]
    unnamed x11 -> x29, local copies, waits for them, and re-layouts: 0.1 us -> 5.03 us
    pallas_call x4 -> x3, Pallas kernels: 10.5 us -> 6.02 us  [apply_blocks(): pl.pallas_call(functools.partial(apply_kernel, factor, members, at_end, t...]
  transfers between devices with their start and end apart: 15 -> 17, of which waited for: 5 -> 4; matrix products, arithmetic and copies ran while one was open for 2% -> 1% of each run, Pallas kernels for 13% -> 10%
where the time goes in v4:
time: 117 us; the launch traced here: 116 us
  starting transfers between devices  67 us (57%)
  Pallas kernels  23 us (20%)
  waiting for transfers between devices  17.3 us (15%)
  local copies, waits for them, and re-layouts  5.87 us (5%)
  other arithmetic  2.03 us (2%)
    ppermute x14, starting transfers between devices, send(): got[chunk, side] = lax.ppermute(array, 'tp', pairs)  56.8 us
    ppermute x14, waiting for transfers between devices, send(): got[chunk, side] = lax.ppermute(array, 'tp', pairs)  17 us
    pallas_call x1, Pallas kernels, all_blocks(): pl.pallas_call(functools.partial(all_kernel, spans, spread, min(width, 25...  9.83 us
    pallas_call x3, Pallas kernels, apply_blocks(): pl.pallas_call(functools.partial(apply_kernel, factor, members, at_end, t...  6.02 us
    all_to_all x1, starting transfers between devices, local(): lax.all_to_all(parts, 'fsdp', split_axis=0, concat_axis=0, tiled=True)  5.21 us
    unnamed x29, local copies, waits for them, and re-layouts  5.03 us
    all_to_all x1, starting transfers between devices, local(): lax.all_to_all(packed, 'fsdp', split_axis=0, concat_axis=0, tiled=True)  4.26 us
    pallas_call x1, Pallas kernels, first_blocks(): pl.pallas_call(functools.partial(first_kernel, wanted, pieces), out_shape...  2.99 us
  transfers between devices with their start and end apart: 17, of which 4 were waited for; matrix products, arithmetic and copies ran while one was open for 1% of the time, Pallas kernels for 10%

profile of v4, /device:TPU:0, one launch (start us, length us, event | category | flops | bytes accessed | tf_op | source)
XLA Modules:
  0.0 116.1 jit_solution(132883248354532062)
XLA Ops:
  0.6 0.7 multiply_add_fusion.place
  1.3 1.3 %select_reduce_fusion.source = s32[16]{0:T(128)} fusion(s32[16]{0:T(128)} %bitcast.2, s32[16]{0:T(128)S(1)} %multiply_add_fusion.place), kind=kLoop, calls=%fused_computation | loop fusion | flops 752 | bytes 192 | tf_op jit(solution)/shard_map/reduce_sum | solution.py:410
  2.7 9.8 %all_blocks.1 = (bf16[16,128,1024]{2,1,0:T(8,128)(2,1)}, f32[8,144,128]{2,1,0:T(8,128)}, bf16[1,128,1024]{2,1,0:T(8,128)(2,1)}, bf16[1,128,1024]{2,1,0:T(8,128)(...) custom-call(s32[16]{0:T(128)} %select_reduce_fusion.source, ...), custom_call_target="tpu_custom_call" | custom-call | tf_op jit(solution)/shard_map/all_blocks/pallas_call | solution.py:199
  12.5 5.2 %all-to-all-start = ((f32[8,144,128]{2,1,0:T(8,128)}), f32[8,144,128]{2,1,0:T(8,128)S(1)}, u32[]{:S(2)}, u32[]{:S(2)}) async-start(f32[8,144,128]{2,1,0:T(8,128)} %get-tuple-element.21), calls=%async_computation | async-start | bytes 1179648 | tf_op jit(solution)/shard_map/all_to_all | solution.py:445
  17.7 1.6 %collective-permute-start.12 = (bf16[1,128,1024]{2,1,0:T(8,128)(2,1)}, bf16[1,128,1024]{2,1,0:T(8,128)(2,1)S(1)}, u32[]{:S(2)}, u32[]{:S(2)}) collective-permute-start(bf16[1,128,1024]{2,1,0:T(8,128)(2,1)} %get-tuple-element.33), channel_id=1, source_target_pairs={{0,1},{1,0},{2,3},{3,2},{4,5},{5,4},{6,7},{7,6},{8,9},{9,8},{10,11... | collective-permute-start | bytes 786440 | tf_op jit(solution)/shard_map/ppermute | solution.py:432
  19.3 2.5 %collective-permute-start.13 = (bf16[1,128,1024]{2,1,0:T(8,128)(2,1)}, bf16[1,128,1024]{2,1,0:T(8,128)(2,1)S(1)}, u32[]{:S(2)}, u32[]{:S(2)}) collective-permute-start(bf16[1,128,1024]{2,1,0:T(8,128)(2,1)} %get-tuple-element.34), channel_id=1, source_target_pairs={{0,3},{1,2},{2,1},{3,0},{4,7},{5,6},{6,5},{7,4},{8,11},{9,10},{10,... | collective-permute-start | bytes 786440 | tf_op jit(solution)/shard_map/ppermute | solution.py:432
  21.8 0.2 collective-permute-start.14
  22.0 3.0 %first_blocks.1 = (bf16[1,128,1024]{2,1,0:T(8,128)(2,1)}, bf16[1,128,1024]{2,1,0:T(8,128)(2,1)}) custom-call(s32[1,16]{1,0:T(1,128)} %codes_ref.1, bf16[16,128,1024]{2,1,0:T(8,128)(2,1)} %g_ref.3, bf16[16,128,1024]{2,1,0:T(8,128)(2,1)} %m_ref.3), custom_call_target="tpu_custom_call" | custom-call | tf_op jit(solution)/shard_map/first_blocks/pallas_call | solution.py:122
  25.0 2.8 %collective-permute-start.10 = (bf16[1,128,1024]{2,1,0:T(8,128)(2,1)}, bf16[1,128,1024]{2,1,0:T(8,128)(2,1)S(1)}, u32[]{:S(2)}, u32[]{:S(2)}) collective-permute-start(bf16[1,128,1024]{2,1,0:T(8,128)(2,1)} %get-tuple-element.31), channel_id=1, source_target_pairs={{0,3},{1,2},{2,1},{3,0},{4,7},{5,6},{6,5},{7,4},{8,11},{9,10},{10,... | collective-permute-start | bytes 786440 | tf_op jit(solution)/shard_map/ppermute | solution.py:432
  27.8 0.1 copy.12.owners
  27.8 0.3 all-to-all-done.parts_ref
  28.1 2.9 %solve.1 = (f32[136,128]{1,0:T(8,128)S(1)}, f32[1,128]{1,0:T(1,128)}) custom-call(s32[16,1]{1,0:T(8,128)S(1)} %copy.12.owners, s32[1,16]{1,0:T(1,128)S(1)} %copy-done.11, f32[8,144,128]{2,1,0:T(8,128)S(1)} %all-to-all-done.parts_ref), custom_call_target="tpu_custom_call" | custom-call | tf_op jit(solution)/shard_map/solve/pallas_call | solution.py:271
  31.1 0.7 collective-permute-start
  31.7 0.0 collective-permute-done.12.refs_3_
  31.7 5.4 %collective-permute-start.11 = (bf16[1,128,1024]{2,1,0:T(8,128)(2,1)}, bf16[1,128,1024]{2,1,0:T(8,128)(2,1)S(1)}, u32[]{:S(2)}, u32[]{:S(2)}) collective-permute-start(bf16[1,128,1024]{2,1,0:T(8,128)(2,1)} %get-tuple-element.32), channel_id=1, source_target_pairs={{0,2},{1,3},{2,0},{3,1},{4,6},{5,7},{6,4},{7,5},{8,10},{9,11},{10,... | collective-permute-start | bytes 786440 | tf_op jit(solution)/shard_map/ppermute | solution.py:432
  37.1 0.0 collective-permute-done.13.refs_4_
  37.1 15.5 %collective-permute-start.5 = (bf16[1,128,1024]{2,1,0:T(8,128)(2,1)}, bf16[1,128,1024]{2,1,0:T(8,128)(2,1)S(1)}, u32[]{:S(2)}, u32[]{:S(2)}) collective-permute-start(bf16[1,128,1024]{2,1,0:T(8,128)(2,1)} %get-tuple-element.25), channel_id=1, source_target_pairs={{0,1},{1,0},{2,3},{3,2},{4,5},{5,4},{6,7},{7,6},{8,9},{9,8},{10,11... | collective-permute-start | bytes 786440 | tf_op jit(solution)/shard_map/ppermute | solution.py:432
  52.7 5.5 %collective-permute-done.14.refs_5_ = bf16[1,128,1024]{2,1,0:T(8,128)(2,1)S(1)} collective-permute-done((bf16[1,128,1024]{2,1,0:T(8,128)(2,1)}, bf16[1,128,1024]{2,1,0:T(8,128)(2,1)S(1)}, u32[]{:S(2)}, u32[]{:S(2)}) %collective-permute-start.14) | collective-permute-done | bytes 262176 | tf_op jit(solution)/shard_map/ppermute | solution.py:432
  58.1 2.9 %collective-permute-start.6 = (bf16[1,128,1024]{2,1,0:T(8,128)(2,1)}, bf16[1,128,1024]{2,1,0:T(8,128)(2,1)S(1)}, u32[]{:S(2)}, u32[]{:S(2)}) collective-permute-start(bf16[1,128,1024]{2,1,0:T(8,128)(2,1)} %get-tuple-element.26), channel_id=1, source_target_pairs={{0,3},{1,2},{2,1},{3,0},{4,7},{5,6},{6,5},{7,4},{8,11},{9,10},{10,... | collective-permute-start | bytes 786440 | tf_op jit(solution)/shard_map/ppermute | solution.py:432
  61.0 0.0 collective-permute-done.10.refs_1_
  61.1 10.3 %collective-permute-start.7 = (bf16[1,128,1024]{2,1,0:T(8,128)(2,1)}, bf16[1,128,1024]{2,1,0:T(8,128)(2,1)}, u32[]{:S(2)}, u32[]{:S(2)}) collective-permute-start(bf16[1,128,1024]{2,1,0:T(8,128)(2,1)} %get-tuple-element.27), channel_id=1, source_target_pairs={{0,2},{1,3},{2,0},{3,1},{4,6},{5,7},{6,4},{7,5},{8,10},{9,11},{10,... | collective-permute-start | bytes 786440 | tf_op jit(solution)/shard_map/ppermute | solution.py:432
  71.4 0.0 collective-permute-done
  71.4 0.0 collective-permute-start.8
  71.4 0.8 broadcast_in_dim.22
  72.2 4.3 %all-to-all-start.1 = ((f32[8,136,128]{2,1,0:T(8,128)}), f32[8,136,128]{2,1,0:T(8,128)S(1)}, u32[]{:S(2)}, u32[]{:S(2)}) async-start(f32[8,136,128]{2,1,0:T(8,128)} %broadcast_in_dim.22), calls=%async_computation.1 | async-start | bytes 1114112 | tf_op jit(solution)/shard_map/all_to_all | solution.py:456
  76.5 5.6 %collective-permute-done.11.refs_2_ = bf16[1,128,1024]{2,1,0:T(8,128)(2,1)S(1)} collective-permute-done((bf16[1,128,1024]{2,1,0:T(8,128)(2,1)}, bf16[1,128,1024]{2,1,0:T(8,128)(2,1)S(1)}, u32[]{:S(2)}, u32[]{:S(2)}) %collective-permute-start.11) | collective-permute-done | bytes 262176 | tf_op jit(solution)/shard_map/ppermute | solution.py:432
  82.1 0.7 copy-done.5
  82.8 3.3 %collective-permute-start.1 = (bf16[1,128,1024]{2,1,0:T(8,128)(2,1)}, bf16[1,128,1024]{2,1,0:T(8,128)(2,1)S(1)}, u32[]{:S(2)}, u32[]{:S(2)}) collective-permute-start(bf16[1,128,1024]{2,1,0:T(8,128)(2,1)} %get-tuple-element.23), channel_id=1, source_target_pairs={{0,3},{3,0},{4,7},{7,4},{8,11},{11,8},{12,15},{15,12},{16,19},{19,... | collective-permute-start | bytes 786440 | tf_op jit(solution)/shard_map/ppermute | solution.py:432
  86.1 0.0 collective-permute-done.5.refs_0_
  86.1 0.7 copy-done.7
  86.8 0.7 collective-permute-start.2
  87.5 0.0 collective-permute-done.6.refs_1_
  87.5 0.7 copy-done.9
  88.2 4.9 %collective-permute-start.9 = (bf16[1,128,1024]{2,1,0:T(8,128)(2,1)}, bf16[1,128,1024]{2,1,0:T(8,128)(2,1)}, u32[]{:S(2)}, u32[]{:S(2)}) collective-permute-start(bf16[1,128,1024]{2,1,0:T(8,128)(2,1)} %get-tuple-element.29), channel_id=1, source_target_pairs={{0,1},{1,0},{2,3},{3,2},{4,5},{5,4},{6,7},{7,6},{8,9},{9,8},{10,11... | collective-permute-start | bytes 786440 | tf_op jit(solution)/shard_map/ppermute | solution.py:432
  93.1 5.9 %collective-permute-done.7.refs_2_ = bf16[1,128,1024]{2,1,0:T(8,128)(2,1)} collective-permute-done((bf16[1,128,1024]{2,1,0:T(8,128)(2,1)}, bf16[1,128,1024]{2,1,0:T(8,128)(2,1)}, u32[]{:S(2)}, u32[]{:S(2)}) %collective-permute-start.7) | collective-permute-done | bytes 262176 | tf_op jit(solution)/shard_map/ppermute | solution.py:432
  99.0 1.3 %collective-permute-start.3 = (bf16[1,128,1024]{2,1,0:T(8,128)(2,1)}, bf16[1,128,1024]{2,1,0:T(8,128)(2,1)S(1)}, u32[]{:S(2)}, u32[]{:S(2)}) collective-permute-start(bf16[1,128,1024]{2,1,0:T(8,128)(2,1)} %get-tuple-element.24), channel_id=1, source_target_pairs={{1,3},{2,0},{5,7},{6,4},{9,11},{10,8},{13,15},{14,12},{17,19},{18,... | collective-permute-start | bytes 786440 | tf_op jit(solution)/shard_map/ppermute | solution.py:432
  100.3 0.0 collective-permute-done.8.refs_3_
  100.3 5.5 %collective-permute-start.4 = (bf16[1,128,1024]{2,1,0:T(8,128)(2,1)}, bf16[1,128,1024]{2,1,0:T(8,128)(2,1)S(1)}, u32[]{:S(2)}, u32[]{:S(2)}) collective-permute-start(bf16[1,128,1024]{2,1,0:T(8,128)(2,1)} %get-tuple-element.24), channel_id=1, source_target_pairs={{0,2},{3,1},{4,6},{7,5},{8,10},{11,9},{12,14},{15,13},{16,18},{19,... | collective-permute-start | bytes 786440 | tf_op jit(solution)/shard_map/ppermute | solution.py:432
  105.8 1.3 %unpack_all.1.q_ref = bf16[16,256,128]{2,1,0:T(8,128)(2,1)S(1)} custom-call(f32[8,136,128]{2,1,0:T(8,128)S(1)} %all-to-all-done.1.packed_ref), custom_call_target="tpu_custom_call" | custom-call | tf_op jit(solution)/shard_map/unpack_all/pallas_call | solution.py:301
  107.1 0.9 copy-done.2
  108.1 0.9 copy-done.4
  109.0 0.9 copy-done.6
  110.0 2.2 %apply_blocks.3.refs_5_ = bf16[16,128,1024]{2,1,0:T(8,128)(2,1)} custom-call(bf16[16,256,128]{2,1,0:T(8,128)(2,1)S(1)} %unpack_all.1.q_ref, bf16[4,128,1024]{2,1,0:T(8,128)(2,1)S(1)} %copy-done, bf16[1,128,1024]{2,1,0:T(8,128)(2,1)S(1)} %copy-done.4, bf16[1,128,1024]{2,1,0:T(8,128)(2,1)S(1)} %copy-done.6, ...), custom_call_target="tpu_custom_call" | custom-call | tf_op jit(solution)/shard_map/apply_blocks/pallas_call | solution.py:356
  112.2 0.0 collective-permute-done.9.refs_4_
  112.2 2.7 %apply_blocks.4.refs_4_ = bf16[16,128,1024]{2,1,0:T(8,128)(2,1)} custom-call(bf16[16,256,128]{2,1,0:T(8,128)(2,1)S(1)} %unpack_all.1.q_ref, bf16[1,128,1024]{2,1,0:T(8,128)(2,1)S(1)} %copy-done.8, bf16[1,128,1024]{2,1,0:T(8,128)(2,1)S(1)} %copy-done.10, bf16[1,128,1024]{2,1,0:T(8,128)(2,1)} %collective-permute-done.7.refs_2_, ...), custom_call_target="tpu_custom_call", output_to_operand_aliasing={{}: (6, {})} | custom-call | tf_op jit(solution)/shard_map/apply_blocks/pallas_call | solution.py:356
  114.9 0.0 collective-permute-done.2.refs_1_
  114.9 0.0 collective-permute-done.3.refs_2_
  114.9 1.2 %apply_blocks.5 = bf16[16,128,1024]{2,1,0:T(8,128)(2,1)} custom-call(bf16[16,256,128]{2,1,0:T(8,128)(2,1)S(1)} %unpack_all.1.q_ref, bf16[1,128,1024]{2,1,0:T(8,128)(2,1)S(1)} %collective-permute-done.1.refs_0_, bf16[1,128,1024]{2,1,0:T(8,128)(2,1)S(1)} %collective-permute-done.2.refs_1_, ...), custom_call_target="tpu_custom_call", output_to_operand_aliasing={{}: (5, {})} | custom-call | tf_op jit(solution)/shard_map/apply_blocks/pallas_call | solution.py:356
  (25 shorter events, 0.0 us)
Async XLA Ops:
  1.3 1.4 %copy-start.12 = (s32[16]{0:T(128)}, s32[16]{0:T(128)S(1)}, u32[]{:S(2)}) copy-start(s32[16]{0:T(128)S(1)} %multiply_add_fusion.place) | copy-start | bytes 196
  12.5 15.6 %all-to-all-start = ((f32[8,144,128]{2,1,0:T(8,128)}), f32[8,144,128]{2,1,0:T(8,128)S(1)}, u32[]{:S(2)}, u32[]{:S(2)}) async-start(f32[8,144,128]{2,1,0:T(8,128)} %get-tuple-element.21), calls=%async_computation | async-start | bytes 1179648 | tf_op jit(solution)/shard_map/all_to_all | solution.py:445
  17.7 14.0 %collective-permute-start.12 = (bf16[1,128,1024]{2,1,0:T(8,128)(2,1)}, bf16[1,128,1024]{2,1,0:T(8,128)(2,1)S(1)}, u32[]{:S(2)}, u32[]{:S(2)}) collective-permute-start(bf16[1,128,1024]{2,1,0:T(8,128)(2,1)} %get-tuple-element.33), channel_id=1, source_target_pairs={{0,1},{1,0},{2,3},{3,2},{4,5},{5,4},{6,7},{7,6},{8,9},{9,8},{10,11... | collective-permute-start | bytes 786440 | tf_op jit(solution)/shard_map/ppermute | solution.py:432
  19.3 17.9 %collective-permute-start.13 = (bf16[1,128,1024]{2,1,0:T(8,128)(2,1)}, bf16[1,128,1024]{2,1,0:T(8,128)(2,1)S(1)}, u32[]{:S(2)}, u32[]{:S(2)}) collective-permute-start(bf16[1,128,1024]{2,1,0:T(8,128)(2,1)} %get-tuple-element.34), channel_id=1, source_target_pairs={{0,3},{1,2},{2,1},{3,0},{4,7},{5,6},{6,5},{7,4},{8,11},{9,10},{10,... | collective-permute-start | bytes 786440 | tf_op jit(solution)/shard_map/ppermute | solution.py:432
  21.8 6.0 %copy-start.13 = (s32[16,1]{0,1:T(1,128)S(1)}, s32[16,1]{0,1:T(1,128)}, u32[]{:S(2)}) copy-start(s32[16,1]{0,1:T(1,128)} %param.8) | copy-start | bytes 196
  21.8 6.4 %copy-start.11 = (s32[1,16]{1,0:T(1,128)S(1)}, s32[1,16]{1,0:T(1,128)}, u32[]{:S(2)}) copy-start(s32[1,16]{1,0:T(1,128)} %codes_ref.1) | copy-start | bytes 196
  21.8 85.4 %copy-start = (bf16[4,128,1024]{2,1,0:T(8,128)(2,1)S(1)}, bf16[4,128,1024]{2,1,0:T(8,128)(2,1)}, u32[]{:S(2)}) copy-start(bf16[4,128,1024]{2,1,0:T(8,128)(2,1)} %get-tuple-element.30.refs_0_) | copy-start | bytes 3145732
  21.8 36.4 %collective-permute-start.14 = (bf16[1,128,1024]{2,1,0:T(8,128)(2,1)}, bf16[1,128,1024]{2,1,0:T(8,128)(2,1)S(1)}, u32[]{:S(2)}, u32[]{:S(2)}) collective-permute-start(bf16[1,128,1024]{2,1,0:T(8,128)(2,1)} %get-tuple-element.35), channel_id=1, source_target_pairs={{0,2},{1,3},{2,0},{3,1},{4,6},{5,7},{6,4},{7,5},{8,10},{9,11},{10,... | collective-permute-start | bytes 786440 | tf_op jit(solution)/shard_map/ppermute | solution.py:432
  25.0 36.1 %collective-permute-start.10 = (bf16[1,128,1024]{2,1,0:T(8,128)(2,1)}, bf16[1,128,1024]{2,1,0:T(8,128)(2,1)S(1)}, u32[]{:S(2)}, u32[]{:S(2)}) collective-permute-start(bf16[1,128,1024]{2,1,0:T(8,128)(2,1)} %get-tuple-element.31), channel_id=1, source_target_pairs={{0,3},{1,2},{2,1},{3,0},{4,7},{5,6},{6,5},{7,4},{8,11},{9,10},{10,... | collective-permute-start | bytes 786440 | tf_op jit(solution)/shard_map/ppermute | solution.py:432
  31.1 40.3 %collective-permute-start = (f32[136,128]{1,0:T(8,128)S(1)}, f32[136,128]{1,0:T(8,128)S(1)}, u32[]{:S(2)}, u32[]{:S(2)}) collective-permute-start(f32[136,128]{1,0:T(8,128)S(1)} %get-tuple-element.22), channel_id=1, source_target_pairs={{0,0},{1,8},{2,16},{3,24},{4,2},{5,10},{6,18},{7,26},{8,1},{9,9},{... | collective-permute-start | bytes 208904 | tf_op jit(solution)/shard_map/ppermute | solution.py:454
  31.7 50.3 %collective-permute-start.11 = (bf16[1,128,1024]{2,1,0:T(8,128)(2,1)}, bf16[1,128,1024]{2,1,0:T(8,128)(2,1)S(1)}, u32[]{:S(2)}, u32[]{:S(2)}) collective-permute-start(bf16[1,128,1024]{2,1,0:T(8,128)(2,1)} %get-tuple-element.32), channel_id=1, source_target_pairs={{0,2},{1,3},{2,0},{3,1},{4,6},{5,7},{6,4},{7,5},{8,10},{9,11},{10,... | collective-permute-start | bytes 786440 | tf_op jit(solution)/shard_map/ppermute | solution.py:432
  37.1 49.0 %collective-permute-start.5 = (bf16[1,128,1024]{2,1,0:T(8,128)(2,1)}, bf16[1,128,1024]{2,1,0:T(8,128)(2,1)S(1)}, u32[]{:S(2)}, u32[]{:S(2)}) collective-permute-start(bf16[1,128,1024]{2,1,0:T(8,128)(2,1)} %get-tuple-element.25), channel_id=1, source_target_pairs={{0,1},{1,0},{2,3},{3,2},{4,5},{5,4},{6,7},{7,6},{8,9},{9,8},{10,11... | collective-permute-start | bytes 786440 | tf_op jit(solution)/shard_map/ppermute | solution.py:432
  58.1 28.0 %copy-start.1 = (bf16[1,128,1024]{2,1,0:T(8,128)(2,1)}, bf16[1,128,1024]{2,1,0:T(8,128)(2,1)S(1)}, u32[]{:S(2)}) copy-start(bf16[1,128,1024]{2,1,0:T(8,128)(2,1)S(1)} %collective-permute-done.14.refs_5_) | copy-start | bytes 786436
  58.1 29.4 %collective-permute-start.6 = (bf16[1,128,1024]{2,1,0:T(8,128)(2,1)}, bf16[1,128,1024]{2,1,0:T(8,128)(2,1)S(1)}, u32[]{:S(2)}, u32[]{:S(2)}) collective-permute-start(bf16[1,128,1024]{2,1,0:T(8,128)(2,1)} %get-tuple-element.26), channel_id=1, source_target_pairs={{0,3},{1,2},{2,1},{3,0},{4,7},{5,6},{6,5},{7,4},{8,11},{9,10},{10,... | collective-permute-start | bytes 786440 | tf_op jit(solution)/shard_map/ppermute | solution.py:432
  61.1 11.2 %copy-start.3 = (bf16[1,128,1024]{2,1,0:T(8,128)(2,1)}, bf16[1,128,1024]{2,1,0:T(8,128)(2,1)S(1)}, u32[]{:S(2)}) copy-start(bf16[1,128,1024]{2,1,0:T(8,128)(2,1)S(1)} %collective-permute-done.10.refs_1_) | copy-start | bytes 786436
  61.1 38.0 %collective-permute-start.7 = (bf16[1,128,1024]{2,1,0:T(8,128)(2,1)}, bf16[1,128,1024]{2,1,0:T(8,128)(2,1)}, u32[]{:S(2)}, u32[]{:S(2)}) collective-permute-start(bf16[1,128,1024]{2,1,0:T(8,128)(2,1)} %get-tuple-element.27), channel_id=1, source_target_pairs={{0,2},{1,3},{2,0},{3,1},{4,6},{5,7},{6,4},{7,5},{8,10},{9,11},{10,... | collective-permute-start | bytes 786440 | tf_op jit(solution)/shard_map/ppermute | solution.py:432
  71.4 28.9 %collective-permute-start.8 = (bf16[1,128,1024]{2,1,0:T(8,128)(2,1)}, bf16[1,128,1024]{2,1,0:T(8,128)(2,1)}, u32[]{:S(2)}, u32[]{:S(2)}) collective-permute-start(bf16[1,128,1024]{2,1,0:T(8,128)(2,1)} %get-tuple-element.28), channel_id=1, source_target_pairs={{0,1},{1,0},{2,3},{3,2},{4,5},{5,4},{6,7},{7,6},{8,9},{9,8},{10,11... | collective-permute-start | bytes 786440 | tf_op jit(solution)/shard_map/ppermute | solution.py:432
  72.2 33.6 %all-to-all-start.1 = ((f32[8,136,128]{2,1,0:T(8,128)}), f32[8,136,128]{2,1,0:T(8,128)S(1)}, u32[]{:S(2)}, u32[]{:S(2)}) async-start(f32[8,136,128]{2,1,0:T(8,128)} %broadcast_in_dim.22), calls=%async_computation.1 | async-start | bytes 1114112 | tf_op jit(solution)/shard_map/all_to_all | solution.py:456
  82.1 0.7 copy-start.5
  82.8 32.1 %collective-permute-start.1 = (bf16[1,128,1024]{2,1,0:T(8,128)(2,1)}, bf16[1,128,1024]{2,1,0:T(8,128)(2,1)S(1)}, u32[]{:S(2)}, u32[]{:S(2)}) collective-permute-start(bf16[1,128,1024]{2,1,0:T(8,128)(2,1)} %get-tuple-element.23), channel_id=1, source_target_pairs={{0,3},{3,0},{4,7},{7,4},{8,11},{11,8},{12,15},{15,12},{16,19},{19,... | collective-permute-start | bytes 786440 | tf_op jit(solution)/shard_map/ppermute | solution.py:432
  86.1 0.7 copy-start.7
  86.8 28.1 %collective-permute-start.2 = (bf16[1,128,1024]{2,1,0:T(8,128)(2,1)}, bf16[1,128,1024]{2,1,0:T(8,128)(2,1)S(1)}, u32[]{:S(2)}, u32[]{:S(2)}) collective-permute-start(bf16[1,128,1024]{2,1,0:T(8,128)(2,1)} %get-tuple-element.23), channel_id=1, source_target_pairs={{1,2},{2,1},{5,6},{6,5},{9,10},{10,9},{13,14},{14,13},{17,18},{18,... | collective-permute-start | bytes 786440 | tf_op jit(solution)/shard_map/ppermute | solution.py:432
  87.5 0.7 copy-start.9
  88.2 23.9 %collective-permute-start.9 = (bf16[1,128,1024]{2,1,0:T(8,128)(2,1)}, bf16[1,128,1024]{2,1,0:T(8,128)(2,1)}, u32[]{:S(2)}, u32[]{:S(2)}) collective-permute-start(bf16[1,128,1024]{2,1,0:T(8,128)(2,1)} %get-tuple-element.29), channel_id=1, source_target_pairs={{0,1},{1,0},{2,3},{3,2},{4,5},{5,4},{6,7},{7,6},{8,9},{9,8},{10,11... | collective-permute-start | bytes 786440 | tf_op jit(solution)/shard_map/ppermute | solution.py:432
  99.0 15.9 %collective-permute-start.3 = (bf16[1,128,1024]{2,1,0:T(8,128)(2,1)}, bf16[1,128,1024]{2,1,0:T(8,128)(2,1)S(1)}, u32[]{:S(2)}, u32[]{:S(2)}) collective-permute-start(bf16[1,128,1024]{2,1,0:T(8,128)(2,1)} %get-tuple-element.24), channel_id=1, source_target_pairs={{1,3},{2,0},{5,7},{6,4},{9,11},{10,8},{13,15},{14,12},{17,19},{18,... | collective-permute-start | bytes 786440 | tf_op jit(solution)/shard_map/ppermute | solution.py:432
  100.3 14.6 %collective-permute-start.4 = (bf16[1,128,1024]{2,1,0:T(8,128)(2,1)}, bf16[1,128,1024]{2,1,0:T(8,128)(2,1)S(1)}, u32[]{:S(2)}, u32[]{:S(2)}) collective-permute-start(bf16[1,128,1024]{2,1,0:T(8,128)(2,1)} %get-tuple-element.24), channel_id=1, source_target_pairs={{0,2},{3,1},{4,6},{7,5},{8,10},{11,9},{12,14},{15,13},{16,18},{19,... | collective-permute-start | bytes 786440 | tf_op jit(solution)/shard_map/ppermute | solution.py:432
  107.1 1.0 copy-start.2
  108.1 0.9 copy-start.4
  109.0 0.9 copy-start.6
  110.0 2.2 %copy-start.8 = (bf16[1,128,1024]{2,1,0:T(8,128)(2,1)S(1)}, bf16[1,128,1024]{2,1,0:T(8,128)(2,1)}, u32[]{:S(2)}) copy-start(bf16[1,128,1024]{2,1,0:T(8,128)(2,1)} %copy-done.7) | copy-start | bytes 786436
  110.0 2.2 %copy-start.10 = (bf16[1,128,1024]{2,1,0:T(8,128)(2,1)S(1)}, bf16[1,128,1024]{2,1,0:T(8,128)(2,1)}, u32[]{:S(2)}) copy-start(bf16[1,128,1024]{2,1,0:T(8,128)(2,1)} %copy-done.9) | copy-start | bytes 786436

commit v5 on v4

--- a/solution.py
+++ b/solution.py
@@ -121,12 +121,11 @@
     buffer = pltpu.VMEM((count, pieces, head // pieces, width), jnp.bfloat16)
     return pl.pallas_call(
         functools.partial(first_kernel, wanted, pieces),
-        out_shape=[jax.ShapeDtypeStruct((1, head, width), jnp.bfloat16)] * count,
+        out_shape=[pltpu.VMEM((1, head, width), jnp.bfloat16)] * count,
         in_specs=[SMEM, HBM, HBM],
         out_specs=[VMEM] * count,
         scratch_shapes=[buffer] * 2 + [pltpu.SemaphoreType.DMA((count, pieces))] * 2,
         compiler_params=params_beside(grads),
-        name="first_blocks",
     )(codes, grads, momentum)
 
 
@@ -431,9 +430,11 @@
             pairs = [(t, to) for t, to in pairs if (to in ends) == (side == 0)]
         got[chunk, side] = lax.ppermute(array, "tp", pairs)
 
-    wanted = [(functools.partial(partner, x=x), cs[0]) for x, cs in first]
-    for chunk, array in zip(first, first_blocks(pool_map, grads, momentum, wanted)):
-        send(chunk, None, array)
+    for some in (first[:1], first[1:]):
+        wanted = [(functools.partial(partner, x=x), cs[0]) for x, cs in some]
+        arrays = first_blocks(pool_map, grads, momentum, wanted) if some else []
+        for chunk, array in zip(some, arrays):
+            send(chunk, None, array)
     rest = chunks[len(first) :]
     new_momentum, parts, *ys = all_blocks(
         source, place_out, grads, momentum, [starts[chunk] for chunk in rest], spread, n_fsdp

time: 117 us -> 116 us (level)
  starting transfers between devices: 67 us -> 64.2 us
  waiting for transfers between devices: 17.3 us -> 19.1 us
  Pallas kernels: 23 us -> 24.5 us
    ppermute x14, starting transfers between devices: 56.8 us -> 52.4 us  [send(): got[chunk, side] = lax.ppermute(array, 'tp', pairs)]
    unnamed x29 -> x21, local copies, waits for them, and re-layouts: 5.03 us -> 3.41 us
    ppermute x1, starting transfers between devices: 0.67 us -> 2.25 us  [local(): packed = lax.ppermute(packed, ('fsdp', 'tp'), pairs)]
    pallas_call x1 -> x2, Pallas kernels: 2.99 us -> 3.68 us  [first_blocks(): pl.pallas_call(functools.partial(first_kernel, wanted, pieces), out_shape...]
  transfers between devices with their start and end apart: 17 -> 17, of which waited for: 4 -> 5; matrix products, arithmetic and copies ran while one was open for 1% -> 2% of each run, Pallas kernels for 10% -> 12%
where the time goes in v5:
time: 116 us
  starting transfers between devices  64.2 us (55%)
  Pallas kernels  24.5 us (21%)
  waiting for transfers between devices  19.1 us (16%)
  local copies, waits for them, and re-layouts  5.17 us (4%)
  other arithmetic  2.03 us (2%)
    ppermute x14, starting transfers between devices, send(): got[chunk, side] = lax.ppermute(array, 'tp', pairs)  52.4 us
    ppermute x14, waiting for transfers between devices, send(): got[chunk, side] = lax.ppermute(array, 'tp', pairs)  17.7 us
    pallas_call x1, Pallas kernels, all_blocks(): pl.pallas_call(functools.partial(all_kernel, spans, spread, min(width, 25...  9.86 us
    pallas_call x3, Pallas kernels, apply_blocks(): pl.pallas_call(functools.partial(apply_kernel, factor, members, at_end, t...  6.09 us
    all_to_all x1, starting transfers between devices, local(): lax.all_to_all(parts, 'fsdp', split_axis=0, concat_axis=0, tiled=True)  5.21 us
    all_to_all x1, starting transfers between devices, local(): lax.all_to_all(packed, 'fsdp', split_axis=0, concat_axis=0, tiled=True)  4.37 us
    pallas_call x2, Pallas kernels, first_blocks(): pl.pallas_call(functools.partial(first_kernel, wanted, pieces), out_shape...  3.68 us
    pallas_call x1, Pallas kernels, solve(): pl.pallas_call(functools.partial(solve_kernel, spread, count, elements),...  3.54 us
  transfers between devices with their start and end apart: 17, of which 5 were waited for; matrix products, arithmetic and copies ran while one was open for 2% of the time, Pallas kernels for 12%

profile of v5, /device:TPU:0, one launch (start us, length us, event | category | flops | bytes accessed | tf_op | source)
XLA Modules:
  0.0 115.8 jit_solution(4761721107227068905)
XLA Ops:
  0.6 0.7 multiply_add_fusion.place
  1.3 1.3 %select_reduce_fusion.source = s32[16]{0:T(128)} fusion(s32[16]{0:T(128)} %bitcast.2, s32[16]{0:T(128)S(1)} %multiply_add_fusion.place), kind=kLoop, calls=%fused_computation | loop fusion | flops 752 | bytes 192 | tf_op jit(solution)/shard_map/reduce_sum | solution.py:409
  2.7 9.9 %all_blocks.1 = (bf16[16,128,1024]{2,1,0:T(8,128)(2,1)}, f32[8,144,128]{2,1,0:T(8,128)}, bf16[1,128,1024]{2,1,0:T(8,128)(2,1)}, bf16[1,128,1024]{2,1,0:T(8,128)(...) custom-call(s32[16]{0:T(128)} %select_reduce_fusion.source, ...), custom_call_target="tpu_custom_call" | custom-call | tf_op jit(solution)/shard_map/all_blocks/pallas_call | solution.py:198
  12.5 5.2 %all-to-all-start = ((f32[8,144,128]{2,1,0:T(8,128)}), f32[8,144,128]{2,1,0:T(8,128)S(1)}, u32[]{:S(2)}, u32[]{:S(2)}) async-start(f32[8,144,128]{2,1,0:T(8,128)} %get-tuple-element.19), calls=%async_computation | async-start | bytes 1179648 | tf_op jit(solution)/shard_map/all_to_all | solution.py:446
  17.7 1.6 %collective-permute-start.12 = (bf16[1,128,1024]{2,1,0:T(8,128)(2,1)}, bf16[1,128,1024]{2,1,0:T(8,128)(2,1)S(1)}, u32[]{:S(2)}, u32[]{:S(2)}) collective-permute-start(bf16[1,128,1024]{2,1,0:T(8,128)(2,1)} %get-tuple-element.29), channel_id=1, source_target_pairs={{0,1},{1,0},{2,3},{3,2},{4,5},{5,4},{6,7},{7,6},{8,9},{9,8},{10,11... | collective-permute-start | bytes 786440 | tf_op jit(solution)/shard_map/ppermute | solution.py:431
  19.3 2.5 %collective-permute-start.13 = (bf16[1,128,1024]{2,1,0:T(8,128)(2,1)}, bf16[1,128,1024]{2,1,0:T(8,128)(2,1)S(1)}, u32[]{:S(2)}, u32[]{:S(2)}) collective-permute-start(bf16[1,128,1024]{2,1,0:T(8,128)(2,1)} %get-tuple-element.30), channel_id=1, source_target_pairs={{0,3},{1,2},{2,1},{3,0},{4,7},{5,6},{6,5},{7,4},{8,11},{9,10},{10,... | collective-permute-start | bytes 786440 | tf_op jit(solution)/shard_map/ppermute | solution.py:431
  21.8 0.1 collective-permute-start.14
  21.9 1.8 %shard_map.85 = bf16[1,128,1024]{2,1,0:T(8,128)(2,1)S(1)} custom-call(s32[1,16]{1,0:T(1,128)} %codes_ref.3, bf16[16,128,1024]{2,1,0:T(8,128)(2,1)} %g_ref.5, bf16[16,128,1024]{2,1,0:T(8,128)(2,1)} %m_ref.5), custom_call_target="tpu_custom_call" | custom-call | tf_op jit(solution)/shard_map/pallas_call | solution.py:122
  23.8 3.0 %collective-permute-start.10 = (bf16[1,128,1024]{2,1,0:T(8,128)(2,1)S(1)}, bf16[1,128,1024]{2,1,0:T(8,128)(2,1)S(1)}, u32[]{:S(2)}, u32[]{:S(2)}) collective-permute-start(bf16[1,128,1024]{2,1,0:T(8,128)(2,1)S(1)} %shard_map.85), channel_id=1, source_target_pairs={{0,3},{1,2},{2,1},{3,0},{4,7},{5,6},{6,5},{7,4},{8,11},{9,10},{10,... | collective-permute-start | bytes 786440 | tf_op jit(solution)/shard_map/ppermute | solution.py:431
  26.8 0.1 copy.12.owners
  26.8 1.3 %all-to-all-done.parts_ref = f32[8,144,128]{2,1,0:T(8,128)S(1)} async-done(((f32[8,144,128]{2,1,0:T(8,128)}), f32[8,144,128]{2,1,0:T(8,128)S(1)}, u32[]{:S(2)}, u32[]{:S(2)}) %all-to-all-start) | async-done | bytes 589856 | tf_op jit(solution)/shard_map/all_to_all | solution.py:446
  28.2 3.5 %solve.1 = (f32[136,128]{1,0:T(8,128)}, f32[1,128]{1,0:T(1,128)}) custom-call(s32[16,1]{1,0:T(8,128)S(1)} %copy.12.owners, s32[1,16]{1,0:T(1,128)S(1)} %copy-done.7, f32[8,144,128]{2,1,0:T(8,128)S(1)} %all-to-all-done.parts_ref), custom_call_target="tpu_custom_call" | custom-call | tf_op jit(solution)/shard_map/solve/pallas_call | solution.py:270
  31.7 2.2 %collective-permute-start = (f32[136,128]{1,0:T(8,128)}, f32[136,128]{1,0:T(8,128)}, u32[]{:S(2)}, u32[]{:S(2)}) collective-permute-start(f32[136,128]{1,0:T(8,128)} %get-tuple-element.20), channel_id=1, source_target_pairs={{0,0},{1,8},{2,16},{3,24},{4,2},{5,10},{6,18},{7,26},{8,1},{9,9},{... | collective-permute-start | bytes 208904 | tf_op jit(solution)/shard_map/ppermute | solution.py:455
  34.0 1.8 %shard_map.86 = bf16[1,128,1024]{2,1,0:T(8,128)(2,1)S(1)} custom-call(s32[1,16]{1,0:T(1,128)} %codes_ref.3, bf16[16,128,1024]{2,1,0:T(8,128)(2,1)} %g_ref.5, bf16[16,128,1024]{2,1,0:T(8,128)(2,1)} %m_ref.5), custom_call_target="tpu_custom_call" | custom-call | tf_op jit(solution)/shard_map/pallas_call | solution.py:122
  35.8 0.0 collective-permute-done.12.refs_3_
  35.8 2.9 %collective-permute-start.11 = (bf16[1,128,1024]{2,1,0:T(8,128)(2,1)S(1)}, bf16[1,128,1024]{2,1,0:T(8,128)(2,1)S(1)}, u32[]{:S(2)}, u32[]{:S(2)}) collective-permute-start(bf16[1,128,1024]{2,1,0:T(8,128)(2,1)S(1)} %shard_map.86), channel_id=1, source_target_pairs={{0,2},{1,3},{2,0},{3,1},{4,6},{5,7},{6,4},{7,5},{8,10},{9,11},{10,... | collective-permute-start | bytes 786440 | tf_op jit(solution)/shard_map/ppermute | solution.py:431
  38.7 0.0 collective-permute-done.13.refs_4_
  38.7 14.0 %collective-permute-start.5 = (bf16[1,128,1024]{2,1,0:T(8,128)(2,1)}, bf16[1,128,1024]{2,1,0:T(8,128)(2,1)S(1)}, u32[]{:S(2)}, u32[]{:S(2)}) collective-permute-start(bf16[1,128,1024]{2,1,0:T(8,128)(2,1)} %get-tuple-element.23), channel_id=1, source_target_pairs={{0,1},{1,0},{2,3},{3,2},{4,5},{5,4},{6,7},{7,6},{8,9},{9,8},{10,11... | collective-permute-start | bytes 786440 | tf_op jit(solution)/shard_map/ppermute | solution.py:431
  52.7 5.5 %collective-permute-done.14.refs_5_ = bf16[1,128,1024]{2,1,0:T(8,128)(2,1)S(1)} collective-permute-done((bf16[1,128,1024]{2,1,0:T(8,128)(2,1)}, bf16[1,128,1024]{2,1,0:T(8,128)(2,1)S(1)}, u32[]{:S(2)}, u32[]{:S(2)}) %collective-permute-start.14) | collective-permute-done | bytes 262176 | tf_op jit(solution)/shard_map/ppermute | solution.py:431
  58.2 2.9 %collective-permute-start.6 = (bf16[1,128,1024]{2,1,0:T(8,128)(2,1)}, bf16[1,128,1024]{2,1,0:T(8,128)(2,1)}, u32[]{:S(2)}, u32[]{:S(2)}) collective-permute-start(bf16[1,128,1024]{2,1,0:T(8,128)(2,1)} %get-tuple-element.24), channel_id=1, source_target_pairs={{0,3},{1,2},{2,1},{3,0},{4,7},{5,6},{6,5},{7,4},{8,11},{9,10},{10,... | collective-permute-start | bytes 786440 | tf_op jit(solution)/shard_map/ppermute | solution.py:431
  61.1 0.0 collective-permute-done.10.refs_1_
  61.1 10.3 %collective-permute-start.7 = (bf16[1,128,1024]{2,1,0:T(8,128)(2,1)}, bf16[1,128,1024]{2,1,0:T(8,128)(2,1)}, u32[]{:S(2)}, u32[]{:S(2)}) collective-permute-start(bf16[1,128,1024]{2,1,0:T(8,128)(2,1)} %get-tuple-element.25), channel_id=1, source_target_pairs={{0,2},{1,3},{2,0},{3,1},{4,6},{5,7},{6,4},{7,5},{8,10},{9,11},{10,... | collective-permute-start | bytes 786440 | tf_op jit(solution)/shard_map/ppermute | solution.py:431
  71.4 0.0 collective-permute-start.8
  71.4 1.8 %broadcast_in_dim.22 = f32[8,136,128]{2,1,0:T(8,128)} broadcast(f32[136,128]{1,0:T(8,128)} %collective-permute-done), dimensions={1,2} | broadcast | bytes 626688 | tf_op jit(solution)/shard_map/broadcast_in_dim | solution.py:456
  73.2 4.4 %all-to-all-start.1 = ((f32[8,136,128]{2,1,0:T(8,128)}), f32[8,136,128]{2,1,0:T(8,128)S(1)}, u32[]{:S(2)}, u32[]{:S(2)}) async-start(f32[8,136,128]{2,1,0:T(8,128)} %broadcast_in_dim.22), calls=%async_computation.1 | async-start | bytes 1114112 | tf_op jit(solution)/shard_map/all_to_all | solution.py:457
  77.6 4.6 %collective-permute-done.11.refs_2_ = bf16[1,128,1024]{2,1,0:T(8,128)(2,1)S(1)} collective-permute-done((bf16[1,128,1024]{2,1,0:T(8,128)(2,1)S(1)}, bf16[1,128,1024]{2,1,0:T(8,128)(2,1)S(1)}, u32[]{:S(2)}, u32[]{:S(2)}) %collective-permute-start.11) | collective-permute-done | bytes 262176 | tf_op jit(solution)/shard_map/ppermute | solution.py:431
  82.1 0.7 copy-done.3
  82.8 3.3 %collective-permute-start.1 = (bf16[1,128,1024]{2,1,0:T(8,128)(2,1)}, bf16[1,128,1024]{2,1,0:T(8,128)(2,1)S(1)}, u32[]{:S(2)}, u32[]{:S(2)}) collective-permute-start(bf16[1,128,1024]{2,1,0:T(8,128)(2,1)} %get-tuple-element.21), channel_id=1, source_target_pairs={{0,3},{3,0},{4,7},{7,4},{8,11},{11,8},{12,15},{15,12},{16,19},{19,... | collective-permute-start | bytes 786440 | tf_op jit(solution)/shard_map/ppermute | solution.py:431
  86.2 0.0 collective-permute-done.5.refs_0_
  86.2 0.7 copy-done.5
  86.9 0.7 collective-permute-start.2
  87.6 0.0 collective-permute-done.6.refs_1_
  87.6 4.4 %collective-permute-start.9 = (bf16[1,128,1024]{2,1,0:T(8,128)(2,1)}, bf16[1,128,1024]{2,1,0:T(8,128)(2,1)}, u32[]{:S(2)}, u32[]{:S(2)}) collective-permute-start(bf16[1,128,1024]{2,1,0:T(8,128)(2,1)} %get-tuple-element.27), channel_id=1, source_target_pairs={{0,1},{1,0},{2,3},{3,2},{4,5},{5,4},{6,7},{7,6},{8,9},{9,8},{10,11... | collective-permute-start | bytes 786440 | tf_op jit(solution)/shard_map/ppermute | solution.py:431
  91.9 7.2 %collective-permute-done.7.refs_2_ = bf16[1,128,1024]{2,1,0:T(8,128)(2,1)} collective-permute-done((bf16[1,128,1024]{2,1,0:T(8,128)(2,1)}, bf16[1,128,1024]{2,1,0:T(8,128)(2,1)}, u32[]{:S(2)}, u32[]{:S(2)}) %collective-permute-start.7) | collective-permute-done | bytes 262176 | tf_op jit(solution)/shard_map/ppermute | solution.py:431
  99.1 1.3 %collective-permute-start.3 = (bf16[1,128,1024]{2,1,0:T(8,128)(2,1)}, bf16[1,128,1024]{2,1,0:T(8,128)(2,1)S(1)}, u32[]{:S(2)}, u32[]{:S(2)}) collective-permute-start(bf16[1,128,1024]{2,1,0:T(8,128)(2,1)} %get-tuple-element.22), channel_id=1, source_target_pairs={{1,3},{2,0},{5,7},{6,4},{9,11},{10,8},{13,15},{14,12},{17,19},{18,... | collective-permute-start | bytes 786440 | tf_op jit(solution)/shard_map/ppermute | solution.py:431
  100.4 0.0 collective-permute-done.8.refs_3_
  100.4 5.5 %collective-permute-start.4 = (bf16[1,128,1024]{2,1,0:T(8,128)(2,1)}, bf16[1,128,1024]{2,1,0:T(8,128)(2,1)S(1)}, u32[]{:S(2)}, u32[]{:S(2)}) collective-permute-start(bf16[1,128,1024]{2,1,0:T(8,128)(2,1)} %get-tuple-element.22), channel_id=1, source_target_pairs={{0,2},{3,1},{4,6},{7,5},{8,10},{11,9},{12,14},{15,13},{16,18},{19,... | collective-permute-start | bytes 786440 | tf_op jit(solution)/shard_map/ppermute | solution.py:431
  105.9 0.0 all-to-all-done.1.packed_ref
  105.9 1.3 %unpack_all.1.q_ref = bf16[16,256,128]{2,1,0:T(8,128)(2,1)S(1)} custom-call(f32[8,136,128]{2,1,0:T(8,128)S(1)} %all-to-all-done.1.packed_ref), custom_call_target="tpu_custom_call" | custom-call | tf_op jit(solution)/shard_map/unpack_all/pallas_call | solution.py:300
  107.2 0.9 copy-done.2
  108.1 0.9 copy-done.4
  109.1 2.2 %apply_blocks.3.refs_5_ = bf16[16,128,1024]{2,1,0:T(8,128)(2,1)} custom-call(bf16[16,256,128]{2,1,0:T(8,128)(2,1)S(1)} %unpack_all.1.q_ref, bf16[4,128,1024]{2,1,0:T(8,128)(2,1)S(1)} %copy-done, bf16[1,128,1024]{2,1,0:T(8,128)(2,1)S(1)} %copy-done.2, bf16[1,128,1024]{2,1,0:T(8,128)(2,1)S(1)} %copy-done.4, ...), custom_call_target="tpu_custom_call" | custom-call | tf_op jit(solution)/shard_map/apply_blocks/pallas_call | solution.py:355
  111.2 0.0 collective-permute-done.9.refs_4_
  111.3 2.8 %apply_blocks.4.refs_4_ = bf16[16,128,1024]{2,1,0:T(8,128)(2,1)} custom-call(bf16[16,256,128]{2,1,0:T(8,128)(2,1)S(1)} %unpack_all.1.q_ref, bf16[1,128,1024]{2,1,0:T(8,128)(2,1)S(1)} %copy-done.6, bf16[1,128,1024]{2,1,0:T(8,128)(2,1)} %collective-permute-done.6.refs_1_, ...), custom_call_target="tpu_custom_call", output_to_operand_aliasing={{}: (6, {})} | custom-call | tf_op jit(solution)/shard_map/apply_blocks/pallas_call | solution.py:355
  114.0 0.0 collective-permute-done.1.refs_0_
  114.1 0.0 collective-permute-done.2.refs_1_
  114.1 0.5 collective-permute-done.3.refs_2_
  114.6 1.2 apply_blocks.5
  (18 shorter events, 0.0 us)
Async XLA Ops:
  1.3 1.4 %copy-start.8 = (s32[16]{0:T(128)}, s32[16]{0:T(128)S(1)}, u32[]{:S(2)}) copy-start(s32[16]{0:T(128)S(1)} %multiply_add_fusion.place) | copy-start | bytes 196
  12.5 15.6 %all-to-all-start = ((f32[8,144,128]{2,1,0:T(8,128)}), f32[8,144,128]{2,1,0:T(8,128)S(1)}, u32[]{:S(2)}, u32[]{:S(2)}) async-start(f32[8,144,128]{2,1,0:T(8,128)} %get-tuple-element.19), calls=%async_computation | async-start | bytes 1179648 | tf_op jit(solution)/shard_map/all_to_all | solution.py:446
  17.7 18.1 %collective-permute-start.12 = (bf16[1,128,1024]{2,1,0:T(8,128)(2,1)}, bf16[1,128,1024]{2,1,0:T(8,128)(2,1)S(1)}, u32[]{:S(2)}, u32[]{:S(2)}) collective-permute-start(bf16[1,128,1024]{2,1,0:T(8,128)(2,1)} %get-tuple-element.29), channel_id=1, source_target_pairs={{0,1},{1,0},{2,3},{3,2},{4,5},{5,4},{6,7},{7,6},{8,9},{9,8},{10,11... | collective-permute-start | bytes 786440 | tf_op jit(solution)/shard_map/ppermute | solution.py:431
  19.3 19.4 %collective-permute-start.13 = (bf16[1,128,1024]{2,1,0:T(8,128)(2,1)}, bf16[1,128,1024]{2,1,0:T(8,128)(2,1)S(1)}, u32[]{:S(2)}, u32[]{:S(2)}) collective-permute-start(bf16[1,128,1024]{2,1,0:T(8,128)(2,1)} %get-tuple-element.30), channel_id=1, source_target_pairs={{0,3},{1,2},{2,1},{3,0},{4,7},{5,6},{6,5},{7,4},{8,11},{9,10},{10,... | collective-permute-start | bytes 786440 | tf_op jit(solution)/shard_map/ppermute | solution.py:431
  21.8 5.0 %copy-start.9 = (s32[16,1]{0,1:T(1,128)S(1)}, s32[16,1]{0,1:T(1,128)}, u32[]{:S(2)}) copy-start(s32[16,1]{0,1:T(1,128)} %param.8) | copy-start | bytes 196
  21.8 6.4 %copy-start.7 = (s32[1,16]{1,0:T(1,128)S(1)}, s32[1,16]{1,0:T(1,128)}, u32[]{:S(2)}) copy-start(s32[1,16]{1,0:T(1,128)} %codes_ref.3) | copy-start | bytes 196
  21.8 36.4 %collective-permute-start.14 = (bf16[1,128,1024]{2,1,0:T(8,128)(2,1)}, bf16[1,128,1024]{2,1,0:T(8,128)(2,1)S(1)}, u32[]{:S(2)}, u32[]{:S(2)}) collective-permute-start(bf16[1,128,1024]{2,1,0:T(8,128)(2,1)} %get-tuple-element.31), channel_id=1, source_target_pairs={{0,2},{1,3},{2,0},{3,1},{4,6},{5,7},{6,4},{7,5},{8,10},{9,11},{10,... | collective-permute-start | bytes 786440 | tf_op jit(solution)/shard_map/ppermute | solution.py:431
  23.8 37.3 %collective-permute-start.10 = (bf16[1,128,1024]{2,1,0:T(8,128)(2,1)S(1)}, bf16[1,128,1024]{2,1,0:T(8,128)(2,1)S(1)}, u32[]{:S(2)}, u32[]{:S(2)}) collective-permute-start(bf16[1,128,1024]{2,1,0:T(8,128)(2,1)S(1)} %shard_map.85), channel_id=1, source_target_pairs={{0,3},{1,2},{2,1},{3,0},{4,7},{5,6},{6,5},{7,4},{8,11},{9,10},{10,... | collective-permute-start | bytes 786440 | tf_op jit(solution)/shard_map/ppermute | solution.py:431
  31.7 75.5 %copy-start = (bf16[4,128,1024]{2,1,0:T(8,128)(2,1)S(1)}, bf16[4,128,1024]{2,1,0:T(8,128)(2,1)}, u32[]{:S(2)}) copy-start(bf16[4,128,1024]{2,1,0:T(8,128)(2,1)} %get-tuple-element.28.refs_0_) | copy-start | bytes 3145732
  31.7 39.7 %collective-permute-start = (f32[136,128]{1,0:T(8,128)}, f32[136,128]{1,0:T(8,128)}, u32[]{:S(2)}, u32[]{:S(2)}) collective-permute-start(f32[136,128]{1,0:T(8,128)} %get-tuple-element.20), channel_id=1, source_target_pairs={{0,0},{1,8},{2,16},{3,24},{4,2},{5,10},{6,18},{7,26},{8,1},{9,9},{... | collective-permute-start | bytes 208904 | tf_op jit(solution)/shard_map/ppermute | solution.py:455
  35.8 46.3 %collective-permute-start.11 = (bf16[1,128,1024]{2,1,0:T(8,128)(2,1)S(1)}, bf16[1,128,1024]{2,1,0:T(8,128)(2,1)S(1)}, u32[]{:S(2)}, u32[]{:S(2)}) collective-permute-start(bf16[1,128,1024]{2,1,0:T(8,128)(2,1)S(1)} %shard_map.86), channel_id=1, source_target_pairs={{0,2},{1,3},{2,0},{3,1},{4,6},{5,7},{6,4},{7,5},{8,10},{9,11},{10,... | collective-permute-start | bytes 786440 | tf_op jit(solution)/shard_map/ppermute | solution.py:431
  38.7 47.4 %collective-permute-start.5 = (bf16[1,128,1024]{2,1,0:T(8,128)(2,1)}, bf16[1,128,1024]{2,1,0:T(8,128)(2,1)S(1)}, u32[]{:S(2)}, u32[]{:S(2)}) collective-permute-start(bf16[1,128,1024]{2,1,0:T(8,128)(2,1)} %get-tuple-element.23), channel_id=1, source_target_pairs={{0,1},{1,0},{2,3},{3,2},{4,5},{5,4},{6,7},{7,6},{8,9},{9,8},{10,11... | collective-permute-start | bytes 786440 | tf_op jit(solution)/shard_map/ppermute | solution.py:431
  58.2 29.4 %collective-permute-start.6 = (bf16[1,128,1024]{2,1,0:T(8,128)(2,1)}, bf16[1,128,1024]{2,1,0:T(8,128)(2,1)}, u32[]{:S(2)}, u32[]{:S(2)}) collective-permute-start(bf16[1,128,1024]{2,1,0:T(8,128)(2,1)} %get-tuple-element.24), channel_id=1, source_target_pairs={{0,3},{1,2},{2,1},{3,0},{4,7},{5,6},{6,5},{7,4},{8,11},{9,10},{10,... | collective-permute-start | bytes 786440 | tf_op jit(solution)/shard_map/ppermute | solution.py:431
  61.1 25.1 %copy-start.1 = (bf16[1,128,1024]{2,1,0:T(8,128)(2,1)}, bf16[1,128,1024]{2,1,0:T(8,128)(2,1)S(1)}, u32[]{:S(2)}) copy-start(bf16[1,128,1024]{2,1,0:T(8,128)(2,1)S(1)} %collective-permute-done.10.refs_1_) | copy-start | bytes 786436
  61.1 38.0 %collective-permute-start.7 = (bf16[1,128,1024]{2,1,0:T(8,128)(2,1)}, bf16[1,128,1024]{2,1,0:T(8,128)(2,1)}, u32[]{:S(2)}, u32[]{:S(2)}) collective-permute-start(bf16[1,128,1024]{2,1,0:T(8,128)(2,1)} %get-tuple-element.25), channel_id=1, source_target_pairs={{0,2},{1,3},{2,0},{3,1},{4,6},{5,7},{6,4},{7,5},{8,10},{9,11},{10,... | collective-permute-start | bytes 786440 | tf_op jit(solution)/shard_map/ppermute | solution.py:431
  71.4 29.0 %collective-permute-start.8 = (bf16[1,128,1024]{2,1,0:T(8,128)(2,1)}, bf16[1,128,1024]{2,1,0:T(8,128)(2,1)}, u32[]{:S(2)}, u32[]{:S(2)}) collective-permute-start(bf16[1,128,1024]{2,1,0:T(8,128)(2,1)} %get-tuple-element.26), channel_id=1, source_target_pairs={{0,1},{1,0},{2,3},{3,2},{4,5},{5,4},{6,7},{7,6},{8,9},{9,8},{10,11... | collective-permute-start | bytes 786440 | tf_op jit(solution)/shard_map/ppermute | solution.py:431
  73.2 32.7 %all-to-all-start.1 = ((f32[8,136,128]{2,1,0:T(8,128)}), f32[8,136,128]{2,1,0:T(8,128)S(1)}, u32[]{:S(2)}, u32[]{:S(2)}) async-start(f32[8,136,128]{2,1,0:T(8,128)} %broadcast_in_dim.22), calls=%async_computation.1 | async-start | bytes 1114112 | tf_op jit(solution)/shard_map/all_to_all | solution.py:457
  82.1 0.7 copy-start.3
  82.8 31.2 %collective-permute-start.1 = (bf16[1,128,1024]{2,1,0:T(8,128)(2,1)}, bf16[1,128,1024]{2,1,0:T(8,128)(2,1)S(1)}, u32[]{:S(2)}, u32[]{:S(2)}) collective-permute-start(bf16[1,128,1024]{2,1,0:T(8,128)(2,1)} %get-tuple-element.21), channel_id=1, source_target_pairs={{0,3},{3,0},{4,7},{7,4},{8,11},{11,8},{12,15},{15,12},{16,19},{19,... | collective-permute-start | bytes 786440 | tf_op jit(solution)/shard_map/ppermute | solution.py:431
  86.2 0.7 copy-start.5
  86.9 27.2 %collective-permute-start.2 = (bf16[1,128,1024]{2,1,0:T(8,128)(2,1)}, bf16[1,128,1024]{2,1,0:T(8,128)(2,1)S(1)}, u32[]{:S(2)}, u32[]{:S(2)}) collective-permute-start(bf16[1,128,1024]{2,1,0:T(8,128)(2,1)} %get-tuple-element.21), channel_id=1, source_target_pairs={{1,2},{2,1},{5,6},{6,5},{9,10},{10,9},{13,14},{14,13},{17,18},{18,... | collective-permute-start | bytes 786440 | tf_op jit(solution)/shard_map/ppermute | solution.py:431
  87.6 23.7 %collective-permute-start.9 = (bf16[1,128,1024]{2,1,0:T(8,128)(2,1)}, bf16[1,128,1024]{2,1,0:T(8,128)(2,1)}, u32[]{:S(2)}, u32[]{:S(2)}) collective-permute-start(bf16[1,128,1024]{2,1,0:T(8,128)(2,1)} %get-tuple-element.27), channel_id=1, source_target_pairs={{0,1},{1,0},{2,3},{3,2},{4,5},{5,4},{6,7},{7,6},{8,9},{9,8},{10,11... | collective-permute-start | bytes 786440 | tf_op jit(solution)/shard_map/ppermute | solution.py:431
  99.1 15.5 %collective-permute-start.3 = (bf16[1,128,1024]{2,1,0:T(8,128)(2,1)}, bf16[1,128,1024]{2,1,0:T(8,128)(2,1)S(1)}, u32[]{:S(2)}, u32[]{:S(2)}) collective-permute-start(bf16[1,128,1024]{2,1,0:T(8,128)(2,1)} %get-tuple-element.22), channel_id=1, source_target_pairs={{1,3},{2,0},{5,7},{6,4},{9,11},{10,8},{13,15},{14,12},{17,19},{18,... | collective-permute-start | bytes 786440 | tf_op jit(solution)/shard_map/ppermute | solution.py:431
  100.4 14.2 %collective-permute-start.4 = (bf16[1,128,1024]{2,1,0:T(8,128)(2,1)}, bf16[1,128,1024]{2,1,0:T(8,128)(2,1)S(1)}, u32[]{:S(2)}, u32[]{:S(2)}) collective-permute-start(bf16[1,128,1024]{2,1,0:T(8,128)(2,1)} %get-tuple-element.22), channel_id=1, source_target_pairs={{0,2},{3,1},{4,6},{7,5},{8,10},{11,9},{12,14},{15,13},{16,18},{19,... | collective-permute-start | bytes 786440 | tf_op jit(solution)/shard_map/ppermute | solution.py:431
  107.2 1.0 copy-start.2
  108.1 0.9 copy-start.4
  109.1 2.2 %copy-start.6 = (bf16[1,128,1024]{2,1,0:T(8,128)(2,1)S(1)}, bf16[1,128,1024]{2,1,0:T(8,128)(2,1)}, u32[]{:S(2)}) copy-start(bf16[1,128,1024]{2,1,0:T(8,128)(2,1)} %copy-done.5) | copy-start | bytes 786436

commit v6 on v5

--- a/solution.py
+++ b/solution.py
@@ -72,15 +72,14 @@
     return rank if n_tp % 2 else rank // 2 + rank % 2 * (n_tp // 2)
 
 
-def user_of(place, spread, per_row, n_tp):
-    unit = place // spread
-    row, k = unit // per_row, unit % per_row
+def user_of(place, group, per_row, n_tp):
+    row, c = place // group, place % group
     rank = row if n_tp % 2 else row % (n_tp // 2) * 2 + row // (n_tp // 2)
-    return k * n_tp + rank
-
-
-def place_of(user, spread, per_row, n_tp):
-    return (row_of(user, n_tp) * per_row + user // n_tp) * spread
+    return c % per_row * n_tp + rank, c // per_row
+
+
+def place_of(user, slot, group, per_row, n_tp):
+    return row_of(user, n_tp) * group + slot * per_row + user // n_tp
 
 
 def first_kernel(wanted, pieces, codes_ref, g_ref, m_ref, *refs):
@@ -175,8 +174,8 @@
             def _():
                 pltpu.make_async_copy(y_buf.at[i], out.at[i - start], y_sem.at[i]).start()
 
-        to = user_of(place[i], spread, per_row, n_tp)
-        at = pl.multiple_of(place[i] % spread * half, half)
+        to, slot = user_of(place[i], blocks // n_tp, per_row, n_tp)
+        at = pl.multiple_of(slot * half, half)
         parts_ref[to, pl.ds(at, half)] = pack(gram)
         diagonal = diagonal_of(gram)
         for f in range(parts_ref.shape[0]):
@@ -210,7 +209,43 @@
     )(source, place, grads, momentum)
 
 
-def solve_kernel(spread, count, elements, owners, codes, parts_ref, out_ref, slot_ref, sum_ref):
+def iterate(work):
+    def dot(a, b):
+        return jnp.dot(a, b, precision=lax.Precision.HIGHEST, preferred_element_type=jnp.float32)
+
+    head = work[0][0].shape[1]
+    rows, columns = iotas((head, head))
+    identity = jnp.where(rows == columns, 1.0, 0.0)
+    inverses = [1.0 / (jnp.sqrt(jnp.sum(d, axis=1, keepdims=True)) + epsilon) for _, d in work]
+    grams = [unpack(p, d) * (inv * inv) for (p, d), inv in zip(work, inverses)]
+    turned = [None] * len(work)
+    for i in range(ITERS):
+        last = i + 1 == ITERS
+        squared = [dot(g, g) for g in grams]
+        mixed = [poly_linear * identity + poly_cubic * g + poly_quintic * s for g, s in zip(grams, squared)]
+        right = [None if last else dot(g, m) for g, m in zip(grams, mixed)]
+        turned = [m if q is None else dot(m, q) for q, m in zip(turned, mixed)]
+        grams = [None if last else dot(m, r) for m, r in zip(mixed, right)]
+    turned = [q * inv for q, inv in zip(turned, inverses)]
+    return [(pack(q), diagonal_of(q)) for q in turned]
+
+
+def write_packed(ref, solved):
+    head = ref.shape[1]
+    half, count = head // 2, len(solved)
+    for k, (packed, diagonal) in enumerate(solved):
+        ref[k * half : (k + 1) * half] = packed
+        ref[count * half + k : count * half + k + 1] = diagonal
+    used = count * half + count
+    ref[used:] = jnp.zeros((ref.shape[0] - used, head), jnp.float32)
+
+
+def packed_rows(count, head):
+    return count * head // 2 + 8 * -(-count // 8)
+
+
+def solve_kernel(spread, skip, count, elements, owners, codes, parts_ref, *refs):
+    slot_ref, sum_ref = refs[-2:]
     n_fsdp, _, head = parts_ref.shape
     half = head // 2
     here = lax.axis_index("fsdp")
@@ -233,55 +268,91 @@
         taken = taken + mine.astype(jnp.int32)
     slot_ref[...] = slots
 
-    def dot(a, b):
-        return jnp.dot(a, b, precision=lax.Precision.HIGHEST, preferred_element_type=jnp.float32)
-
-    eye_rows, eye_columns = iotas((head, head))
-    identity = jnp.where(eye_rows == eye_columns, 1.0, 0.0)
     work = []
     for k in range(spread):
-        at = jnp.minimum(place_of(here, spread, per_row, n_tp) + k, count - 1)
-        diagonal = sum_ref[pl.ds(at, 1)]
-        inverse = 1.0 / (jnp.sqrt(jnp.sum(diagonal, axis=1, keepdims=True)) + epsilon)
-        gram = unpack(total[k * half : (k + 1) * half], diagonal) * (inverse * inverse)
-        work.append((inverse, gram, None))
-    for i in range(ITERS):
-        last = i + 1 == ITERS
-        squared = [dot(gram, gram) for _, gram, _ in work]
-        mixed = [
-            poly_linear * identity + poly_cubic * gram + poly_quintic * s
-            for (_, gram, _), s in zip(work, squared)
-        ]
-        right = [None if last else dot(gram, m) for (_, gram, _), m in zip(work, mixed)]
-        turned = [m if q is None else dot(m, q) for (_, _, q), m in zip(work, mixed)]
-        grams = [None if last else dot(m, r) for m, r in zip(mixed, right)]
-        work = [(inverse, gram, q) for (inverse, _, _), gram, q in zip(work, grams, turned)]
-    for k, (inverse, _, q) in enumerate(work):
-        q = q * inverse
-        out_ref[k * half : (k + 1) * half] = pack(q)
-        out_ref[spread * half + k : spread * half + k + 1] = diagonal_of(q)
-    rest = out_ref.shape[0] - spread * half - spread
-    out_ref[spread * half + spread :] = jnp.zeros((rest, head), jnp.float32)
-
-
-def solve(parts, owners, codes, spread, elements):
+        at = jnp.minimum(place_of(here, k, spread * per_row, per_row, n_tp), count - 1)
+        work.append((total[k * half : (k + 1) * half], sum_ref[pl.ds(at, 1)]))
+    solved = iterate(work)
+    write_packed(refs[0], solved)
+    if skip:
+        write_packed(refs[1], solved[skip:])
+
+
+def solve(parts, owners, codes, spread, skip, elements):
     _, _, head = parts.shape
     count = codes.shape[1]
-    return pl.pallas_call(
-        functools.partial(solve_kernel, spread, count, elements),
-        out_shape=[
-            jax.ShapeDtypeStruct((spread * head // 2 + 8 * -(-spread // 8), head), jnp.float32),
-            jax.ShapeDtypeStruct((1, head), jnp.float32),
-        ],
+    outs = [packed_rows(spread, head)] + ([packed_rows(spread - skip, head)] if skip else [])
+    return pl.pallas_call(
+        functools.partial(solve_kernel, spread, skip, count, elements),
+        out_shape=[jax.ShapeDtypeStruct((n, head), jnp.float32) for n in outs + [1]],
         in_specs=[SMEM, SMEM, VMEM],
-        out_specs=[VMEM, VMEM],
+        out_specs=[VMEM] * (len(outs) + 1),
         scratch_shapes=[pltpu.VMEM((2 * count, head), jnp.float32)],
         compiler_params=params(4 * parts.size * 4),
         name="solve",
     )(owners, codes, parts)
 
 
-def unpack_kernel(spread, packed_ref, out_ref):
+def far_kernel(members, per_row, *refs):
+    parts_ref = refs[-1]
+    head = parts_ref.shape[2]
+    half = head // 2
+    row = lax.axis_index("tp")
+    parts_ref[...] = jnp.zeros(parts_ref.shape, jnp.float32)
+    for (source_row, c), ref in zip(members, refs):
+        y = ref[0]
+        gram = lax.dot_general(y, y, (((1,), (1,)), ((), ())), preferred_element_type=jnp.float32)
+        to = source_row(row) * per_row + c
+        parts_ref[to, :half] = pack(gram)
+        parts_ref[to, half : half + 1] = diagonal_of(gram)
+
+
+def far_parts(arrays, members, per_row, devices):
+    head = arrays[0].shape[1]
+    return pl.pallas_call(
+        functools.partial(far_kernel, members, per_row),
+        out_shape=pltpu.VMEM((devices, packed_rows(1, head), head), jnp.float32),
+        in_specs=[VMEM] * len(arrays),
+        out_specs=VMEM,
+        compiler_params=params(8 * devices * packed_rows(1, head) * head * 4),
+        name="far_parts",
+    )(*arrays)
+
+
+def finish_kernel(spread, per_row, parts_ref, same_ref, cross_ref, out_ref):
+    n_fsdp, _, head = parts_ref.shape
+    half = head // 2
+    middle = lax.axis_size("tp") // 2
+    source_row = lax.axis_index("fsdp") // per_row
+    crossed = (source_row >= middle) != (lax.axis_index("tp") >= middle)
+    total = parts_ref[0]
+    for f in range(1, n_fsdp):
+        total = total + parts_ref[f]
+    solved = iterate([(total[:half], total[half : half + 1])])
+    sent = spread - 1
+    for k in range(sent):
+        diagonal = cross_ref[sent * half + k : sent * half + k + 1]
+        solved.append((cross_ref[k * half : (k + 1) * half], diagonal))
+    chosen = []
+    for k, (packed, diagonal) in enumerate(solved):
+        other = same_ref[k * half : (k + 1) * half]
+        other_diagonal = same_ref[spread * half + k : spread * half + k + 1]
+        chosen.append((jnp.where(crossed, packed, other), jnp.where(crossed, diagonal, other_diagonal)))
+    write_packed(out_ref, chosen)
+
+
+def finish(parts, same, cross, spread, per_row):
+    return pl.pallas_call(
+        functools.partial(finish_kernel, spread, per_row),
+        out_shape=jax.ShapeDtypeStruct(same.shape, jnp.float32),
+        in_specs=[VMEM] * 3,
+        out_specs=VMEM,
+        compiler_params=params(8 * parts.size * 4),
+        name="finish",
+    )(parts, same, cross)
+
+
+def unpack_kernel(spread, per_row, packed_ref, out_ref):
     head = packed_ref.shape[2]
     half = head // 2
 
@@ -291,15 +362,16 @@
             packed = packed_ref[f, k * half : (k + 1) * half]
             q = unpack(packed, packed_ref[f, spread * half + k : spread * half + k + 1])
             high = q.astype(jnp.bfloat16)
-            out_ref[f * spread + k, :head] = high
-            out_ref[f * spread + k, head:] = (q - high.astype(jnp.float32)).astype(jnp.bfloat16)
-
-
-def unpack_all(packed, spread, blocks):
+            place = (f // per_row * spread + k) * per_row + f % per_row
+            out_ref[place, :, :head] = high
+            out_ref[place, :, head:] = (q - high.astype(jnp.float32)).astype(jnp.bfloat16)
+
+
+def unpack_all(packed, spread, per_row, blocks):
     head = packed.shape[2]
     return pl.pallas_call(
-        functools.partial(unpack_kernel, spread),
-        out_shape=jax.ShapeDtypeStruct((blocks, 2 * head, head), jnp.bfloat16),
+        functools.partial(unpack_kernel, spread, per_row),
+        out_shape=jax.ShapeDtypeStruct((blocks, head, 2 * head), jnp.bfloat16),
         in_specs=[VMEM],
         out_specs=VMEM,
         compiler_params=params(4 * packed.size * 4),
@@ -310,7 +382,6 @@
 def apply_kernel(factor, members, at_end, tiles, q_ref, *refs):
     out = refs[-3]
     u_buf, u_sem = refs[-2:]
-    head = u_buf.shape[1]
     width = u_buf.shape[2] // tiles
     row = lax.axis_index("tp")
 
@@ -326,8 +397,8 @@
             y = refs[ways[0]][k, :, part]
             if len(ways) > 1:
                 y = jnp.where(at_end(row), y, refs[ways[1]][k, :, part])
+            y = jnp.concatenate([y, y], axis=0)
             ortho = jnp.dot(q, y, preferred_element_type=jnp.float32)
-            ortho = ortho[:head] + ortho[head:]
             ortho = ortho.astype(jnp.bfloat16).astype(jnp.float32)
             u_buf[i, :, part] = (-factor * ortho).astype(jnp.bfloat16)
             u_copy(i, j).start()
@@ -389,8 +460,7 @@
         return [(x, (c,)) for c in places for x in partners]
 
     first = singles(far, range(1))
-    middle = [chunk for c in range(1, cut) for chunk in singles(near, [c - 1]) + singles(far, [c])]
-    early = first + middle
+    early = first + singles(far, range(1, cut)) + singles(near, range(cut - 1))
     late = singles(near, range(cut - 1, cut))
     for c in range(cut, group - 1):
         late += singles(far, [c]) + singles(near, [c])
@@ -444,18 +514,29 @@
         send(chunk, side, ys[chunk])
 
     parts = lax.all_to_all(parts, "fsdp", split_axis=0, concat_axis=0, tiled=True)
-    packed, slots = solve(parts, owner_table, pool_map, spread, head * width * n_fsdp)
-
     per_row = group // spread
-    pairs = []
+    skip = 1 if paired and spread > 1 else 0
+    *packed, slots = solve(parts, owner_table, pool_map, spread, skip, head * width * n_fsdp)
+    same_pairs, cross_pairs = [], []
     for f in range(blocks // spread):
         for t in range(n_tp):
-            to = (t * per_row + f // n_tp) * n_tp + row_of(f, n_tp)
-            pairs.append((f * n_tp + t, to))
-    packed = lax.ppermute(packed, ("fsdp", "tp"), pairs)
+            row_to = row_of(f, n_tp)
+            pair = (f * n_tp + t, (t * per_row + f // n_tp) * n_tp + row_to)
+            crosses = skip and (t < n_tp // 2) != (row_to < n_tp // 2)
+            (cross_pairs if crosses else same_pairs).append(pair)
+    if skip:
+        cross = lax.ppermute(packed[1], ("fsdp", "tp"), cross_pairs)
+    packed = lax.ppermute(packed[0], ("fsdp", "tp"), same_pairs)
+    if skip:
+        arrived = singles(far, range(per_row))
+        members = [(functools.partial(sender, x=x), cs[0]) for x, cs in arrived]
+        parts = far_parts([got[chunk, None] for chunk in arrived], members, per_row, n_fsdp)
+        parts, packed, cross = lax.optimization_barrier((parts, packed, cross))
+        parts = lax.all_to_all(parts, "fsdp", split_axis=0, concat_axis=0, tiled=True)
+        packed = finish(parts, packed, cross, spread, per_row)
     packed = jnp.broadcast_to(packed[None], (n_fsdp,) + packed.shape)
     packed = lax.all_to_all(packed, "fsdp", split_axis=0, concat_axis=0, tiled=True)
-    transforms = unpack_all(packed, spread, blocks)
+    transforms = unpack_all(packed, spread, per_row, blocks)
 
     factor = step_size * 0.2 * math.sqrt(width * n_fsdp)
     for chunk in own:

time: 116 us -> 128 us (1.10)
  waiting for transfers between devices: 19.1 us -> 48.3 us
  starting transfers between devices: 64.2 us -> 44.3 us
  Pallas kernels: 24.5 us -> 28 us
  local copies, waits for them, and re-layouts: 5.17 us -> 3.38 us
    ppermute x14, waiting for transfers between devices: 17.7 us -> 47.5 us  [send(): got[chunk, side] = lax.ppermute(array, 'tp', pairs)]
    ppermute x14, starting transfers between devices: 52.4 us -> 30.4 us  [send(): got[chunk, side] = lax.ppermute(array, 'tp', pairs)]
    all_to_all x1 -> x2, starting transfers between devices: 5.21 us -> 9.02 us  [local(): lax.all_to_all(parts, 'fsdp', split_axis=0, concat_axis=0, tiled=True)]
    pallas_call x2 -> x4, Pallas kernels: 4.83 us -> 7.38 us  [the longest x1 2.92 us: solve(): pl.pallas_call(functools.partial(solve_kernel, spread, skip, count, eleme...]
    unnamed x21 -> x17, local copies, waits for them, and re-layouts: 3.41 us -> 2.52 us
  transfers between devices with their start and end apart: 17 -> 19, of which waited for: 5 -> 7; matrix products, arithmetic and copies ran while one was open for 2% -> 1% of each run, Pallas kernels for 12% -> 13%
where the time goes in v6:
time: 128 us; the launch traced here: 127 us
  waiting for transfers between devices  48.3 us (38%)
  starting transfers between devices  44.3 us (35%)
  Pallas kernels  28 us (22%)
  local copies, waits for them, and re-layouts  3.38 us (3%)
  other arithmetic  2.03 us (2%)
    ppermute x14, waiting for transfers between devices, send(): got[chunk, side] = lax.ppermute(array, 'tp', pairs)  47.5 us
    ppermute x14, starting transfers between devices, send(): got[chunk, side] = lax.ppermute(array, 'tp', pairs)  30.4 us
    pallas_call x1, Pallas kernels, all_blocks(): pl.pallas_call(functools.partial(all_kernel, spans, spread, min(width, 25...  9.93 us
    all_to_all x2, starting transfers between devices, local(): lax.all_to_all(parts, 'fsdp', split_axis=0, concat_axis=0, tiled=True)  9.02 us
    pallas_call x3, Pallas kernels, apply_blocks(): pl.pallas_call(functools.partial(apply_kernel, factor, members, at_end, t...  6.35 us
    pallas_call x2, Pallas kernels, first_blocks(): pl.pallas_call(functools.partial(first_kernel, wanted, pieces), out_shape...  4.37 us
    all_to_all x1, starting transfers between devices, local(): lax.all_to_all(packed, 'fsdp', split_axis=0, concat_axis=0, tiled=True)  3.54 us
    pallas_call x1, Pallas kernels, solve(): pl.pallas_call(functools.partial(solve_kernel, spread, skip, count, eleme...  2.92 us
  transfers between devices with their start and end apart: 19, of which 7 were waited for; matrix products, arithmetic and copies ran while one was open for 1% of the time, Pallas kernels for 13%

profile of v6, /device:TPU:0, one launch (start us, length us, event | category | flops | bytes accessed | tf_op | source)
XLA Modules:
  0.0 126.9 jit_solution(5144349505123451882)
XLA Ops:
  0.6 0.7 multiply_add_fusion.place
  1.3 1.3 %select_reduce_fusion.source = s32[16]{0:T(128)} fusion(s32[16]{0:T(128)} %bitcast.2, s32[16]{0:T(128)S(1)} %multiply_add_fusion.place), kind=kLoop, calls=%fused_computation | loop fusion | flops 752 | bytes 192 | tf_op jit(solution)/shard_map/reduce_sum | solution.py:479
  2.7 9.9 %all_blocks.1 = (bf16[16,128,1024]{2,1,0:T(8,128)(2,1)}, f32[8,144,128]{2,1,0:T(8,128)}, bf16[1,128,1024]{2,1,0:T(8,128)(2,1)}, bf16[1,128,1024]{2,1,0:T(8,128)(...) custom-call(s32[16]{0:T(128)} %select_reduce_fusion.source, ...), custom_call_target="tpu_custom_call" | custom-call | tf_op jit(solution)/shard_map/all_blocks/pallas_call | solution.py:197
  12.6 5.2 %all-to-all-start = ((f32[8,144,128]{2,1,0:T(8,128)}), f32[8,144,128]{2,1,0:T(8,128)S(1)}, u32[]{:S(2)}, u32[]{:S(2)}) async-start(f32[8,144,128]{2,1,0:T(8,128)} %get-tuple-element.25), calls=%async_computation | async-start | bytes 1179648 | tf_op jit(solution)/shard_map/all_to_all | solution.py:516
  17.8 3.6 %collective-permute-start.2 = (bf16[1,128,1024]{2,1,0:T(8,128)(2,1)}, bf16[1,128,1024]{2,1,0:T(8,128)(2,1)S(1)}, u32[]{:S(2)}, u32[]{:S(2)}) collective-permute-start(bf16[1,128,1024]{2,1,0:T(8,128)(2,1)} %get-tuple-element.23), channel_id=1, source_target_pairs={{0,3},{1,2},{2,1},{3,0},{4,7},{5,6},{6,5},{7,4},{8,11},{9,10},{10,... | collective-permute-start | bytes 786440 | tf_op jit(solution)/shard_map/ppermute | solution.py:501
  21.4 2.5 %shard_map.85 = bf16[1,128,1024]{2,1,0:T(8,128)(2,1)} custom-call(s32[1,16]{1,0:T(1,128)} %codes.1, bf16[16,128,1024]{2,1,0:T(8,128)(2,1)} %g_ref.5, bf16[16,128,1024]{2,1,0:T(8,128)(2,1)} %m_ref.5), custom_call_target="tpu_custom_call" | custom-call | tf_op jit(solution)/shard_map/pallas_call | solution.py:121
  24.0 0.0 copy-start.7
  24.0 0.0 copy-start.5
  24.0 2.0 %collective-permute-start = (bf16[1,128,1024]{2,1,0:T(8,128)(2,1)}, bf16[1,128,1024]{2,1,0:T(8,128)(2,1)S(1)}, u32[]{:S(2)}, u32[]{:S(2)}) collective-permute-start(bf16[1,128,1024]{2,1,0:T(8,128)(2,1)} %shard_map.85), channel_id=1, source_target_pairs={{0,3},{1,2},{2,1},{3,0},{4,7},{5,6},{6,5},{7,4},{8,11},{9,10},{10,... | collective-permute-start | bytes 786440 | tf_op jit(solution)/shard_map/ppermute | solution.py:501
  26.0 1.8 %shard_map.86 = bf16[1,128,1024]{2,1,0:T(8,128)(2,1)S(1)} custom-call(s32[1,16]{1,0:T(1,128)} %codes.1, bf16[16,128,1024]{2,1,0:T(8,128)(2,1)} %g_ref.5, bf16[16,128,1024]{2,1,0:T(8,128)(2,1)} %m_ref.5), custom_call_target="tpu_custom_call" | custom-call | tf_op jit(solution)/shard_map/pallas_call | solution.py:121
  27.8 0.0 copy-start
  27.8 1.1 collective-permute-start.1
  28.9 0.1 copy.12.owners
  29.0 2.9 %solve.1 = (f32[136,128]{1,0:T(8,128)S(1)}, f32[72,128]{1,0:T(8,128)S(1)}, f32[1,128]{1,0:T(1,128)}) custom-call(s32[16,1]{1,0:T(8,128)S(1)} %copy.12.owners, s32[1,16]{1,0:T(1,128)S(1)} %copy-done.5, f32[8,144,128]{2,1,0:T(8,128)S(1)} %all-to-all-done.parts_ref), custom_call_target="tpu_custom_call" | custom-call | tf_op jit(solution)/shard_map/solve/pallas_call | solution.py:285
  31.9 0.7 collective-permute-start.4
  32.6 0.0 collective-permute-done.2.refs_2_.refs_3_
  32.6 0.7 collective-permute-start.5
  33.3 23.4 %collective-permute-done.3.refs_3_.refs_4_ = bf16[1,128,1024]{2,1,0:T(8,128)(2,1)S(1)} collective-permute-done((bf16[1,128,1024]{2,1,0:T(8,128)(2,1)}, bf16[1,128,1024]{2,1,0:T(8,128)(2,1)S(1)}, u32[]{:S(2)}, u32[]{:S(2)}) %collective-permute-start.3) | collective-permute-done | bytes 262176 | tf_op jit(solution)/shard_map/ppermute | solution.py:501
  56.7 10.8 %collective-permute-done.1.refs_1_.refs_2_ = bf16[1,128,1024]{2,1,0:T(8,128)(2,1)S(1)} collective-permute-done((bf16[1,128,1024]{2,1,0:T(8,128)(2,1)S(1)}, bf16[1,128,1024]{2,1,0:T(8,128)(2,1)S(1)}, u32[]{:S(2)}, u32[]{:S(2)}) %collective-permute-start.1) | collective-permute-done | bytes 262176 | tf_op jit(solution)/shard_map/ppermute | solution.py:501
  67.5 1.2 far_parts.1
  68.7 0.0 collective-permute-done.5.cross_ref
  68.7 0.0 collective-permute-done.4.same_ref
  68.7 3.8 %all-to-all-start.1 = ((f32[8,72,128]{2,1,0:T(8,128)}), f32[8,72,128]{2,1,0:T(8,128)S(1)}, u32[]{:S(2)}, u32[]{:S(2)}) async-start(f32[8,72,128]{2,1,0:T(8,128)} %far_parts.1), calls=%async_computation.1 | async-start | bytes 589824 | tf_op jit(solution)/shard_map/all_to_all | solution.py:535
  72.5 0.1 collective-permute-start.15
  72.6 2.0 %collective-permute-start.10 = (bf16[1,128,1024]{2,1,0:T(8,128)(2,1)}, bf16[1,128,1024]{2,1,0:T(8,128)(2,1)S(1)}, u32[]{:S(2)}, u32[]{:S(2)}) collective-permute-start(bf16[1,128,1024]{2,1,0:T(8,128)(2,1)} %get-tuple-element.33), channel_id=1, source_target_pairs={{0,1},{1,0},{2,3},{3,2},{4,5},{5,4},{6,7},{7,6},{8,9},{9,8},{10,11... | collective-permute-start | bytes 786440 | tf_op jit(solution)/shard_map/ppermute | solution.py:501
  74.5 2.9 %collective-permute-start.11 = (bf16[1,128,1024]{2,1,0:T(8,128)(2,1)}, bf16[1,128,1024]{2,1,0:T(8,128)(2,1)}, u32[]{:S(2)}, u32[]{:S(2)}) collective-permute-start(bf16[1,128,1024]{2,1,0:T(8,128)(2,1)} %get-tuple-element.34), channel_id=1, source_target_pairs={{0,3},{1,2},{2,1},{3,0},{4,7},{5,6},{6,5},{7,4},{8,11},{9,10},{10,... | collective-permute-start | bytes 786440 | tf_op jit(solution)/shard_map/ppermute | solution.py:501
  77.4 1.5 %collective-permute-start.13 = (bf16[1,128,1024]{2,1,0:T(8,128)(2,1)}, bf16[1,128,1024]{2,1,0:T(8,128)(2,1)}, u32[]{:S(2)}, u32[]{:S(2)}) collective-permute-start(bf16[1,128,1024]{2,1,0:T(8,128)(2,1)} %get-tuple-element.36), channel_id=1, source_target_pairs={{0,1},{1,0},{2,3},{3,2},{4,5},{5,4},{6,7},{7,6},{8,9},{9,8},{10,11... | collective-permute-start | bytes 786440 | tf_op jit(solution)/shard_map/ppermute | solution.py:501
  78.9 0.8 all-to-all-done.1.parts_ref
  79.8 2.0 %finish.1 = f32[136,128]{1,0:T(8,128)S(1)} custom-call(f32[8,72,128]{2,1,0:T(8,128)S(1)} %all-to-all-done.1.parts_ref, f32[136,128]{1,0:T(8,128)S(1)} %collective-permute-done.4.same_ref, f32[72,128]{1,0:T(8,128)S(1)} %collective-permute-done.5.cross_ref), custom_call_target="tpu_custom_call" | custom-call | tf_op jit(solution)/shard_map/finish/pallas_call | solution.py:345
  81.7 0.9 broadcast_in_dim.22
  82.6 3.5 %all-to-all-start.2 = ((f32[8,136,128]{2,1,0:T(8,128)}), f32[8,136,128]{2,1,0:T(8,128)S(1)}, u32[]{:S(2)}, u32[]{:S(2)}) async-start(f32[8,136,128]{2,1,0:T(8,128)} %broadcast_in_dim.22), calls=%async_computation.2 | async-start | bytes 1114112 | tf_op jit(solution)/shard_map/all_to_all | solution.py:538
  86.1 0.0 collective-permute-done.15.refs_5_
  86.2 0.7 copy-done.3
  86.9 4.8 %collective-permute-start.6 = (bf16[1,128,1024]{2,1,0:T(8,128)(2,1)}, bf16[1,128,1024]{2,1,0:T(8,128)(2,1)S(1)}, u32[]{:S(2)}, u32[]{:S(2)}) collective-permute-start(bf16[1,128,1024]{2,1,0:T(8,128)(2,1)} %get-tuple-element.31), channel_id=1, source_target_pairs={{0,3},{3,0},{4,7},{7,4},{8,11},{11,8},{12,15},{15,12},{16,19},{19,... | collective-permute-start | bytes 786440 | tf_op jit(solution)/shard_map/ppermute | solution.py:501
  91.7 6.9 %collective-permute-done.10.refs_0_ = bf16[1,128,1024]{2,1,0:T(8,128)(2,1)S(1)} collective-permute-done((bf16[1,128,1024]{2,1,0:T(8,128)(2,1)}, bf16[1,128,1024]{2,1,0:T(8,128)(2,1)S(1)}, u32[]{:S(2)}, u32[]{:S(2)}) %collective-permute-start.10) | collective-permute-done | bytes 262176 | tf_op jit(solution)/shard_map/ppermute | solution.py:501
  98.5 0.7 copy-done.1
  99.2 0.7 collective-permute-start.7
  99.9 1.2 collective-permute-start.14
  101.1 1.3 %collective-permute-start.8 = (bf16[1,128,1024]{2,1,0:T(8,128)(2,1)}, bf16[1,128,1024]{2,1,0:T(8,128)(2,1)}, u32[]{:S(2)}, u32[]{:S(2)}) collective-permute-start(bf16[1,128,1024]{2,1,0:T(8,128)(2,1)} %get-tuple-element.32), channel_id=1, source_target_pairs={{1,3},{2,0},{5,7},{6,4},{9,11},{10,8},{13,15},{14,12},{17,19},{18,... | collective-permute-start | bytes 786440 | tf_op jit(solution)/shard_map/ppermute | solution.py:501
  102.4 2.1 %collective-permute-done.13.refs_3_ = bf16[1,128,1024]{2,1,0:T(8,128)(2,1)} collective-permute-done((bf16[1,128,1024]{2,1,0:T(8,128)(2,1)}, bf16[1,128,1024]{2,1,0:T(8,128)(2,1)}, u32[]{:S(2)}, u32[]{:S(2)}) %collective-permute-start.13) | collective-permute-done | bytes 262176 | tf_op jit(solution)/shard_map/ppermute | solution.py:501
  104.5 9.3 %collective-permute-start.9 = (bf16[1,128,1024]{2,1,0:T(8,128)(2,1)}, bf16[1,128,1024]{2,1,0:T(8,128)(2,1)}, u32[]{:S(2)}, u32[]{:S(2)}) collective-permute-start(bf16[1,128,1024]{2,1,0:T(8,128)(2,1)} %get-tuple-element.32), channel_id=1, source_target_pairs={{0,2},{3,1},{4,6},{7,5},{8,10},{11,9},{12,14},{15,13},{16,18},{19,... | collective-permute-start | bytes 786440 | tf_op jit(solution)/shard_map/ppermute | solution.py:501
  113.8 1.3 %unpack_all.1.q_ref = bf16[16,128,256]{2,1,0:T(8,128)(2,1)S(1)} custom-call(f32[8,136,128]{2,1,0:T(8,128)S(1)} %all-to-all-done.2.packed_ref), custom_call_target="tpu_custom_call" | custom-call | tf_op jit(solution)/shard_map/unpack_all/pallas_call | solution.py:372
  115.2 1.0 copy-done.4
  116.1 1.7 %apply_blocks.3.refs_5_ = bf16[16,128,1024]{2,1,0:T(8,128)(2,1)} custom-call(bf16[16,128,256]{2,1,0:T(8,128)(2,1)S(1)} %unpack_all.1.q_ref, bf16[4,128,1024]{2,1,0:T(8,128)(2,1)S(1)} %copy-done, bf16[1,128,1024]{2,1,0:T(8,128)(2,1)S(1)} %collective-permute-done.refs_0_.refs_1_, bf16[1,128,1024]{2,1,0:T(8,128)(2,1)S(1)} %collective-permute-done.1.refs_1_.refs_2_, ...), custom_call_target="tpu_custom_call" | custom-call | tf_op jit(solution)/shard_map/apply_blocks/pallas_call | solution.py:426
  117.9 0.3 collective-permute-done.14.refs_4_
  118.2 2.5 %apply_blocks.4.refs_4_ = bf16[16,128,1024]{2,1,0:T(8,128)(2,1)} custom-call(bf16[16,128,256]{2,1,0:T(8,128)(2,1)S(1)} %unpack_all.1.q_ref, bf16[1,128,1024]{2,1,0:T(8,128)(2,1)S(1)} %copy-done.2, bf16[1,128,1024]{2,1,0:T(8,128)(2,1)} %collective-permute-done.11.refs_1_, ...), custom_call_target="tpu_custom_call", output_to_operand_aliasing={{}: (6, {})} | custom-call | tf_op jit(solution)/shard_map/apply_blocks/pallas_call | solution.py:426
  120.7 4.1 %collective-permute-done.8.refs_2_ = bf16[1,128,1024]{2,1,0:T(8,128)(2,1)} collective-permute-done((bf16[1,128,1024]{2,1,0:T(8,128)(2,1)}, bf16[1,128,1024]{2,1,0:T(8,128)(2,1)}, u32[]{:S(2)}, u32[]{:S(2)}) %collective-permute-start.8) | collective-permute-done | bytes 262176 | tf_op jit(solution)/shard_map/ppermute | solution.py:501
  124.8 2.1 %apply_blocks.5 = bf16[16,128,1024]{2,1,0:T(8,128)(2,1)} custom-call(bf16[16,128,256]{2,1,0:T(8,128)(2,1)S(1)} %unpack_all.1.q_ref, bf16[1,128,1024]{2,1,0:T(8,128)(2,1)S(1)} %collective-permute-done.6.refs_0_, bf16[1,128,1024]{2,1,0:T(8,128)(2,1)S(1)} %collective-permute-done.7.refs_1_, ...), custom_call_target="tpu_custom_call", output_to_operand_aliasing={{}: (5, {})} | custom-call | tf_op jit(solution)/shard_map/apply_blocks/pallas_call | solution.py:426
  (20 shorter events, 0.0 us)
Async XLA Ops:
  1.3 1.4 %copy-start.6 = (s32[16]{0:T(128)}, s32[16]{0:T(128)S(1)}, u32[]{:S(2)}) copy-start(s32[16]{0:T(128)S(1)} %multiply_add_fusion.place) | copy-start | bytes 196
  12.6 16.4 %all-to-all-start = ((f32[8,144,128]{2,1,0:T(8,128)}), f32[8,144,128]{2,1,0:T(8,128)S(1)}, u32[]{:S(2)}, u32[]{:S(2)}) async-start(f32[8,144,128]{2,1,0:T(8,128)} %get-tuple-element.25), calls=%async_computation | async-start | bytes 1179648 | tf_op jit(solution)/shard_map/all_to_all | solution.py:516
  17.8 14.8 %collective-permute-start.2 = (bf16[1,128,1024]{2,1,0:T(8,128)(2,1)}, bf16[1,128,1024]{2,1,0:T(8,128)(2,1)S(1)}, u32[]{:S(2)}, u32[]{:S(2)}) collective-permute-start(bf16[1,128,1024]{2,1,0:T(8,128)(2,1)} %get-tuple-element.23), channel_id=1, source_target_pairs={{0,3},{1,2},{2,1},{3,0},{4,7},{5,6},{6,5},{7,4},{8,11},{9,10},{10,... | collective-permute-start | bytes 786440 | tf_op jit(solution)/shard_map/ppermute | solution.py:501
  21.4 35.3 %collective-permute-start.3 = (bf16[1,128,1024]{2,1,0:T(8,128)(2,1)}, bf16[1,128,1024]{2,1,0:T(8,128)(2,1)S(1)}, u32[]{:S(2)}, u32[]{:S(2)}) collective-permute-start(bf16[1,128,1024]{2,1,0:T(8,128)(2,1)} %get-tuple-element.24), channel_id=1, source_target_pairs={{0,2},{1,3},{2,0},{3,1},{4,6},{5,7},{6,4},{7,5},{8,10},{9,11},{10,... | collective-permute-start | bytes 786440 | tf_op jit(solution)/shard_map/ppermute | solution.py:501
  24.0 5.0 %copy-start.7 = (s32[16,1]{0,1:T(1,128)S(1)}, s32[16,1]{0,1:T(1,128)}, u32[]{:S(2)}) copy-start(s32[16,1]{0,1:T(1,128)} %param.8) | copy-start | bytes 196
  24.0 5.0 %copy-start.5 = (s32[1,16]{1,0:T(1,128)S(1)}, s32[1,16]{1,0:T(1,128)}, u32[]{:S(2)}) copy-start(s32[1,16]{1,0:T(1,128)} %codes.1) | copy-start | bytes 196
  24.0 32.7 %collective-permute-start = (bf16[1,128,1024]{2,1,0:T(8,128)(2,1)}, bf16[1,128,1024]{2,1,0:T(8,128)(2,1)S(1)}, u32[]{:S(2)}, u32[]{:S(2)}) collective-permute-start(bf16[1,128,1024]{2,1,0:T(8,128)(2,1)} %shard_map.85), channel_id=1, source_target_pairs={{0,3},{1,2},{2,1},{3,0},{4,7},{5,6},{6,5},{7,4},{8,11},{9,10},{10,... | collective-permute-start | bytes 786440 | tf_op jit(solution)/shard_map/ppermute | solution.py:501
  27.8 87.3 %copy-start = (bf16[4,128,1024]{2,1,0:T(8,128)(2,1)S(1)}, bf16[4,128,1024]{2,1,0:T(8,128)(2,1)}, u32[]{:S(2)}) copy-start(bf16[4,128,1024]{2,1,0:T(8,128)(2,1)} %get-tuple-element.38.refs_0_) | copy-start | bytes 3145732
  27.8 39.7 %collective-permute-start.1 = (bf16[1,128,1024]{2,1,0:T(8,128)(2,1)S(1)}, bf16[1,128,1024]{2,1,0:T(8,128)(2,1)S(1)}, u32[]{:S(2)}, u32[]{:S(2)}) collective-permute-start(bf16[1,128,1024]{2,1,0:T(8,128)(2,1)S(1)} %shard_map.86), channel_id=1, source_target_pairs={{0,2},{1,3},{2,0},{3,1},{4,6},{5,7},{6,4},{7,5},{8,10},{9,11},{10,... | collective-permute-start | bytes 786440 | tf_op jit(solution)/shard_map/ppermute | solution.py:501
  31.9 36.8 %collective-permute-start.4 = (f32[136,128]{1,0:T(8,128)S(1)}, f32[136,128]{1,0:T(8,128)S(1)}, u32[]{:S(2)}, u32[]{:S(2)}) collective-permute-start(f32[136,128]{1,0:T(8,128)S(1)} %get-tuple-element.26), channel_id=1, source_target_pairs={{0,0},{1,8},{6,18},{7,26},{8,1},{9,9},{14,19},{15,27},{16,4},{17,1... | collective-permute-start | bytes 208904 | tf_op jit(solution)/shard_map/ppermute | solution.py:529
  32.6 36.1 %collective-permute-start.5 = (f32[72,128]{1,0:T(8,128)S(1)}, f32[72,128]{1,0:T(8,128)S(1)}, u32[]{:S(2)}, u32[]{:S(2)}) collective-permute-start(f32[72,128]{1,0:T(8,128)S(1)} %get-tuple-element.27), channel_id=1, source_target_pairs={{2,16},{3,24},{4,2},{5,10},{10,17},{11,25},{12,3},{13,11},{18,20},... | collective-permute-start | bytes 110600 | tf_op jit(solution)/shard_map/ppermute | solution.py:528
  68.7 11.1 %all-to-all-start.1 = ((f32[8,72,128]{2,1,0:T(8,128)}), f32[8,72,128]{2,1,0:T(8,128)S(1)}, u32[]{:S(2)}, u32[]{:S(2)}) async-start(f32[8,72,128]{2,1,0:T(8,128)} %far_parts.1), calls=%async_computation.1 | async-start | bytes 589824 | tf_op jit(solution)/shard_map/all_to_all | solution.py:535
  72.5 13.6 %collective-permute-start.15 = (bf16[1,128,1024]{2,1,0:T(8,128)(2,1)}, bf16[1,128,1024]{2,1,0:T(8,128)(2,1)S(1)}, u32[]{:S(2)}, u32[]{:S(2)}) collective-permute-start(bf16[1,128,1024]{2,1,0:T(8,128)(2,1)} %get-tuple-element.39), channel_id=1, source_target_pairs={{0,1},{1,0},{2,3},{3,2},{4,5},{5,4},{6,7},{7,6},{8,9},{9,8},{10,11... | collective-permute-start | bytes 786440 | tf_op jit(solution)/shard_map/ppermute | solution.py:501
  72.6 25.9 %collective-permute-start.10 = (bf16[1,128,1024]{2,1,0:T(8,128)(2,1)}, bf16[1,128,1024]{2,1,0:T(8,128)(2,1)S(1)}, u32[]{:S(2)}, u32[]{:S(2)}) collective-permute-start(bf16[1,128,1024]{2,1,0:T(8,128)(2,1)} %get-tuple-element.33), channel_id=1, source_target_pairs={{0,1},{1,0},{2,3},{3,2},{4,5},{5,4},{6,7},{7,6},{8,9},{9,8},{10,11... | collective-permute-start | bytes 786440 | tf_op jit(solution)/shard_map/ppermute | solution.py:501
  74.5 25.3 %collective-permute-start.11 = (bf16[1,128,1024]{2,1,0:T(8,128)(2,1)}, bf16[1,128,1024]{2,1,0:T(8,128)(2,1)}, u32[]{:S(2)}, u32[]{:S(2)}) collective-permute-start(bf16[1,128,1024]{2,1,0:T(8,128)(2,1)} %get-tuple-element.34), channel_id=1, source_target_pairs={{0,3},{1,2},{2,1},{3,0},{4,7},{5,6},{6,5},{7,4},{8,11},{9,10},{10,... | collective-permute-start | bytes 786440 | tf_op jit(solution)/shard_map/ppermute | solution.py:501
  77.4 23.7 %collective-permute-start.12 = (bf16[1,128,1024]{2,1,0:T(8,128)(2,1)}, bf16[1,128,1024]{2,1,0:T(8,128)(2,1)}, u32[]{:S(2)}, u32[]{:S(2)}) collective-permute-start(bf16[1,128,1024]{2,1,0:T(8,128)(2,1)} %get-tuple-element.35), channel_id=1, source_target_pairs={{0,2},{1,3},{2,0},{3,1},{4,6},{5,7},{6,4},{7,5},{8,10},{9,11},{10,... | collective-permute-start | bytes 786440 | tf_op jit(solution)/shard_map/ppermute | solution.py:501
  77.4 27.1 %collective-permute-start.13 = (bf16[1,128,1024]{2,1,0:T(8,128)(2,1)}, bf16[1,128,1024]{2,1,0:T(8,128)(2,1)}, u32[]{:S(2)}, u32[]{:S(2)}) collective-permute-start(bf16[1,128,1024]{2,1,0:T(8,128)(2,1)} %get-tuple-element.36), channel_id=1, source_target_pairs={{0,1},{1,0},{2,3},{3,2},{4,5},{5,4},{6,7},{7,6},{8,9},{9,8},{10,11... | collective-permute-start | bytes 786440 | tf_op jit(solution)/shard_map/ppermute | solution.py:501
  82.6 31.2 %all-to-all-start.2 = ((f32[8,136,128]{2,1,0:T(8,128)}), f32[8,136,128]{2,1,0:T(8,128)S(1)}, u32[]{:S(2)}, u32[]{:S(2)}) async-start(f32[8,136,128]{2,1,0:T(8,128)} %broadcast_in_dim.22), calls=%async_computation.2 | async-start | bytes 1114112 | tf_op jit(solution)/shard_map/all_to_all | solution.py:538
  86.1 0.7 copy-start.3
  86.9 33.8 %collective-permute-start.6 = (bf16[1,128,1024]{2,1,0:T(8,128)(2,1)}, bf16[1,128,1024]{2,1,0:T(8,128)(2,1)S(1)}, u32[]{:S(2)}, u32[]{:S(2)}) collective-permute-start(bf16[1,128,1024]{2,1,0:T(8,128)(2,1)} %get-tuple-element.31), channel_id=1, source_target_pairs={{0,3},{3,0},{4,7},{7,4},{8,11},{11,8},{12,15},{15,12},{16,19},{19,... | collective-permute-start | bytes 786440 | tf_op jit(solution)/shard_map/ppermute | solution.py:501
  98.5 0.7 copy-start.1
  99.2 21.5 %collective-permute-start.7 = (bf16[1,128,1024]{2,1,0:T(8,128)(2,1)}, bf16[1,128,1024]{2,1,0:T(8,128)(2,1)S(1)}, u32[]{:S(2)}, u32[]{:S(2)}) collective-permute-start(bf16[1,128,1024]{2,1,0:T(8,128)(2,1)} %get-tuple-element.31), channel_id=1, source_target_pairs={{1,2},{2,1},{5,6},{6,5},{9,10},{10,9},{13,14},{14,13},{17,18},{18,... | collective-permute-start | bytes 786440 | tf_op jit(solution)/shard_map/ppermute | solution.py:501
  99.9 18.3 %collective-permute-start.14 = (bf16[1,128,1024]{2,1,0:T(8,128)(2,1)}, bf16[1,128,1024]{2,1,0:T(8,128)(2,1)}, u32[]{:S(2)}, u32[]{:S(2)}) collective-permute-start(bf16[1,128,1024]{2,1,0:T(8,128)(2,1)} %get-tuple-element.37), channel_id=1, source_target_pairs={{0,1},{1,0},{2,3},{3,2},{4,5},{5,4},{6,7},{7,6},{8,9},{9,8},{10,11... | collective-permute-start | bytes 786440 | tf_op jit(solution)/shard_map/ppermute | solution.py:501
  101.1 23.7 %collective-permute-start.8 = (bf16[1,128,1024]{2,1,0:T(8,128)(2,1)}, bf16[1,128,1024]{2,1,0:T(8,128)(2,1)}, u32[]{:S(2)}, u32[]{:S(2)}) collective-permute-start(bf16[1,128,1024]{2,1,0:T(8,128)(2,1)} %get-tuple-element.32), channel_id=1, source_target_pairs={{1,3},{2,0},{5,7},{6,4},{9,11},{10,8},{13,15},{14,12},{17,19},{18,... | collective-permute-start | bytes 786440 | tf_op jit(solution)/shard_map/ppermute | solution.py:501
  104.5 20.3 %collective-permute-start.9 = (bf16[1,128,1024]{2,1,0:T(8,128)(2,1)}, bf16[1,128,1024]{2,1,0:T(8,128)(2,1)}, u32[]{:S(2)}, u32[]{:S(2)}) collective-permute-start(bf16[1,128,1024]{2,1,0:T(8,128)(2,1)} %get-tuple-element.32), channel_id=1, source_target_pairs={{0,2},{3,1},{4,6},{7,5},{8,10},{11,9},{12,14},{15,13},{16,18},{19,... | collective-permute-start | bytes 786440 | tf_op jit(solution)/shard_map/ppermute | solution.py:501
  115.1 3.0 %copy-start.2 = (bf16[1,128,1024]{2,1,0:T(8,128)(2,1)S(1)}, bf16[1,128,1024]{2,1,0:T(8,128)(2,1)}, u32[]{:S(2)}) copy-start(bf16[1,128,1024]{2,1,0:T(8,128)(2,1)} %copy-done.1) | copy-start | bytes 786436
  115.1 1.0 copy-start.4

commit v7 on v6

--- a/solution.py
+++ b/solution.py
@@ -128,9 +128,9 @@
     )(codes, grads, momentum)
 
 
-def all_kernel(spans, spread, tile, source, place, g_ref, m_ref, newm_ref, parts_ref, *refs):
+def all_kernel(wanted, spans, spread, tile, codes, g_ref, m_ref, newm_ref, parts_ref, *refs):
     outs = refs[: len(spans)]
-    g_buf, m_buf, v_buf, y_buf, g_sem, m_sem, v_sem, y_sem = refs[len(spans) :]
+    g_buf, m_buf, v_buf, y_buf, g_sem, m_sem, v_sem, y_sem, at_place, source, place = refs[len(spans) :]
     blocks, head, width = g_buf.shape
     half = head // 2
     users = blocks // spread
@@ -142,6 +142,13 @@
             pltpu.make_async_copy(g_ref.at[source[i]], g_buf.at[i], g_sem.at[i]),
             pltpu.make_async_copy(m_ref.at[source[i]], m_buf.at[i], m_sem.at[i]),
         )
+
+    row = lax.axis_index("tp")
+    for j in range(blocks):
+        at_place[codes[0, j]] = jnp.int32(j)
+    for i, (partner, c) in enumerate(wanted):
+        place[i] = partner(row) * (blocks // n_tp) + c
+        source[i] = at_place[place[i]]
 
     def newm_copy(i):
         return pltpu.make_async_copy(v_buf.at[i], newm_ref.at[source[i]], v_sem.at[i])
@@ -191,22 +198,24 @@
             pltpu.make_async_copy(y_buf.at[i], out.at[k], y_sem.at[i]).wait()
 
 
-def all_blocks(source, place, grads, momentum, spans, spread, devices):
+def all_blocks(codes, grads, momentum, wanted, spans, spread, devices):
     blocks, head, width = grads.shape
     buffer = pltpu.VMEM(grads.shape, jnp.bfloat16)
     return pl.pallas_call(
-        functools.partial(all_kernel, spans, spread, min(width, 256)),
+        functools.partial(all_kernel, wanted, spans, spread, min(width, 256)),
         out_shape=[
             jax.ShapeDtypeStruct(grads.shape, jnp.bfloat16),
             jax.ShapeDtypeStruct((devices, spread * head // 2 + blocks, head), jnp.float32),
         ]
         + [jax.ShapeDtypeStruct((count, head, width), jnp.bfloat16) for _, count in spans],
-        in_specs=[SMEM, SMEM, HBM, HBM],
+        in_specs=[SMEM, HBM, HBM],
         out_specs=[HBM, VMEM] + [HBM] * len(spans),
-        scratch_shapes=[buffer] * 4 + [pltpu.SemaphoreType.DMA((blocks,))] * 4,
+        scratch_shapes=[buffer] * 4
+        + [pltpu.SemaphoreType.DMA((blocks,))] * 4
+        + [pltpu.SMEM((blocks,), jnp.int32)] * 3,
         compiler_params=params_beside(grads),
         name="all_blocks",
-    )(source, place, grads, momentum)
+    )(codes, grads, momentum)
 
 
 def iterate(work):
@@ -440,7 +449,6 @@
 
 def local(grads, momentum, owner_table, pool_map):
     n_fsdp, n_tp = lax.axis_size("fsdp"), lax.axis_size("tp")
-    row = lax.axis_index("tp")
     blocks, head, width = grads.shape
     group = blocks // n_tp
     spread = -(-blocks // n_fsdp)
@@ -461,22 +469,15 @@
 
     first = singles(far, range(1))
     early = first + singles(far, range(1, cut)) + singles(near, range(cut - 1))
-    late = singles(near, range(cut - 1, cut))
+    late = []
     for c in range(cut, group - 1):
-        late += singles(far, [c]) + singles(near, [c])
+        late += singles(far, [c]) + singles(near, [c - 1, c])
     late += singles(near, [group - 1]) if group > cut else []
     last = singles(far, range(max(cut, group - 1), group))
     late += last
     own = [(0, tuple(range(group)))]
     chunks = early + late + own
     steps = [(x, c) for x, cs in chunks for c in cs]
-
-    codes = pool_map[0]
-    position = jnp.arange(blocks, dtype=jnp.int32)
-    offsets = jnp.array([c for _, c in steps], jnp.int32)
-    partners = jnp.array([x for x, _ in steps], jnp.int32)
-    place_out = partner(row, partners) * group + offsets
-    source = jnp.sum(jnp.where(codes[None, :] == place_out[:, None], position[None, :], 0), axis=1)
 
     starts, total = {}, 0
     for chunk in chunks:
@@ -506,8 +507,9 @@
         for chunk, array in zip(some, arrays):
             send(chunk, None, array)
     rest = chunks[len(first) :]
+    order = [(functools.partial(partner, x=x), c) for x, c in steps]
     new_momentum, parts, *ys = all_blocks(
-        source, place_out, grads, momentum, [starts[chunk] for chunk in rest], spread, n_fsdp
+        pool_map, grads, momentum, order, [starts[chunk] for chunk in rest], spread, n_fsdp
     )
     ys = dict(zip(rest, ys))
     for chunk, side in sends[len(first) :]:

time: 128 us -> 124 us (0.969)
  other arithmetic: 2.03 us -> 0 us
    ppermute x14, waiting for transfers between devices: 47.5 us -> 45.8 us  [send(): got[chunk, side] = lax.ppermute(array, 'tp', pairs)]
    reduce_sum x1 -> x0, other arithmetic: 1.35 us -> none  [local(): jnp.sum(jnp.where(codes[None, :] == place_out[:, None], position[None, :]...]
  transfers between devices with their start and end apart: 19 -> 19, of which waited for: 7 -> 6; matrix products, arithmetic and copies ran while one was open for 1% -> 1% of each run, Pallas kernels for 13% -> 13%
where the time goes in v7:
time: 124 us; the launch traced here: 123 us
  waiting for transfers between devices  47.5 us (38%)
  starting transfers between devices  43.6 us (35%)
  Pallas kernels  28.1 us (23%)
  local copies, waits for them, and re-layouts  3.37 us (3%)
    ppermute x14, waiting for transfers between devices, send(): got[chunk, side] = lax.ppermute(array, 'tp', pairs)  45.8 us
    ppermute x14, starting transfers between devices, send(): got[chunk, side] = lax.ppermute(array, 'tp', pairs)  29.7 us
    pallas_call x1, Pallas kernels, all_blocks(): pl.pallas_call(functools.partial(all_kernel, wanted, spans, spread, min(w...  9.96 us
    all_to_all x2, starting transfers between devices, local(): lax.all_to_all(parts, 'fsdp', split_axis=0, concat_axis=0, tiled=True)  9.02 us
    pallas_call x3, Pallas kernels, apply_blocks(): pl.pallas_call(functools.partial(apply_kernel, factor, members, at_end, t...  6.36 us
    pallas_call x2, Pallas kernels, first_blocks(): pl.pallas_call(functools.partial(first_kernel, wanted, pieces), out_shape...  4.38 us
    all_to_all x1, starting transfers between devices, local(): lax.all_to_all(packed, 'fsdp', split_axis=0, concat_axis=0, tiled=True)  3.54 us
    pallas_call x1, Pallas kernels, solve(): pl.pallas_call(functools.partial(solve_kernel, spread, skip, count, eleme...  2.92 us
  transfers between devices with their start and end apart: 19, of which 6 were waited for; matrix products, arithmetic and copies ran while one was open for 1% of the time, Pallas kernels for 13%

profile of v7, /device:TPU:0, one launch (start us, length us, event | category | flops | bytes accessed | tf_op | source)
XLA Modules:
  0.0 123.4 jit_solution(7494527356289379238)
XLA Ops:
  0.6 10.0 %all_blocks.1 = (bf16[16,128,1024]{2,1,0:T(8,128)(2,1)}, f32[8,144,128]{2,1,0:T(8,128)}, bf16[1,128,1024]{2,1,0:T(8,128)(2,1)}, bf16[1,128,1024]{2,1,0:T(8,128)(...) custom-call(s32[1,16]{1,0:T(1,128)} %codes.3, ...), custom_call_target="tpu_custom_call" | custom-call | tf_op jit(solution)/shard_map/all_blocks/pallas_call | solution.py:204
  10.6 5.2 %all-to-all-start = ((f32[8,144,128]{2,1,0:T(8,128)}), f32[8,144,128]{2,1,0:T(8,128)S(1)}, u32[]{:S(2)}, u32[]{:S(2)}) async-start(f32[8,144,128]{2,1,0:T(8,128)} %get-tuple-element.25), calls=%async_computation | async-start | bytes 1179648 | tf_op jit(solution)/shard_map/all_to_all | solution.py:518
  15.8 3.6 %collective-permute-start.2 = (bf16[1,128,1024]{2,1,0:T(8,128)(2,1)}, bf16[1,128,1024]{2,1,0:T(8,128)(2,1)S(1)}, u32[]{:S(2)}, u32[]{:S(2)}) collective-permute-start(bf16[1,128,1024]{2,1,0:T(8,128)(2,1)} %get-tuple-element.23), channel_id=1, source_target_pairs={{0,3},{1,2},{2,1},{3,0},{4,7},{5,6},{6,5},{7,4},{8,11},{9,10},{10,... | collective-permute-start | bytes 786440 | tf_op jit(solution)/shard_map/ppermute | solution.py:502
  19.4 0.0 collective-permute-start.3
  19.4 2.5 %shard_map.67 = bf16[1,128,1024]{2,1,0:T(8,128)(2,1)} custom-call(s32[1,16]{1,0:T(1,128)} %codes.3, bf16[16,128,1024]{2,1,0:T(8,128)(2,1)} %g_ref.5, bf16[16,128,1024]{2,1,0:T(8,128)(2,1)} %m_ref.5), custom_call_target="tpu_custom_call" | custom-call | tf_op jit(solution)/shard_map/pallas_call | solution.py:121
  22.0 0.0 copy-start.6
  22.0 0.0 copy-start.5
  22.0 2.0 %collective-permute-start = (bf16[1,128,1024]{2,1,0:T(8,128)(2,1)}, bf16[1,128,1024]{2,1,0:T(8,128)(2,1)S(1)}, u32[]{:S(2)}, u32[]{:S(2)}) collective-permute-start(bf16[1,128,1024]{2,1,0:T(8,128)(2,1)} %shard_map.67), channel_id=1, source_target_pairs={{0,3},{1,2},{2,1},{3,0},{4,7},{5,6},{6,5},{7,4},{8,11},{9,10},{10,... | collective-permute-start | bytes 786440 | tf_op jit(solution)/shard_map/ppermute | solution.py:502
  24.0 1.8 %shard_map.68 = bf16[1,128,1024]{2,1,0:T(8,128)(2,1)S(1)} custom-call(s32[1,16]{1,0:T(1,128)} %codes.3, bf16[16,128,1024]{2,1,0:T(8,128)(2,1)} %g_ref.5, bf16[16,128,1024]{2,1,0:T(8,128)(2,1)} %m_ref.5), custom_call_target="tpu_custom_call" | custom-call | tf_op jit(solution)/shard_map/pallas_call | solution.py:121
  25.8 0.0 copy-start
  25.8 1.1 collective-permute-start.1
  26.9 0.1 copy.9.owners
  27.0 0.0 all-to-all-done.parts_ref
  27.0 2.9 %solve.1 = (f32[136,128]{1,0:T(8,128)S(1)}, f32[72,128]{1,0:T(8,128)S(1)}, f32[1,128]{1,0:T(1,128)}) custom-call(s32[16,1]{1,0:T(8,128)S(1)} %copy.9.owners, s32[1,16]{1,0:T(1,128)S(1)} %copy-done.5, f32[8,144,128]{2,1,0:T(8,128)S(1)} %all-to-all-done.parts_ref), custom_call_target="tpu_custom_call" | custom-call | tf_op jit(solution)/shard_map/solve/pallas_call | solution.py:294
  29.9 0.7 collective-permute-start.4
  30.6 0.7 collective-permute-start.5
  31.3 23.4 %collective-permute-done.3.refs_3_.refs_4_ = bf16[1,128,1024]{2,1,0:T(8,128)(2,1)S(1)} collective-permute-done((bf16[1,128,1024]{2,1,0:T(8,128)(2,1)}, bf16[1,128,1024]{2,1,0:T(8,128)(2,1)S(1)}, u32[]{:S(2)}, u32[]{:S(2)}) %collective-permute-start.3) | collective-permute-done | bytes 262176 | tf_op jit(solution)/shard_map/ppermute | solution.py:502
  54.7 0.0 collective-permute-done.refs_0_.refs_1_
  54.7 10.8 %collective-permute-done.1.refs_1_.refs_2_ = bf16[1,128,1024]{2,1,0:T(8,128)(2,1)S(1)} collective-permute-done((bf16[1,128,1024]{2,1,0:T(8,128)(2,1)S(1)}, bf16[1,128,1024]{2,1,0:T(8,128)(2,1)S(1)}, u32[]{:S(2)}, u32[]{:S(2)}) %collective-permute-start.1) | collective-permute-done | bytes 262176 | tf_op jit(solution)/shard_map/ppermute | solution.py:502
  65.5 1.2 far_parts.1
  66.7 0.0 collective-permute-done.5.cross_ref
  66.7 0.0 collective-permute-done.4.same_ref
  66.7 3.8 %all-to-all-start.1 = ((f32[8,72,128]{2,1,0:T(8,128)}), f32[8,72,128]{2,1,0:T(8,128)S(1)}, u32[]{:S(2)}, u32[]{:S(2)}) async-start(f32[8,72,128]{2,1,0:T(8,128)} %far_parts.1), calls=%async_computation.1 | async-start | bytes 589824 | tf_op jit(solution)/shard_map/all_to_all | solution.py:537
  70.5 0.1 collective-permute-start.15
  70.6 2.9 %collective-permute-start.10 = (bf16[1,128,1024]{2,1,0:T(8,128)(2,1)}, bf16[1,128,1024]{2,1,0:T(8,128)(2,1)S(1)}, u32[]{:S(2)}, u32[]{:S(2)}) collective-permute-start(bf16[1,128,1024]{2,1,0:T(8,128)(2,1)} %get-tuple-element.33), channel_id=1, source_target_pairs={{0,3},{1,2},{2,1},{3,0},{4,7},{5,6},{6,5},{7,4},{8,11},{9,10},{10,... | collective-permute-start | bytes 786440 | tf_op jit(solution)/shard_map/ppermute | solution.py:502
  73.4 0.5 collective-permute-start.11
  74.0 1.0 collective-permute-start.12
  75.0 1.1 collective-permute-start.13
  76.0 1.7 %all-to-all-done.1.parts_ref = f32[8,72,128]{2,1,0:T(8,128)S(1)} async-done(((f32[8,72,128]{2,1,0:T(8,128)}), f32[8,72,128]{2,1,0:T(8,128)S(1)}, u32[]{:S(2)}, u32[]{:S(2)}) %all-to-all-start.1) | async-done | bytes 294944 | tf_op jit(solution)/shard_map/all_to_all | solution.py:537
  77.8 2.0 %finish.1 = f32[136,128]{1,0:T(8,128)S(1)} custom-call(f32[8,72,128]{2,1,0:T(8,128)S(1)} %all-to-all-done.1.parts_ref, f32[136,128]{1,0:T(8,128)S(1)} %collective-permute-done.4.same_ref, f32[72,128]{1,0:T(8,128)S(1)} %collective-permute-done.5.cross_ref), custom_call_target="tpu_custom_call" | custom-call | tf_op jit(solution)/shard_map/finish/pallas_call | solution.py:354
  79.7 0.9 broadcast_in_dim.2
  80.6 3.5 %all-to-all-start.2 = ((f32[8,136,128]{2,1,0:T(8,128)}), f32[8,136,128]{2,1,0:T(8,128)S(1)}, u32[]{:S(2)}, u32[]{:S(2)}) async-start(f32[8,136,128]{2,1,0:T(8,128)} %broadcast_in_dim.2), calls=%async_computation.2 | async-start | bytes 1114112 | tf_op jit(solution)/shard_map/all_to_all | solution.py:540
  84.1 0.0 collective-permute-done.15.refs_5_
  84.1 0.7 copy-done.3
  84.9 6.1 %collective-permute-start.6 = (bf16[1,128,1024]{2,1,0:T(8,128)(2,1)}, bf16[1,128,1024]{2,1,0:T(8,128)(2,1)S(1)}, u32[]{:S(2)}, u32[]{:S(2)}) collective-permute-start(bf16[1,128,1024]{2,1,0:T(8,128)(2,1)} %get-tuple-element.31), channel_id=1, source_target_pairs={{0,3},{3,0},{4,7},{7,4},{8,11},{11,8},{12,15},{15,12},{16,19},{19,... | collective-permute-start | bytes 786440 | tf_op jit(solution)/shard_map/ppermute | solution.py:502
  91.0 0.7 copy-done.1
  91.7 0.7 collective-permute-start.7
  92.4 6.0 %collective-permute-done.11.refs_1_ = bf16[1,128,1024]{2,1,0:T(8,128)(2,1)} collective-permute-done((bf16[1,128,1024]{2,1,0:T(8,128)(2,1)}, bf16[1,128,1024]{2,1,0:T(8,128)(2,1)}, u32[]{:S(2)}, u32[]{:S(2)}) %collective-permute-start.11) | collective-permute-done | bytes 262176 | tf_op jit(solution)/shard_map/ppermute | solution.py:502
  98.4 0.1 collective-permute-start.14
  98.4 1.3 %collective-permute-start.8 = (bf16[1,128,1024]{2,1,0:T(8,128)(2,1)}, bf16[1,128,1024]{2,1,0:T(8,128)(2,1)}, u32[]{:S(2)}, u32[]{:S(2)}) collective-permute-start(bf16[1,128,1024]{2,1,0:T(8,128)(2,1)} %get-tuple-element.32), channel_id=1, source_target_pairs={{1,3},{2,0},{5,7},{6,4},{9,11},{10,8},{13,15},{14,12},{17,19},{18,... | collective-permute-start | bytes 786440 | tf_op jit(solution)/shard_map/ppermute | solution.py:502
  99.7 2.8 %collective-permute-done.13.refs_3_ = bf16[1,128,1024]{2,1,0:T(8,128)(2,1)} collective-permute-done((bf16[1,128,1024]{2,1,0:T(8,128)(2,1)}, bf16[1,128,1024]{2,1,0:T(8,128)(2,1)}, u32[]{:S(2)}, u32[]{:S(2)}) %collective-permute-start.13) | collective-permute-done | bytes 262176 | tf_op jit(solution)/shard_map/ppermute | solution.py:502
  102.5 9.3 %collective-permute-start.9 = (bf16[1,128,1024]{2,1,0:T(8,128)(2,1)}, bf16[1,128,1024]{2,1,0:T(8,128)(2,1)}, u32[]{:S(2)}, u32[]{:S(2)}) collective-permute-start(bf16[1,128,1024]{2,1,0:T(8,128)(2,1)} %get-tuple-element.32), channel_id=1, source_target_pairs={{0,2},{3,1},{4,6},{7,5},{8,10},{11,9},{12,14},{15,13},{16,18},{19,... | collective-permute-start | bytes 786440 | tf_op jit(solution)/shard_map/ppermute | solution.py:502
  111.8 1.3 %unpack_all.1.q_ref = bf16[16,128,256]{2,1,0:T(8,128)(2,1)S(1)} custom-call(f32[8,136,128]{2,1,0:T(8,128)S(1)} %all-to-all-done.2.packed_ref), custom_call_target="tpu_custom_call" | custom-call | tf_op jit(solution)/shard_map/unpack_all/pallas_call | solution.py:381
  113.1 1.0 copy-done.4
  114.1 1.7 %apply_blocks.3.refs_5_ = bf16[16,128,1024]{2,1,0:T(8,128)(2,1)} custom-call(bf16[16,128,256]{2,1,0:T(8,128)(2,1)S(1)} %unpack_all.1.q_ref, bf16[4,128,1024]{2,1,0:T(8,128)(2,1)S(1)} %copy-done, bf16[1,128,1024]{2,1,0:T(8,128)(2,1)S(1)} %collective-permute-done.refs_0_.refs_1_, bf16[1,128,1024]{2,1,0:T(8,128)(2,1)S(1)} %collective-permute-done.1.refs_1_.refs_2_, ...), custom_call_target="tpu_custom_call" | custom-call | tf_op jit(solution)/shard_map/apply_blocks/pallas_call | solution.py:435
  115.8 2.9 %collective-permute-done.14.refs_4_ = bf16[1,128,1024]{2,1,0:T(8,128)(2,1)} collective-permute-done((bf16[1,128,1024]{2,1,0:T(8,128)(2,1)}, bf16[1,128,1024]{2,1,0:T(8,128)(2,1)}, u32[]{:S(2)}, u32[]{:S(2)}) %collective-permute-start.14) | collective-permute-done | bytes 262176 | tf_op jit(solution)/shard_map/ppermute | solution.py:502
  118.7 2.5 %apply_blocks.4.refs_4_ = bf16[16,128,1024]{2,1,0:T(8,128)(2,1)} custom-call(bf16[16,128,256]{2,1,0:T(8,128)(2,1)S(1)} %unpack_all.1.q_ref, bf16[1,128,1024]{2,1,0:T(8,128)(2,1)S(1)} %copy-done.2, bf16[1,128,1024]{2,1,0:T(8,128)(2,1)} %collective-permute-done.11.refs_1_, ...), custom_call_target="tpu_custom_call", output_to_operand_aliasing={{}: (6, {})} | custom-call | tf_op jit(solution)/shard_map/apply_blocks/pallas_call | solution.py:435
  121.3 2.1 %apply_blocks.5 = bf16[16,128,1024]{2,1,0:T(8,128)(2,1)} custom-call(bf16[16,128,256]{2,1,0:T(8,128)(2,1)S(1)} %unpack_all.1.q_ref, bf16[1,128,1024]{2,1,0:T(8,128)(2,1)S(1)} %collective-permute-done.6.refs_0_, bf16[1,128,1024]{2,1,0:T(8,128)(2,1)S(1)} %collective-permute-done.7.refs_1_, ...), custom_call_target="tpu_custom_call", output_to_operand_aliasing={{}: (5, {})} | custom-call | tf_op jit(solution)/shard_map/apply_blocks/pallas_call | solution.py:435
  (16 shorter events, 0.0 us)
Async XLA Ops:
  10.6 16.4 %all-to-all-start = ((f32[8,144,128]{2,1,0:T(8,128)}), f32[8,144,128]{2,1,0:T(8,128)S(1)}, u32[]{:S(2)}, u32[]{:S(2)}) async-start(f32[8,144,128]{2,1,0:T(8,128)} %get-tuple-element.25), calls=%async_computation | async-start | bytes 1179648 | tf_op jit(solution)/shard_map/all_to_all | solution.py:518
  15.8 14.8 %collective-permute-start.2 = (bf16[1,128,1024]{2,1,0:T(8,128)(2,1)}, bf16[1,128,1024]{2,1,0:T(8,128)(2,1)S(1)}, u32[]{:S(2)}, u32[]{:S(2)}) collective-permute-start(bf16[1,128,1024]{2,1,0:T(8,128)(2,1)} %get-tuple-element.23), channel_id=1, source_target_pairs={{0,3},{1,2},{2,1},{3,0},{4,7},{5,6},{6,5},{7,4},{8,11},{9,10},{10,... | collective-permute-start | bytes 786440 | tf_op jit(solution)/shard_map/ppermute | solution.py:502
  19.4 35.3 %collective-permute-start.3 = (bf16[1,128,1024]{2,1,0:T(8,128)(2,1)}, bf16[1,128,1024]{2,1,0:T(8,128)(2,1)S(1)}, u32[]{:S(2)}, u32[]{:S(2)}) collective-permute-start(bf16[1,128,1024]{2,1,0:T(8,128)(2,1)} %get-tuple-element.24), channel_id=1, source_target_pairs={{0,2},{1,3},{2,0},{3,1},{4,6},{5,7},{6,4},{7,5},{8,10},{9,11},{10,... | collective-permute-start | bytes 786440 | tf_op jit(solution)/shard_map/ppermute | solution.py:502
  22.0 5.0 %copy-start.6 = (s32[16,1]{0,1:T(1,128)S(1)}, s32[16,1]{0,1:T(1,128)}, u32[]{:S(2)}) copy-start(s32[16,1]{0,1:T(1,128)} %param.6) | copy-start | bytes 196
  22.0 5.0 %copy-start.5 = (s32[1,16]{1,0:T(1,128)S(1)}, s32[1,16]{1,0:T(1,128)}, u32[]{:S(2)}) copy-start(s32[1,16]{1,0:T(1,128)} %codes.3) | copy-start | bytes 196
  22.0 32.7 %collective-permute-start = (bf16[1,128,1024]{2,1,0:T(8,128)(2,1)}, bf16[1,128,1024]{2,1,0:T(8,128)(2,1)S(1)}, u32[]{:S(2)}, u32[]{:S(2)}) collective-permute-start(bf16[1,128,1024]{2,1,0:T(8,128)(2,1)} %shard_map.67), channel_id=1, source_target_pairs={{0,3},{1,2},{2,1},{3,0},{4,7},{5,6},{6,5},{7,4},{8,11},{9,10},{10,... | collective-permute-start | bytes 786440 | tf_op jit(solution)/shard_map/ppermute | solution.py:502
  25.8 87.3 %copy-start = (bf16[4,128,1024]{2,1,0:T(8,128)(2,1)S(1)}, bf16[4,128,1024]{2,1,0:T(8,128)(2,1)}, u32[]{:S(2)}) copy-start(bf16[4,128,1024]{2,1,0:T(8,128)(2,1)} %get-tuple-element.38.refs_0_) | copy-start | bytes 3145732
  25.8 39.6 %collective-permute-start.1 = (bf16[1,128,1024]{2,1,0:T(8,128)(2,1)S(1)}, bf16[1,128,1024]{2,1,0:T(8,128)(2,1)S(1)}, u32[]{:S(2)}, u32[]{:S(2)}) collective-permute-start(bf16[1,128,1024]{2,1,0:T(8,128)(2,1)S(1)} %shard_map.68), channel_id=1, source_target_pairs={{0,2},{1,3},{2,0},{3,1},{4,6},{5,7},{6,4},{7,5},{8,10},{9,11},{10,... | collective-permute-start | bytes 786440 | tf_op jit(solution)/shard_map/ppermute | solution.py:502
  29.9 36.8 %collective-permute-start.4 = (f32[136,128]{1,0:T(8,128)S(1)}, f32[136,128]{1,0:T(8,128)S(1)}, u32[]{:S(2)}, u32[]{:S(2)}) collective-permute-start(f32[136,128]{1,0:T(8,128)S(1)} %get-tuple-element.26), channel_id=1, source_target_pairs={{0,0},{1,8},{6,18},{7,26},{8,1},{9,9},{14,19},{15,27},{16,4},{17,1... | collective-permute-start | bytes 208904 | tf_op jit(solution)/shard_map/ppermute | solution.py:531
  30.6 36.1 %collective-permute-start.5 = (f32[72,128]{1,0:T(8,128)S(1)}, f32[72,128]{1,0:T(8,128)S(1)}, u32[]{:S(2)}, u32[]{:S(2)}) collective-permute-start(f32[72,128]{1,0:T(8,128)S(1)} %get-tuple-element.27), channel_id=1, source_target_pairs={{2,16},{3,24},{4,2},{5,10},{10,17},{11,25},{12,3},{13,11},{18,20},... | collective-permute-start | bytes 110600 | tf_op jit(solution)/shard_map/ppermute | solution.py:530
  66.7 11.1 %all-to-all-start.1 = ((f32[8,72,128]{2,1,0:T(8,128)}), f32[8,72,128]{2,1,0:T(8,128)S(1)}, u32[]{:S(2)}, u32[]{:S(2)}) async-start(f32[8,72,128]{2,1,0:T(8,128)} %far_parts.1), calls=%async_computation.1 | async-start | bytes 589824 | tf_op jit(solution)/shard_map/all_to_all | solution.py:537
  70.5 13.6 %collective-permute-start.15 = (bf16[1,128,1024]{2,1,0:T(8,128)(2,1)}, bf16[1,128,1024]{2,1,0:T(8,128)(2,1)S(1)}, u32[]{:S(2)}, u32[]{:S(2)}) collective-permute-start(bf16[1,128,1024]{2,1,0:T(8,128)(2,1)} %get-tuple-element.39), channel_id=1, source_target_pairs={{0,1},{1,0},{2,3},{3,2},{4,5},{5,4},{6,7},{7,6},{8,9},{9,8},{10,11... | collective-permute-start | bytes 786440 | tf_op jit(solution)/shard_map/ppermute | solution.py:502
  70.6 20.5 %collective-permute-start.10 = (bf16[1,128,1024]{2,1,0:T(8,128)(2,1)}, bf16[1,128,1024]{2,1,0:T(8,128)(2,1)S(1)}, u32[]{:S(2)}, u32[]{:S(2)}) collective-permute-start(bf16[1,128,1024]{2,1,0:T(8,128)(2,1)} %get-tuple-element.33), channel_id=1, source_target_pairs={{0,3},{1,2},{2,1},{3,0},{4,7},{5,6},{6,5},{7,4},{8,11},{9,10},{10,... | collective-permute-start | bytes 786440 | tf_op jit(solution)/shard_map/ppermute | solution.py:502
  73.4 24.9 %collective-permute-start.11 = (bf16[1,128,1024]{2,1,0:T(8,128)(2,1)}, bf16[1,128,1024]{2,1,0:T(8,128)(2,1)}, u32[]{:S(2)}, u32[]{:S(2)}) collective-permute-start(bf16[1,128,1024]{2,1,0:T(8,128)(2,1)} %get-tuple-element.34), channel_id=1, source_target_pairs={{0,2},{1,3},{2,0},{3,1},{4,6},{5,7},{6,4},{7,5},{8,10},{9,11},{10,... | collective-permute-start | bytes 786440 | tf_op jit(solution)/shard_map/ppermute | solution.py:502
  74.0 24.4 %collective-permute-start.12 = (bf16[1,128,1024]{2,1,0:T(8,128)(2,1)}, bf16[1,128,1024]{2,1,0:T(8,128)(2,1)}, u32[]{:S(2)}, u32[]{:S(2)}) collective-permute-start(bf16[1,128,1024]{2,1,0:T(8,128)(2,1)} %get-tuple-element.35), channel_id=1, source_target_pairs={{0,1},{1,0},{2,3},{3,2},{4,5},{5,4},{6,7},{7,6},{8,9},{9,8},{10,11... | collective-permute-start | bytes 786440 | tf_op jit(solution)/shard_map/ppermute | solution.py:502
  75.0 27.5 %collective-permute-start.13 = (bf16[1,128,1024]{2,1,0:T(8,128)(2,1)}, bf16[1,128,1024]{2,1,0:T(8,128)(2,1)}, u32[]{:S(2)}, u32[]{:S(2)}) collective-permute-start(bf16[1,128,1024]{2,1,0:T(8,128)(2,1)} %get-tuple-element.36), channel_id=1, source_target_pairs={{0,1},{1,0},{2,3},{3,2},{4,5},{5,4},{6,7},{7,6},{8,9},{9,8},{10,11... | collective-permute-start | bytes 786440 | tf_op jit(solution)/shard_map/ppermute | solution.py:502
  80.6 31.2 %all-to-all-start.2 = ((f32[8,136,128]{2,1,0:T(8,128)}), f32[8,136,128]{2,1,0:T(8,128)S(1)}, u32[]{:S(2)}, u32[]{:S(2)}) async-start(f32[8,136,128]{2,1,0:T(8,128)} %broadcast_in_dim.2), calls=%async_computation.2 | async-start | bytes 1114112 | tf_op jit(solution)/shard_map/all_to_all | solution.py:540
  84.1 0.7 copy-start.3
  84.9 36.4 %collective-permute-start.6 = (bf16[1,128,1024]{2,1,0:T(8,128)(2,1)}, bf16[1,128,1024]{2,1,0:T(8,128)(2,1)S(1)}, u32[]{:S(2)}, u32[]{:S(2)}) collective-permute-start(bf16[1,128,1024]{2,1,0:T(8,128)(2,1)} %get-tuple-element.31), channel_id=1, source_target_pairs={{0,3},{3,0},{4,7},{7,4},{8,11},{11,8},{12,15},{15,12},{16,19},{19,... | collective-permute-start | bytes 786440 | tf_op jit(solution)/shard_map/ppermute | solution.py:502
  91.0 0.7 copy-start.1
  91.7 29.5 %collective-permute-start.7 = (bf16[1,128,1024]{2,1,0:T(8,128)(2,1)}, bf16[1,128,1024]{2,1,0:T(8,128)(2,1)S(1)}, u32[]{:S(2)}, u32[]{:S(2)}) collective-permute-start(bf16[1,128,1024]{2,1,0:T(8,128)(2,1)} %get-tuple-element.31), channel_id=1, source_target_pairs={{1,2},{2,1},{5,6},{6,5},{9,10},{10,9},{13,14},{14,13},{17,18},{18,... | collective-permute-start | bytes 786440 | tf_op jit(solution)/shard_map/ppermute | solution.py:502
  98.4 20.4 %collective-permute-start.14 = (bf16[1,128,1024]{2,1,0:T(8,128)(2,1)}, bf16[1,128,1024]{2,1,0:T(8,128)(2,1)}, u32[]{:S(2)}, u32[]{:S(2)}) collective-permute-start(bf16[1,128,1024]{2,1,0:T(8,128)(2,1)} %get-tuple-element.37), channel_id=1, source_target_pairs={{0,1},{1,0},{2,3},{3,2},{4,5},{5,4},{6,7},{7,6},{8,9},{9,8},{10,11... | collective-permute-start | bytes 786440 | tf_op jit(solution)/shard_map/ppermute | solution.py:502
  98.4 22.9 %collective-permute-start.8 = (bf16[1,128,1024]{2,1,0:T(8,128)(2,1)}, bf16[1,128,1024]{2,1,0:T(8,128)(2,1)}, u32[]{:S(2)}, u32[]{:S(2)}) collective-permute-start(bf16[1,128,1024]{2,1,0:T(8,128)(2,1)} %get-tuple-element.32), channel_id=1, source_target_pairs={{1,3},{2,0},{5,7},{6,4},{9,11},{10,8},{13,15},{14,12},{17,19},{18,... | collective-permute-start | bytes 786440 | tf_op jit(solution)/shard_map/ppermute | solution.py:502
  102.5 18.8 %collective-permute-start.9 = (bf16[1,128,1024]{2,1,0:T(8,128)(2,1)}, bf16[1,128,1024]{2,1,0:T(8,128)(2,1)}, u32[]{:S(2)}, u32[]{:S(2)}) collective-permute-start(bf16[1,128,1024]{2,1,0:T(8,128)(2,1)} %get-tuple-element.32), channel_id=1, source_target_pairs={{0,2},{3,1},{4,6},{7,5},{8,10},{11,9},{12,14},{15,13},{16,18},{19,... | collective-permute-start | bytes 786440 | tf_op jit(solution)/shard_map/ppermute | solution.py:502
  113.1 5.6 %copy-start.2 = (bf16[1,128,1024]{2,1,0:T(8,128)(2,1)S(1)}, bf16[1,128,1024]{2,1,0:T(8,128)(2,1)}, u32[]{:S(2)}) copy-start(bf16[1,128,1024]{2,1,0:T(8,128)(2,1)} %copy-done.1) | copy-start | bytes 786436
  113.1 1.0 copy-start.4

commit v8 on v6

--- a/solution.py
+++ b/solution.py
@@ -390,18 +390,29 @@
         return pltpu.make_async_copy(u_buf.at[i, :, part], out.at[places[i], :, part], u_sem.at[i, j])
 
     places = [place_at(row) for place_at, _, _ in members]
-    for i, (_, ways, k) in enumerate(members):
+
+    def update(i, way, k):
         q = q_ref[places[i]]
         for j in range(tiles):
             part = pl.ds(j * width, width)
-            y = refs[ways[0]][k, :, part]
-            if len(ways) > 1:
-                y = jnp.where(at_end(row), y, refs[ways[1]][k, :, part])
+            y = refs[way][k, :, part]
             y = jnp.concatenate([y, y], axis=0)
             ortho = jnp.dot(q, y, preferred_element_type=jnp.float32)
             ortho = ortho.astype(jnp.bfloat16).astype(jnp.float32)
             u_buf[i, :, part] = (-factor * ortho).astype(jnp.bfloat16)
             u_copy(i, j).start()
+
+    if len(members[0][1]) == 1:
+        for i, (_, ways, k) in enumerate(members):
+            update(i, ways[0], k)
+    else:
+        for way, here in ((0, at_end(row)), (1, jnp.logical_not(at_end(row)))):
+
+            @pl.when(here)
+            def _():
+                for i, (_, ways, k) in enumerate(members):
+                    update(i, ways[way], k)
+
     for i in range(len(members)):
         for j in range(tiles):
             u_copy(i, j).wait()

time: 128 us -> 128 us (level)
  no operation moved by 1% of the time
where the time goes in v8:
time: 128 us; the launch traced here: 127 us
  waiting for transfers between devices  48.3 us (38%)
  starting transfers between devices  44.3 us (35%)
  Pallas kernels  28 us (22%)
  local copies, waits for them, and re-layouts  3.38 us (3%)
  other arithmetic  2.03 us (2%)
    ppermute x14, waiting for transfers between devices, send(): got[chunk, side] = lax.ppermute(array, 'tp', pairs)  47.5 us
    ppermute x14, starting transfers between devices, send(): got[chunk, side] = lax.ppermute(array, 'tp', pairs)  30.4 us
    pallas_call x1, Pallas kernels, all_blocks(): pl.pallas_call(functools.partial(all_kernel, spans, spread, min(width, 25...  9.93 us
    all_to_all x2, starting transfers between devices, local(): lax.all_to_all(parts, 'fsdp', split_axis=0, concat_axis=0, tiled=True)  9.02 us
    pallas_call x3, Pallas kernels, apply_blocks(): pl.pallas_call(functools.partial(apply_kernel, factor, members, at_end, t...  6.34 us
    pallas_call x2, Pallas kernels, first_blocks(): pl.pallas_call(functools.partial(first_kernel, wanted, pieces), out_shape...  4.37 us
    all_to_all x1, starting transfers between devices, local(): lax.all_to_all(packed, 'fsdp', split_axis=0, concat_axis=0, tiled=True)  3.54 us
    pallas_call x1, Pallas kernels, solve(): pl.pallas_call(functools.partial(solve_kernel, spread, skip, count, eleme...  2.92 us
  transfers between devices with their start and end apart: 19, of which 7 were waited for; matrix products, arithmetic and copies ran while one was open for 1% of the time, Pallas kernels for 13%

profile of v8, /device:TPU:0, one launch (start us, length us, event | category | flops | bytes accessed | tf_op | source)
XLA Modules:
  0.0 126.9 jit_solution(16736772477902165521)
XLA Ops:
  0.6 0.7 multiply_add_fusion.place
  1.3 1.3 %select_reduce_fusion.source = s32[16]{0:T(128)} fusion(s32[16]{0:T(128)} %bitcast.2, s32[16]{0:T(128)S(1)} %multiply_add_fusion.place), kind=kLoop, calls=%fused_computation | loop fusion | flops 752 | bytes 192 | tf_op jit(solution)/shard_map/reduce_sum | solution.py:490
  2.7 9.9 %all_blocks.1 = (bf16[16,128,1024]{2,1,0:T(8,128)(2,1)}, f32[8,144,128]{2,1,0:T(8,128)}, bf16[1,128,1024]{2,1,0:T(8,128)(2,1)}, bf16[1,128,1024]{2,1,0:T(8,128)(...) custom-call(s32[16]{0:T(128)} %select_reduce_fusion.source, ...), custom_call_target="tpu_custom_call" | custom-call | tf_op jit(solution)/shard_map/all_blocks/pallas_call | solution.py:197
  12.6 5.2 %all-to-all-start = ((f32[8,144,128]{2,1,0:T(8,128)}), f32[8,144,128]{2,1,0:T(8,128)S(1)}, u32[]{:S(2)}, u32[]{:S(2)}) async-start(f32[8,144,128]{2,1,0:T(8,128)} %get-tuple-element.25), calls=%async_computation | async-start | bytes 1179648 | tf_op jit(solution)/shard_map/all_to_all | solution.py:527
  17.8 3.6 %collective-permute-start.2 = (bf16[1,128,1024]{2,1,0:T(8,128)(2,1)}, bf16[1,128,1024]{2,1,0:T(8,128)(2,1)S(1)}, u32[]{:S(2)}, u32[]{:S(2)}) collective-permute-start(bf16[1,128,1024]{2,1,0:T(8,128)(2,1)} %get-tuple-element.23), channel_id=1, source_target_pairs={{0,3},{1,2},{2,1},{3,0},{4,7},{5,6},{6,5},{7,4},{8,11},{9,10},{10,... | collective-permute-start | bytes 786440 | tf_op jit(solution)/shard_map/ppermute | solution.py:512
  21.4 2.5 %shard_map.85 = bf16[1,128,1024]{2,1,0:T(8,128)(2,1)} custom-call(s32[1,16]{1,0:T(1,128)} %codes.1, bf16[16,128,1024]{2,1,0:T(8,128)(2,1)} %g_ref.5, bf16[16,128,1024]{2,1,0:T(8,128)(2,1)} %m_ref.5), custom_call_target="tpu_custom_call" | custom-call | tf_op jit(solution)/shard_map/pallas_call | solution.py:121
  24.0 0.0 copy-start.7
  24.0 0.0 copy-start.5
  24.0 2.0 %collective-permute-start = (bf16[1,128,1024]{2,1,0:T(8,128)(2,1)}, bf16[1,128,1024]{2,1,0:T(8,128)(2,1)S(1)}, u32[]{:S(2)}, u32[]{:S(2)}) collective-permute-start(bf16[1,128,1024]{2,1,0:T(8,128)(2,1)} %shard_map.85), channel_id=1, source_target_pairs={{0,3},{1,2},{2,1},{3,0},{4,7},{5,6},{6,5},{7,4},{8,11},{9,10},{10,... | collective-permute-start | bytes 786440 | tf_op jit(solution)/shard_map/ppermute | solution.py:512
  26.0 1.8 %shard_map.86 = bf16[1,128,1024]{2,1,0:T(8,128)(2,1)S(1)} custom-call(s32[1,16]{1,0:T(1,128)} %codes.1, bf16[16,128,1024]{2,1,0:T(8,128)(2,1)} %g_ref.5, bf16[16,128,1024]{2,1,0:T(8,128)(2,1)} %m_ref.5), custom_call_target="tpu_custom_call" | custom-call | tf_op jit(solution)/shard_map/pallas_call | solution.py:121
  27.8 0.0 copy-start
  27.8 1.1 collective-permute-start.1
  28.9 0.1 copy.12.owners
  29.0 2.9 %solve.1 = (f32[136,128]{1,0:T(8,128)S(1)}, f32[72,128]{1,0:T(8,128)S(1)}, f32[1,128]{1,0:T(1,128)}) custom-call(s32[16,1]{1,0:T(8,128)S(1)} %copy.12.owners, s32[1,16]{1,0:T(1,128)S(1)} %copy-done.5, f32[8,144,128]{2,1,0:T(8,128)S(1)} %all-to-all-done.parts_ref), custom_call_target="tpu_custom_call" | custom-call | tf_op jit(solution)/shard_map/solve/pallas_call | solution.py:285
  31.9 0.7 collective-permute-start.4
  32.6 0.0 collective-permute-done.2.refs_2_.refs_3_
  32.6 0.7 collective-permute-start.5
  33.3 23.4 %collective-permute-done.3.refs_3_.refs_4_ = bf16[1,128,1024]{2,1,0:T(8,128)(2,1)S(1)} collective-permute-done((bf16[1,128,1024]{2,1,0:T(8,128)(2,1)}, bf16[1,128,1024]{2,1,0:T(8,128)(2,1)S(1)}, u32[]{:S(2)}, u32[]{:S(2)}) %collective-permute-start.3) | collective-permute-done | bytes 262176 | tf_op jit(solution)/shard_map/ppermute | solution.py:512
  56.7 10.8 %collective-permute-done.1.refs_1_.refs_2_ = bf16[1,128,1024]{2,1,0:T(8,128)(2,1)S(1)} collective-permute-done((bf16[1,128,1024]{2,1,0:T(8,128)(2,1)S(1)}, bf16[1,128,1024]{2,1,0:T(8,128)(2,1)S(1)}, u32[]{:S(2)}, u32[]{:S(2)}) %collective-permute-start.1) | collective-permute-done | bytes 262176 | tf_op jit(solution)/shard_map/ppermute | solution.py:512
  67.5 1.2 far_parts.1
  68.7 0.0 collective-permute-done.5.cross_ref
  68.7 0.0 collective-permute-done.4.same_ref
  68.7 3.8 %all-to-all-start.1 = ((f32[8,72,128]{2,1,0:T(8,128)}), f32[8,72,128]{2,1,0:T(8,128)S(1)}, u32[]{:S(2)}, u32[]{:S(2)}) async-start(f32[8,72,128]{2,1,0:T(8,128)} %far_parts.1), calls=%async_computation.1 | async-start | bytes 589824 | tf_op jit(solution)/shard_map/all_to_all | solution.py:546
  72.5 0.1 collective-permute-start.15
  72.6 2.0 %collective-permute-start.10 = (bf16[1,128,1024]{2,1,0:T(8,128)(2,1)}, bf16[1,128,1024]{2,1,0:T(8,128)(2,1)S(1)}, u32[]{:S(2)}, u32[]{:S(2)}) collective-permute-start(bf16[1,128,1024]{2,1,0:T(8,128)(2,1)} %get-tuple-element.33), channel_id=1, source_target_pairs={{0,1},{1,0},{2,3},{3,2},{4,5},{5,4},{6,7},{7,6},{8,9},{9,8},{10,11... | collective-permute-start | bytes 786440 | tf_op jit(solution)/shard_map/ppermute | solution.py:512
  74.5 2.9 %collective-permute-start.11 = (bf16[1,128,1024]{2,1,0:T(8,128)(2,1)}, bf16[1,128,1024]{2,1,0:T(8,128)(2,1)}, u32[]{:S(2)}, u32[]{:S(2)}) collective-permute-start(bf16[1,128,1024]{2,1,0:T(8,128)(2,1)} %get-tuple-element.34), channel_id=1, source_target_pairs={{0,3},{1,2},{2,1},{3,0},{4,7},{5,6},{6,5},{7,4},{8,11},{9,10},{10,... | collective-permute-start | bytes 786440 | tf_op jit(solution)/shard_map/ppermute | solution.py:512
  77.4 1.5 %collective-permute-start.13 = (bf16[1,128,1024]{2,1,0:T(8,128)(2,1)}, bf16[1,128,1024]{2,1,0:T(8,128)(2,1)}, u32[]{:S(2)}, u32[]{:S(2)}) collective-permute-start(bf16[1,128,1024]{2,1,0:T(8,128)(2,1)} %get-tuple-element.36), channel_id=1, source_target_pairs={{0,1},{1,0},{2,3},{3,2},{4,5},{5,4},{6,7},{7,6},{8,9},{9,8},{10,11... | collective-permute-start | bytes 786440 | tf_op jit(solution)/shard_map/ppermute | solution.py:512
  78.9 0.8 all-to-all-done.1.parts_ref
  79.8 2.0 %finish.1 = f32[136,128]{1,0:T(8,128)S(1)} custom-call(f32[8,72,128]{2,1,0:T(8,128)S(1)} %all-to-all-done.1.parts_ref, f32[136,128]{1,0:T(8,128)S(1)} %collective-permute-done.4.same_ref, f32[72,128]{1,0:T(8,128)S(1)} %collective-permute-done.5.cross_ref), custom_call_target="tpu_custom_call" | custom-call | tf_op jit(solution)/shard_map/finish/pallas_call | solution.py:345
  81.7 0.9 broadcast_in_dim.22
  82.6 3.5 %all-to-all-start.2 = ((f32[8,136,128]{2,1,0:T(8,128)}), f32[8,136,128]{2,1,0:T(8,128)S(1)}, u32[]{:S(2)}, u32[]{:S(2)}) async-start(f32[8,136,128]{2,1,0:T(8,128)} %broadcast_in_dim.22), calls=%async_computation.2 | async-start | bytes 1114112 | tf_op jit(solution)/shard_map/all_to_all | solution.py:549
  86.1 0.0 collective-permute-done.15.refs_5_
  86.2 0.7 copy-done.3
  86.9 4.8 %collective-permute-start.6 = (bf16[1,128,1024]{2,1,0:T(8,128)(2,1)}, bf16[1,128,1024]{2,1,0:T(8,128)(2,1)S(1)}, u32[]{:S(2)}, u32[]{:S(2)}) collective-permute-start(bf16[1,128,1024]{2,1,0:T(8,128)(2,1)} %get-tuple-element.31), channel_id=1, source_target_pairs={{0,3},{3,0},{4,7},{7,4},{8,11},{11,8},{12,15},{15,12},{16,19},{19,... | collective-permute-start | bytes 786440 | tf_op jit(solution)/shard_map/ppermute | solution.py:512
  91.7 6.9 %collective-permute-done.10.refs_0_ = bf16[1,128,1024]{2,1,0:T(8,128)(2,1)S(1)} collective-permute-done((bf16[1,128,1024]{2,1,0:T(8,128)(2,1)}, bf16[1,128,1024]{2,1,0:T(8,128)(2,1)S(1)}, u32[]{:S(2)}, u32[]{:S(2)}) %collective-permute-start.10) | collective-permute-done | bytes 262176 | tf_op jit(solution)/shard_map/ppermute | solution.py:512
  98.5 0.7 copy-done.1
  99.2 0.7 collective-permute-start.7
  99.9 1.2 collective-permute-start.14
  101.1 1.3 %collective-permute-start.8 = (bf16[1,128,1024]{2,1,0:T(8,128)(2,1)}, bf16[1,128,1024]{2,1,0:T(8,128)(2,1)}, u32[]{:S(2)}, u32[]{:S(2)}) collective-permute-start(bf16[1,128,1024]{2,1,0:T(8,128)(2,1)} %get-tuple-element.32), channel_id=1, source_target_pairs={{1,3},{2,0},{5,7},{6,4},{9,11},{10,8},{13,15},{14,12},{17,19},{18,... | collective-permute-start | bytes 786440 | tf_op jit(solution)/shard_map/ppermute | solution.py:512
  102.4 2.1 %collective-permute-done.13.refs_3_ = bf16[1,128,1024]{2,1,0:T(8,128)(2,1)} collective-permute-done((bf16[1,128,1024]{2,1,0:T(8,128)(2,1)}, bf16[1,128,1024]{2,1,0:T(8,128)(2,1)}, u32[]{:S(2)}, u32[]{:S(2)}) %collective-permute-start.13) | collective-permute-done | bytes 262176 | tf_op jit(solution)/shard_map/ppermute | solution.py:512
  104.5 9.3 %collective-permute-start.9 = (bf16[1,128,1024]{2,1,0:T(8,128)(2,1)}, bf16[1,128,1024]{2,1,0:T(8,128)(2,1)}, u32[]{:S(2)}, u32[]{:S(2)}) collective-permute-start(bf16[1,128,1024]{2,1,0:T(8,128)(2,1)} %get-tuple-element.32), channel_id=1, source_target_pairs={{0,2},{3,1},{4,6},{7,5},{8,10},{11,9},{12,14},{15,13},{16,18},{19,... | collective-permute-start | bytes 786440 | tf_op jit(solution)/shard_map/ppermute | solution.py:512
  113.8 1.3 %unpack_all.1.q_ref = bf16[16,128,256]{2,1,0:T(8,128)(2,1)S(1)} custom-call(f32[8,136,128]{2,1,0:T(8,128)S(1)} %all-to-all-done.2.packed_ref), custom_call_target="tpu_custom_call" | custom-call | tf_op jit(solution)/shard_map/unpack_all/pallas_call | solution.py:372
  115.2 1.0 copy-done.4
  116.1 1.7 %apply_blocks.3.refs_5_ = bf16[16,128,1024]{2,1,0:T(8,128)(2,1)} custom-call(bf16[16,128,256]{2,1,0:T(8,128)(2,1)S(1)} %unpack_all.1.q_ref, bf16[4,128,1024]{2,1,0:T(8,128)(2,1)S(1)} %copy-done, bf16[1,128,1024]{2,1,0:T(8,128)(2,1)S(1)} %collective-permute-done.refs_0_.refs_1_, bf16[1,128,1024]{2,1,0:T(8,128)(2,1)S(1)} %collective-permute-done.1.refs_1_.refs_2_, ...), custom_call_target="tpu_custom_call" | custom-call | tf_op jit(solution)/shard_map/apply_blocks/pallas_call | solution.py:437
  117.9 0.3 collective-permute-done.14.refs_4_
  118.2 2.5 %apply_blocks.4.refs_4_ = bf16[16,128,1024]{2,1,0:T(8,128)(2,1)} custom-call(bf16[16,128,256]{2,1,0:T(8,128)(2,1)S(1)} %unpack_all.1.q_ref, bf16[1,128,1024]{2,1,0:T(8,128)(2,1)S(1)} %copy-done.2, bf16[1,128,1024]{2,1,0:T(8,128)(2,1)} %collective-permute-done.11.refs_1_, ...), custom_call_target="tpu_custom_call", output_to_operand_aliasing={{}: (6, {})} | custom-call | tf_op jit(solution)/shard_map/apply_blocks/pallas_call | solution.py:437
  120.7 4.1 %collective-permute-done.8.refs_2_ = bf16[1,128,1024]{2,1,0:T(8,128)(2,1)} collective-permute-done((bf16[1,128,1024]{2,1,0:T(8,128)(2,1)}, bf16[1,128,1024]{2,1,0:T(8,128)(2,1)}, u32[]{:S(2)}, u32[]{:S(2)}) %collective-permute-start.8) | collective-permute-done | bytes 262176 | tf_op jit(solution)/shard_map/ppermute | solution.py:512
  124.8 2.1 %apply_blocks.5 = bf16[16,128,1024]{2,1,0:T(8,128)(2,1)} custom-call(bf16[16,128,256]{2,1,0:T(8,128)(2,1)S(1)} %unpack_all.1.q_ref, bf16[1,128,1024]{2,1,0:T(8,128)(2,1)S(1)} %collective-permute-done.6.refs_0_, bf16[1,128,1024]{2,1,0:T(8,128)(2,1)S(1)} %collective-permute-done.7.refs_1_, ...), custom_call_target="tpu_custom_call", output_to_operand_aliasing={{}: (5, {})} | custom-call | tf_op jit(solution)/shard_map/apply_blocks/pallas_call | solution.py:437
  (20 shorter events, 0.0 us)
Async XLA Ops:
  1.3 1.4 %copy-start.6 = (s32[16]{0:T(128)}, s32[16]{0:T(128)S(1)}, u32[]{:S(2)}) copy-start(s32[16]{0:T(128)S(1)} %multiply_add_fusion.place) | copy-start | bytes 196
  12.6 16.4 %all-to-all-start = ((f32[8,144,128]{2,1,0:T(8,128)}), f32[8,144,128]{2,1,0:T(8,128)S(1)}, u32[]{:S(2)}, u32[]{:S(2)}) async-start(f32[8,144,128]{2,1,0:T(8,128)} %get-tuple-element.25), calls=%async_computation | async-start | bytes 1179648 | tf_op jit(solution)/shard_map/all_to_all | solution.py:527
  17.8 14.8 %collective-permute-start.2 = (bf16[1,128,1024]{2,1,0:T(8,128)(2,1)}, bf16[1,128,1024]{2,1,0:T(8,128)(2,1)S(1)}, u32[]{:S(2)}, u32[]{:S(2)}) collective-permute-start(bf16[1,128,1024]{2,1,0:T(8,128)(2,1)} %get-tuple-element.23), channel_id=1, source_target_pairs={{0,3},{1,2},{2,1},{3,0},{4,7},{5,6},{6,5},{7,4},{8,11},{9,10},{10,... | collective-permute-start | bytes 786440 | tf_op jit(solution)/shard_map/ppermute | solution.py:512
  21.4 35.3 %collective-permute-start.3 = (bf16[1,128,1024]{2,1,0:T(8,128)(2,1)}, bf16[1,128,1024]{2,1,0:T(8,128)(2,1)S(1)}, u32[]{:S(2)}, u32[]{:S(2)}) collective-permute-start(bf16[1,128,1024]{2,1,0:T(8,128)(2,1)} %get-tuple-element.24), channel_id=1, source_target_pairs={{0,2},{1,3},{2,0},{3,1},{4,6},{5,7},{6,4},{7,5},{8,10},{9,11},{10,... | collective-permute-start | bytes 786440 | tf_op jit(solution)/shard_map/ppermute | solution.py:512
  24.0 5.0 %copy-start.7 = (s32[16,1]{0,1:T(1,128)S(1)}, s32[16,1]{0,1:T(1,128)}, u32[]{:S(2)}) copy-start(s32[16,1]{0,1:T(1,128)} %param.8) | copy-start | bytes 196
  24.0 5.0 %copy-start.5 = (s32[1,16]{1,0:T(1,128)S(1)}, s32[1,16]{1,0:T(1,128)}, u32[]{:S(2)}) copy-start(s32[1,16]{1,0:T(1,128)} %codes.1) | copy-start | bytes 196
  24.0 32.7 %collective-permute-start = (bf16[1,128,1024]{2,1,0:T(8,128)(2,1)}, bf16[1,128,1024]{2,1,0:T(8,128)(2,1)S(1)}, u32[]{:S(2)}, u32[]{:S(2)}) collective-permute-start(bf16[1,128,1024]{2,1,0:T(8,128)(2,1)} %shard_map.85), channel_id=1, source_target_pairs={{0,3},{1,2},{2,1},{3,0},{4,7},{5,6},{6,5},{7,4},{8,11},{9,10},{10,... | collective-permute-start | bytes 786440 | tf_op jit(solution)/shard_map/ppermute | solution.py:512
  27.8 87.3 %copy-start = (bf16[4,128,1024]{2,1,0:T(8,128)(2,1)S(1)}, bf16[4,128,1024]{2,1,0:T(8,128)(2,1)}, u32[]{:S(2)}) copy-start(bf16[4,128,1024]{2,1,0:T(8,128)(2,1)} %get-tuple-element.38.refs_0_) | copy-start | bytes 3145732
  27.8 39.7 %collective-permute-start.1 = (bf16[1,128,1024]{2,1,0:T(8,128)(2,1)S(1)}, bf16[1,128,1024]{2,1,0:T(8,128)(2,1)S(1)}, u32[]{:S(2)}, u32[]{:S(2)}) collective-permute-start(bf16[1,128,1024]{2,1,0:T(8,128)(2,1)S(1)} %shard_map.86), channel_id=1, source_target_pairs={{0,2},{1,3},{2,0},{3,1},{4,6},{5,7},{6,4},{7,5},{8,10},{9,11},{10,... | collective-permute-start | bytes 786440 | tf_op jit(solution)/shard_map/ppermute | solution.py:512
  31.9 36.8 %collective-permute-start.4 = (f32[136,128]{1,0:T(8,128)S(1)}, f32[136,128]{1,0:T(8,128)S(1)}, u32[]{:S(2)}, u32[]{:S(2)}) collective-permute-start(f32[136,128]{1,0:T(8,128)S(1)} %get-tuple-element.26), channel_id=1, source_target_pairs={{0,0},{1,8},{6,18},{7,26},{8,1},{9,9},{14,19},{15,27},{16,4},{17,1... | collective-permute-start | bytes 208904 | tf_op jit(solution)/shard_map/ppermute | solution.py:540
  32.6 36.1 %collective-permute-start.5 = (f32[72,128]{1,0:T(8,128)S(1)}, f32[72,128]{1,0:T(8,128)S(1)}, u32[]{:S(2)}, u32[]{:S(2)}) collective-permute-start(f32[72,128]{1,0:T(8,128)S(1)} %get-tuple-element.27), channel_id=1, source_target_pairs={{2,16},{3,24},{4,2},{5,10},{10,17},{11,25},{12,3},{13,11},{18,20},... | collective-permute-start | bytes 110600 | tf_op jit(solution)/shard_map/ppermute | solution.py:539
  68.7 11.1 %all-to-all-start.1 = ((f32[8,72,128]{2,1,0:T(8,128)}), f32[8,72,128]{2,1,0:T(8,128)S(1)}, u32[]{:S(2)}, u32[]{:S(2)}) async-start(f32[8,72,128]{2,1,0:T(8,128)} %far_parts.1), calls=%async_computation.1 | async-start | bytes 589824 | tf_op jit(solution)/shard_map/all_to_all | solution.py:546
  72.5 13.6 %collective-permute-start.15 = (bf16[1,128,1024]{2,1,0:T(8,128)(2,1)}, bf16[1,128,1024]{2,1,0:T(8,128)(2,1)S(1)}, u32[]{:S(2)}, u32[]{:S(2)}) collective-permute-start(bf16[1,128,1024]{2,1,0:T(8,128)(2,1)} %get-tuple-element.39), channel_id=1, source_target_pairs={{0,1},{1,0},{2,3},{3,2},{4,5},{5,4},{6,7},{7,6},{8,9},{9,8},{10,11... | collective-permute-start | bytes 786440 | tf_op jit(solution)/shard_map/ppermute | solution.py:512
  72.6 25.9 %collective-permute-start.10 = (bf16[1,128,1024]{2,1,0:T(8,128)(2,1)}, bf16[1,128,1024]{2,1,0:T(8,128)(2,1)S(1)}, u32[]{:S(2)}, u32[]{:S(2)}) collective-permute-start(bf16[1,128,1024]{2,1,0:T(8,128)(2,1)} %get-tuple-element.33), channel_id=1, source_target_pairs={{0,1},{1,0},{2,3},{3,2},{4,5},{5,4},{6,7},{7,6},{8,9},{9,8},{10,11... | collective-permute-start | bytes 786440 | tf_op jit(solution)/shard_map/ppermute | solution.py:512
  74.5 25.3 %collective-permute-start.11 = (bf16[1,128,1024]{2,1,0:T(8,128)(2,1)}, bf16[1,128,1024]{2,1,0:T(8,128)(2,1)}, u32[]{:S(2)}, u32[]{:S(2)}) collective-permute-start(bf16[1,128,1024]{2,1,0:T(8,128)(2,1)} %get-tuple-element.34), channel_id=1, source_target_pairs={{0,3},{1,2},{2,1},{3,0},{4,7},{5,6},{6,5},{7,4},{8,11},{9,10},{10,... | collective-permute-start | bytes 786440 | tf_op jit(solution)/shard_map/ppermute | solution.py:512
  77.4 23.7 %collective-permute-start.12 = (bf16[1,128,1024]{2,1,0:T(8,128)(2,1)}, bf16[1,128,1024]{2,1,0:T(8,128)(2,1)}, u32[]{:S(2)}, u32[]{:S(2)}) collective-permute-start(bf16[1,128,1024]{2,1,0:T(8,128)(2,1)} %get-tuple-element.35), channel_id=1, source_target_pairs={{0,2},{1,3},{2,0},{3,1},{4,6},{5,7},{6,4},{7,5},{8,10},{9,11},{10,... | collective-permute-start | bytes 786440 | tf_op jit(solution)/shard_map/ppermute | solution.py:512
  77.4 27.1 %collective-permute-start.13 = (bf16[1,128,1024]{2,1,0:T(8,128)(2,1)}, bf16[1,128,1024]{2,1,0:T(8,128)(2,1)}, u32[]{:S(2)}, u32[]{:S(2)}) collective-permute-start(bf16[1,128,1024]{2,1,0:T(8,128)(2,1)} %get-tuple-element.36), channel_id=1, source_target_pairs={{0,1},{1,0},{2,3},{3,2},{4,5},{5,4},{6,7},{7,6},{8,9},{9,8},{10,11... | collective-permute-start | bytes 786440 | tf_op jit(solution)/shard_map/ppermute | solution.py:512
  82.6 31.2 %all-to-all-start.2 = ((f32[8,136,128]{2,1,0:T(8,128)}), f32[8,136,128]{2,1,0:T(8,128)S(1)}, u32[]{:S(2)}, u32[]{:S(2)}) async-start(f32[8,136,128]{2,1,0:T(8,128)} %broadcast_in_dim.22), calls=%async_computation.2 | async-start | bytes 1114112 | tf_op jit(solution)/shard_map/all_to_all | solution.py:549
  86.1 0.7 copy-start.3
  86.9 33.8 %collective-permute-start.6 = (bf16[1,128,1024]{2,1,0:T(8,128)(2,1)}, bf16[1,128,1024]{2,1,0:T(8,128)(2,1)S(1)}, u32[]{:S(2)}, u32[]{:S(2)}) collective-permute-start(bf16[1,128,1024]{2,1,0:T(8,128)(2,1)} %get-tuple-element.31), channel_id=1, source_target_pairs={{0,3},{3,0},{4,7},{7,4},{8,11},{11,8},{12,15},{15,12},{16,19},{19,... | collective-permute-start | bytes 786440 | tf_op jit(solution)/shard_map/ppermute | solution.py:512
  98.5 0.7 copy-start.1
  99.2 21.5 %collective-permute-start.7 = (bf16[1,128,1024]{2,1,0:T(8,128)(2,1)}, bf16[1,128,1024]{2,1,0:T(8,128)(2,1)S(1)}, u32[]{:S(2)}, u32[]{:S(2)}) collective-permute-start(bf16[1,128,1024]{2,1,0:T(8,128)(2,1)} %get-tuple-element.31), channel_id=1, source_target_pairs={{1,2},{2,1},{5,6},{6,5},{9,10},{10,9},{13,14},{14,13},{17,18},{18,... | collective-permute-start | bytes 786440 | tf_op jit(solution)/shard_map/ppermute | solution.py:512
  99.9 18.3 %collective-permute-start.14 = (bf16[1,128,1024]{2,1,0:T(8,128)(2,1)}, bf16[1,128,1024]{2,1,0:T(8,128)(2,1)}, u32[]{:S(2)}, u32[]{:S(2)}) collective-permute-start(bf16[1,128,1024]{2,1,0:T(8,128)(2,1)} %get-tuple-element.37), channel_id=1, source_target_pairs={{0,1},{1,0},{2,3},{3,2},{4,5},{5,4},{6,7},{7,6},{8,9},{9,8},{10,11... | collective-permute-start | bytes 786440 | tf_op jit(solution)/shard_map/ppermute | solution.py:512
  101.1 23.7 %collective-permute-start.8 = (bf16[1,128,1024]{2,1,0:T(8,128)(2,1)}, bf16[1,128,1024]{2,1,0:T(8,128)(2,1)}, u32[]{:S(2)}, u32[]{:S(2)}) collective-permute-start(bf16[1,128,1024]{2,1,0:T(8,128)(2,1)} %get-tuple-element.32), channel_id=1, source_target_pairs={{1,3},{2,0},{5,7},{6,4},{9,11},{10,8},{13,15},{14,12},{17,19},{18,... | collective-permute-start | bytes 786440 | tf_op jit(solution)/shard_map/ppermute | solution.py:512
  104.5 20.3 %collective-permute-start.9 = (bf16[1,128,1024]{2,1,0:T(8,128)(2,1)}, bf16[1,128,1024]{2,1,0:T(8,128)(2,1)}, u32[]{:S(2)}, u32[]{:S(2)}) collective-permute-start(bf16[1,128,1024]{2,1,0:T(8,128)(2,1)} %get-tuple-element.32), channel_id=1, source_target_pairs={{0,2},{3,1},{4,6},{7,5},{8,10},{11,9},{12,14},{15,13},{16,18},{19,... | collective-permute-start | bytes 786440 | tf_op jit(solution)/shard_map/ppermute | solution.py:512
  115.1 3.0 %copy-start.2 = (bf16[1,128,1024]{2,1,0:T(8,128)(2,1)S(1)}, bf16[1,128,1024]{2,1,0:T(8,128)(2,1)}, u32[]{:S(2)}) copy-start(bf16[1,128,1024]{2,1,0:T(8,128)(2,1)} %copy-done.1) | copy-start | bytes 786436
  115.1 1.0 copy-start.4
